TPU v7x, 512 devices: a whole 4x8x8 slice. The times are simulated.
512 devices in a mesh: node: 64 (over y, x, core), edge: 8 (over z).
Axes of the slice: x: 4, y: 8, z: 8, core: 2. Of those that a mesh axis runs over, the one named last changes fastest.
Arguments:
- embedding: bfloat16 [512, 128, 512], P('node'), may hold values from -6 to 6
- send_list: int32 [8, 64, 64], P('edge', 'node'), may hold values from -1 to 7, as said below
- edge_ends: int32 [2, 1048576], P(None, ('node', 'edge')), may hold values from 0 to 65535, as said below
- pair_index: int32 [1048576], P(('node', 'edge')), may hold values from 0 to 65535, as said below
- w_first: bfloat16 [1024, 512], replicated, may hold values from -0.1875 to 0.1875
- b_first: float32 [512], replicated, may hold values from -3 to 3
- w_second: bfloat16 [512], replicated, may hold values from -0.25 to 0.25
Outputs:
- edge_score: float32 [1048576], P(('node', 'edge'))
- pair_cost: float32 [65536], P(('node', 'edge'))
Inputs may be any that keep to these rules, and one draw needn't show every extreme that they name: Each entry is -1 or a block index of the sending node index; send_list[e, k, k] is never -1. `edge_ends`: node ids; most ends lie in a block that the send list delivers to the edge's node group and edge index. `pair_index`: an edge of node group j has a pair in j * 1024 to (j + 1) * 1024 - 1.
All inputs are finite; a program needn't handle non-finite values.
Results may differ from a plain program's by a relative error of at most 0.0003.
Values may be sent and summed in bfloat16 or wider, within the bound.
A program may use at most 64 MiB of HBM per device.

v0:
```python
import jax
import jax.numpy as jnp
from jax import lax
from jax.sharding import PartitionSpec as P

PAIRS_ROW = 1024


def body(embedding, send_list, edge_ends, pair_index, w_first, b_first, w_second):
    node_count = lax.axis_size("node")
    node_self = lax.axis_index("node")
    blocks_here = embedding.shape[0]
    block_rows = embedding.shape[1]
    feature_width = embedding.shape[2]
    wanted = send_list[0, 0]
    picked = jnp.take(embedding, jnp.clip(wanted, 0, blocks_here - 1), axis=0)
    picked = jnp.where((wanted >= 0)[:, None, None], picked, jnp.zeros_like(picked))
    labels = jnp.where(wanted >= 0, node_self * blocks_here + wanted, -1)
    arrived, slot_ids = (
        lax.all_to_all(picked, "node", split_axis=0, concat_axis=0, tiled=True),
        lax.all_to_all(labels, "node", split_axis=0, concat_axis=0, tiled=True),
    )
    flat_rows = arrived.reshape(node_count * block_rows, feature_width)
    target = edge_ends // block_rows
    within = edge_ends % block_rows
    matches = target[..., None] == slot_ids
    located = jnp.any(matches, axis=-1)
    slot_index = jnp.sum(jnp.where(matches, jnp.arange(node_count, dtype=jnp.int32), 0), axis=-1)
    position = slot_index * block_rows + within
    edge_total = edge_ends.shape[1]
    tile_rows = min(512, edge_total)
    tile_count = edge_total // tile_rows
    position = position.reshape(2, tile_count, tile_rows).transpose(1, 0, 2)
    located = located.reshape(2, tile_count, tile_rows).transpose(1, 0, 2)
    pair_ids = (pair_index - node_self * PAIRS_ROW).reshape(tile_count, tile_rows)
    upper = w_first[:feature_width]
    bottom = w_first[feature_width:]
    w_out = w_second.astype(jnp.float32)
    pair_range = jnp.arange(PAIRS_ROW, dtype=jnp.int32)

    def tile_step(pooled_sum, pieces):
        rows_at, present, pair_here = pieces
        end_rows = jnp.take(flat_rows, rows_at, axis=0)
        end_rows = jnp.where(present[..., None], end_rows, jnp.zeros_like(end_rows))
        preact = jnp.dot(end_rows[0], upper, preferred_element_type=jnp.float32)
        preact = preact + jnp.dot(end_rows[1], bottom, preferred_element_type=jnp.float32) + b_first
        hidden = jax.nn.gelu(preact, approximate=True)
        scores = jnp.dot(hidden, w_out, precision=lax.Precision.HIGHEST)
        onehot = (pair_here[:, None] == pair_range[None, :]).astype(jnp.float32)
        pooled_sum = pooled_sum + jnp.dot(scores, onehot, precision=lax.Precision.HIGHEST)
        return (pooled_sum, scores)

    pooled_sum, scores = lax.scan(
        tile_step, jnp.zeros((PAIRS_ROW,), jnp.float32), (position, located, pair_ids)
    )
    edge_score = scores.reshape(edge_total)
    pair_cost = lax.psum_scatter(pooled_sum, "edge", scatter_dimension=0, tiled=True)
    return (edge_score, pair_cost)


def solution(mesh):
    return jax.shard_map(
        body,
        mesh=mesh,
        in_specs=(
            P("node", None, None),
            P("edge", "node", None),
            P(None, ("node", "edge")),
            P(("node", "edge")),
            P(),
            P(),
            P(),
        ),
        out_specs=(P(("node", "edge")), P(("node", "edge"))),
        check_vma=False,
    )
```

profile of v0, /device:TPU:10, one launch (start us, length us, event | category | flops | bytes accessed | tf_op | source)
XLA Modules:
  0.0 297.3 jit_solution(16352510401790665070)
XLA Ops:
  0.6 0.0 copy-start
  0.6 0.7 fusion.17
  1.4 0.7 copy.11
  2.1 10.5 %all-to-all-start = ((s32[64,1,1]{2,1,0:T(1,128)}), s32[64,1,1]{2,1,0:T(1,128)S(1)}, u32[]{:S(2)}, u32[]{:S(2)}) async-start(s32[64,1,1]{2,1,0:T(1,128)} %copy.11), calls=%async_computation | async-start | bytes 65536 | tf_op jit(solution)/shard_map/all_to_all | solution.py:21
  12.7 0.7 fusion.18
  13.3 0.7 compare_and_fusion.1
  14.0 0.7 compare_bitcast_fusion
  14.7 0.0 copy-done
  14.7 5.4 %gather_fusion.1 = bf16[64,128,512]{2,1,0:T(8,128)(2,1)} fusion(bf16[8,128,512]{2,1,0:T(8,128)(2,1)S(1)} %copy-done, s32[1024]{0:T(1024)S(1)} %pad_clamp_fusion), kind=kCustom, calls=%fused_computation.1 | custom fusion | bytes 16777472 | tf_op jit(solution)/shard_map/jit(_take)/gather | solution.py:16
  20.1 7.6 %select_select_fusion.1 = bf16[64,128,512]{2,1,0:T(8,128)(2,1)} fusion(bf16[64,128,512]{2,1,0:T(8,128)(2,1)} %gather_fusion.1, pred[64]{0:T(512)(128)(4,1)S(1)} %compare_and_fusion.1, pred[64]{0:T(512)(128)(4,1)S(1)} %compare_bitcast_fusion), kind=kLoop, calls=%fused_computation.29 | loop fusion | flops 8388608 | bytes 16777344 | tf_op jit(solution)/shard_map/jit(_where)/select_n | solution.py:17
  27.7 0.0 copy-start.5
  27.7 0.0 all-to-all-done
  27.7 10.6 %all-to-all-start.1 = ((bf16[64,128,512]{2,1,0:T(8,128)(2,1)}), bf16[64,128,512]{2,1,0:T(8,128)(2,1)}, u32[]{:S(2)}, u32[]{:S(2)}) async-start(bf16[64,128,512]{2,1,0:T(8,128)(2,1)} %select_select_fusion.1), calls=%async_computation.1 | async-start | bytes 16777216 | tf_op jit(solution)/shard_map/all_to_all | solution.py:20
  38.4 0.0 copy-done.3
  38.4 1.3 dynamic-slice
  40.4 0.1 fusion.19
  40.5 1.2 reduce
  41.7 0.2 compare_reduce_fusion
  42.0 0.2 fusion.15
  42.2 182.6 %all-to-all-done.1 = bf16[64,128,512]{2,1,0:T(8,128)(2,1)} async-done(((bf16[64,128,512]{2,1,0:T(8,128)(2,1)}), bf16[64,128,512]{2,1,0:T(8,128)(2,1)}, u32[]{:S(2)}, u32[]{:S(2)}) %all-to-all-start.1) | async-done | bytes 8388640 | tf_op jit(solution)/shard_map/all_to_all | solution.py:20
  224.8 48.1 %while.13 = (s32[]{:T(128)}, f32[1024]{0:T(1024)S(1)}, f32[4,512]{1,0:T(4,128)S(1)}, pred[4,2,512]{2,1,0:T(4,128)(4,1)S(1)}, s32[4,2,512]{2,1,0:T(2,128)S(1)}, /...) while((s32[]{:T(128)}, f32[1024]{0:T(1024)S(1)}, ...), condition=%wide.region_3.4_spmd.clone, body=%wide.region_2.3_spmd.clone.sunk | while | flops 550514688 | bytes 10558627 | solution.py:53
  224.9 8.5 %gather_fusion = bf16[1024,512]{1,0:T(8,128)(2,1)S(1)} fusion(bf16[8192,512]{1,0:T(8,128)(2,1)} %get-tuple-element.227, s32[1024]{0:T(1024)S(1)} %broadcast_clamp_fusion.2), kind=kCustom, calls=%fused_computation.clone.clone.1 | custom fusion | bytes 2101248 | tf_op jit(solution)/shard_map/while/body/eval_jaxpr/jit(_take)/gather | solution.py:43
  233.4 0.4 select_select_fusion.3
  233.8 0.4 fusion.41
  234.3 0.7 fusion.42
  234.9 1.0 fusion.43
  235.9 0.8 fusion.44
  236.9 8.5 %gather_fusion = bf16[1024,512]{1,0:T(8,128)(2,1)S(1)} fusion(bf16[8192,512]{1,0:T(8,128)(2,1)} %get-tuple-element.227, s32[1024]{0:T(1024)S(1)} %broadcast_clamp_fusion.2), kind=kCustom, calls=%fused_computation.clone.clone.1 | custom fusion | bytes 2101248 | tf_op jit(solution)/shard_map/while/body/eval_jaxpr/jit(_take)/gather | solution.py:43
  245.4 0.4 select_select_fusion.3
  245.8 0.4 fusion.41
  246.3 0.7 fusion.42
  247.0 1.0 fusion.43
  248.0 0.8 fusion.44
  248.9 8.5 %gather_fusion = bf16[1024,512]{1,0:T(8,128)(2,1)S(1)} fusion(bf16[8192,512]{1,0:T(8,128)(2,1)} %get-tuple-element.227, s32[1024]{0:T(1024)S(1)} %broadcast_clamp_fusion.2), kind=kCustom, calls=%fused_computation.clone.clone.1 | custom fusion | bytes 2101248 | tf_op jit(solution)/shard_map/while/body/eval_jaxpr/jit(_take)/gather | solution.py:43
  257.4 0.4 select_select_fusion.3
  257.9 0.4 fusion.41
  258.3 0.7 fusion.42
  259.0 1.0 fusion.43
  260.0 0.8 fusion.44
  260.9 8.5 %gather_fusion = bf16[1024,512]{1,0:T(8,128)(2,1)S(1)} fusion(bf16[8192,512]{1,0:T(8,128)(2,1)} %get-tuple-element.227, s32[1024]{0:T(1024)S(1)} %broadcast_clamp_fusion.2), kind=kCustom, calls=%fused_computation.clone.clone.1 | custom fusion | bytes 2101248 | tf_op jit(solution)/shard_map/while/body/eval_jaxpr/jit(_take)/gather | solution.py:43
  269.4 0.4 select_select_fusion.3
  269.9 0.4 fusion.41
  270.3 0.7 fusion.42
  271.0 1.0 fusion.43
  272.0 0.8 fusion.44
  272.9 0.6 copy.15
  273.5 23.2 %all-reduce = f32[1024]{0:T(1024)S(1)} all-reduce(f32[1024]{0:T(1024)S(1)} %get-tuple-element.66), channel_id=2, replica_groups=mesh['node'=64,'edge'=8] {'edge'}, use_global_device_ids=true, to_apply=%region_4.5.clone | all-reduce | flops 1024 | bytes 8192
  296.7 0.6 dynamic-slice.1
  (48 shorter events, 0.5 us)
Async XLA Ops:
  0.6 14.0 %copy-start = (bf16[8,128,512]{2,1,0:T(8,128)(2,1)S(1)}, bf16[8,128,512]{2,1,0:T(8,128)(2,1)}, u32[]{:S(2)}) copy-start(bf16[8,128,512]{2,1,0:T(8,128)(2,1)} %param.9) | copy-start | bytes 3145732
  2.1 25.6 %all-to-all-start = ((s32[64,1,1]{2,1,0:T(1,128)}), s32[64,1,1]{2,1,0:T(1,128)S(1)}, u32[]{:S(2)}, u32[]{:S(2)}) async-start(s32[64,1,1]{2,1,0:T(1,128)} %copy.11), calls=%async_computation | async-start | bytes 65536 | tf_op jit(solution)/shard_map/all_to_all | solution.py:21
  27.7 10.7 %copy-start.4 = (bf16[512]{0:T(512)(128)(2,1)S(1)}, bf16[512]{0:T(512)(128)(2,1)}, u32[]{:S(2)}) copy-start(bf16[512]{0:T(512)(128)(2,1)} %param.15) | copy-start | bytes 3076
  27.7 10.7 %copy-start.3 = (s32[2048]{0:T(1024)S(1)}, s32[2048]{0:T(1024)}, u32[]{:S(2)}) copy-start(s32[2048]{0:T(1024)} %param.12) | copy-start | bytes 24580
  27.7 12.7 %copy-start.1 = (bf16[1024,512]{1,0:T(8,128)(2,1)S(1)}, bf16[1024,512]{1,0:T(8,128)(2,1)}, u32[]{:S(2)}) copy-start(bf16[1024,512]{1,0:T(8,128)(2,1)} %param.13) | copy-start | bytes 3145732
  27.7 12.7 %copy-start.2 = (s32[2,2048]{1,0:T(2,128)S(1)}, s32[2,2048]{1,0:T(2,128)}, u32[]{:S(2)}) copy-start(s32[2,2048]{1,0:T(2,128)} %param.11) | copy-start | bytes 49156
  27.7 197.1 %copy-start.5 = (f32[512]{0:T(512)S(1)}, f32[512]{0:T(512)}, u32[]{:S(2)}) copy-start(f32[512]{0:T(512)} %param.14) | copy-start | bytes 6148
  27.7 197.1 %all-to-all-start.1 = ((bf16[64,128,512]{2,1,0:T(8,128)(2,1)}), bf16[64,128,512]{2,1,0:T(8,128)(2,1)}, u32[]{:S(2)}, u32[]{:S(2)}) async-start(bf16[64,128,512]{2,1,0:T(8,128)(2,1)} %select_select_fusion.1), calls=%async_computation.1 | async-start | bytes 16777216 | tf_op jit(solution)/shard_map/all_to_all | solution.py:20
where the time goes:
time: 298 us; the launch traced here: 297 us
  waiting for transfers between devices  183 us (61%)
  local copies, waits for them, and re-layouts  42.8 us (14%)
  blocking collectives  23.2 us (8%)
  starting transfers between devices  21.1 us (7%)
  other arithmetic  14 us (5%)
  matrix products  11.7 us (4%)
    all_to_all x1, waiting for transfers between devices, body(): lax.all_to_all(picked, 'node', split_axis=0, concat_axis=0, tiled=True)  183 us
    gather x4, local copies, waits for them, and re-layouts, tile_step(): end_rows = jnp.take(flat_rows, rows_at, axis=0)  33.8 us
    unnamed x1, blocking collectives  23.2 us
    all_to_all x1, starting transfers between devices, body(): lax.all_to_all(picked, 'node', split_axis=0, concat_axis=0, tiled=True)  10.6 us
    all_to_all x1, starting transfers between devices, body(): lax.all_to_all(labels, 'node', split_axis=0, concat_axis=0, tiled=True)  10.5 us
    select_n x1, other arithmetic, body(): jnp.where((wanted >= 0)[:, None, None], picked, jnp.zeros_like(picked))  7.6 us
  transfers between devices with their start and end apart: 2, of which 1 were waited for; matrix products, arithmetic and copies ran while one was open for 6% of the time, Pallas kernels for 0%

commit v1 on v0

v1 whole, which is shorter than its diff:
```python
import functools

import jax
import jax.numpy as jnp
from jax import lax
from jax.experimental import pallas as pl
from jax.experimental.pallas import tpu as pltpu
from jax.sharding import PartitionSpec as P

PAIRS_ROW = 1024
TILE = 256


def gelu_tanh(x):
    return x * (0.5 * (1.0 + jnp.tanh(0.7978845608028654 * (x + 0.044715 * (x * x * x)))))


def score_kernel(edges, pos_ref, table, mask_ref, wt_ref, wb_ref, bias_ref, wo_ref, pid_ref,
                 score_ref, pool_ref, buf, sems):
    step = pl.program_id(0)
    steps = pl.num_programs(0)

    def fetch(tile, slot):
        base = tile * TILE

        def one(r, carry):
            p0 = pos_ref[base + r]
            p1 = pos_ref[edges + base + r]
            pltpu.make_async_copy(table.at[pl.ds(p0, 1)], buf.at[0, slot, pl.ds(r, 1)], sems.at[0, slot]).start()
            pltpu.make_async_copy(table.at[pl.ds(p1, 1)], buf.at[1, slot, pl.ds(r, 1)], sems.at[1, slot]).start()
            return carry

        lax.fori_loop(0, TILE, one, 0, unroll=8)

    @pl.when(step == 0)
    def _():
        fetch(0, 0)
        pool_ref[...] = jnp.zeros_like(pool_ref)

    slot = step % 2

    @pl.when(step + 1 < steps)
    def _():
        fetch(step + 1, 1 - slot)

    for end in range(2):
        pltpu.make_async_copy(table.at[pl.ds(0, TILE)], buf.at[end, slot], sems.at[end, slot]).wait()

    mask = mask_ref[...]
    rows0 = buf[0, slot].astype(jnp.bfloat16)
    rows1 = buf[1, slot].astype(jnp.bfloat16)
    rows0 = jnp.where(mask[:, 0:1] > 0, rows0, jnp.zeros_like(rows0))
    rows1 = jnp.where(mask[:, 1:2] > 0, rows1, jnp.zeros_like(rows1))
    preact = jnp.dot(rows0, wt_ref[...], preferred_element_type=jnp.float32)
    preact = preact + jnp.dot(rows1, wb_ref[...], preferred_element_type=jnp.float32) + bias_ref[...]
    hidden = gelu_tanh(preact)
    scores = lax.dot_general(wo_ref[...], hidden, (((1,), (1,)), ((), ())),
                             precision=lax.Precision.HIGHEST, preferred_element_type=jnp.float32)
    score_ref[...] = scores[0:1]
    pair_range = lax.broadcasted_iota(jnp.int32, (TILE, PAIRS_ROW), 1)
    onehot = (pid_ref[...] == pair_range).astype(jnp.float32)
    pooled = jnp.dot(scores, onehot, precision=lax.Precision.HIGHEST, preferred_element_type=jnp.float32)
    pool_ref[...] += pooled[0:1]


def edge_scores(position, located, pair_ids, table, w_first, b_first, w_second):
    edges = position.shape[1]
    width = table.shape[1]
    hid = w_first.shape[1]
    tiles = edges // TILE
    pos_flat = position.reshape(2 * edges)
    mask = located.T.astype(jnp.float32)
    wo8 = jnp.broadcast_to(w_second.astype(jnp.float32)[None, :], (8, hid))
    grid_spec = pltpu.PrefetchScalarGridSpec(
        num_scalar_prefetch=1,
        grid=(tiles,),
        in_specs=[
            pl.BlockSpec(memory_space=pl.ANY),
            pl.BlockSpec((TILE, 2), lambda i, p: (i, 0)),
            pl.BlockSpec((width, hid), lambda i, p: (0, 0)),
            pl.BlockSpec((width, hid), lambda i, p: (1, 0)),
            pl.BlockSpec((1, hid), lambda i, p: (0, 0)),
            pl.BlockSpec((8, hid), lambda i, p: (0, 0)),
            pl.BlockSpec((TILE, 1), lambda i, p: (i, 0)),
        ],
        out_specs=[
            pl.BlockSpec((1, TILE), lambda i, p: (0, i)),
            pl.BlockSpec((1, PAIRS_ROW), lambda i, p: (0, 0)),
        ],
        scratch_shapes=[
            pltpu.VMEM((2, 2, TILE, width), table.dtype),
            pltpu.SemaphoreType.DMA((2, 2)),
        ],
    )
    scores, pooled = pl.pallas_call(
        functools.partial(score_kernel, edges),
        grid_spec=grid_spec,
        out_shape=[
            jax.ShapeDtypeStruct((1, edges), jnp.float32),
            jax.ShapeDtypeStruct((1, PAIRS_ROW), jnp.float32),
        ],
        compiler_params=pltpu.CompilerParams(dimension_semantics=("arbitrary",)),
        cost_estimate=pl.CostEstimate(
            flops=2 * edges * 2 * width * hid, transcendentals=edges * hid,
            bytes_accessed=2 * edges * width * table.dtype.itemsize),
    )(pos_flat, table, mask, w_first, w_first, b_first.reshape(1, hid), wo8, pair_ids.reshape(edges, 1))
    return scores.reshape(edges), pooled.reshape(PAIRS_ROW)


def body(embedding, send_list, edge_ends, pair_index, w_first, b_first, w_second):
    node_count = lax.axis_size("node")
    node_self = lax.axis_index("node")
    blocks_here = embedding.shape[0]
    block_rows = embedding.shape[1]
    feature_width = embedding.shape[2]
    wanted = send_list[0, 0]
    picked = jnp.take(embedding, jnp.clip(wanted, 0, blocks_here - 1), axis=0)
    labels = jnp.where(wanted >= 0, node_self * blocks_here + wanted, -1)
    arrived, slot_ids = (
        lax.all_to_all(picked, "node", split_axis=0, concat_axis=0, tiled=True),
        lax.all_to_all(labels, "node", split_axis=0, concat_axis=0, tiled=True),
    )
    table = arrived.reshape(node_count * block_rows, feature_width).astype(jnp.float32)
    target = edge_ends // block_rows
    within = edge_ends % block_rows
    matches = target[..., None] == slot_ids
    located = jnp.any(matches, axis=-1)
    slot_index = jnp.sum(jnp.where(matches, jnp.arange(node_count, dtype=jnp.int32), 0), axis=-1)
    position = slot_index * block_rows + within
    pair_ids = pair_index - node_self * PAIRS_ROW
    edge_score, pooled_sum = edge_scores(position, located, pair_ids, table, w_first, b_first, w_second)
    pair_cost = lax.psum_scatter(pooled_sum, "edge", scatter_dimension=0, tiled=True)
    return (edge_score, pair_cost)


def solution(mesh):
    return jax.shard_map(
        body,
        mesh=mesh,
        in_specs=(
            P("node", None, None),
            P("edge", "node", None),
            P(None, ("node", "edge")),
            P(("node", "edge")),
            P(),
            P(),
            P(),
        ),
        out_specs=(P(("node", "edge")), P(("node", "edge"))),
        check_vma=False,
    )
```

time: 298 us -> 304 us (1.020)
  the two profiles are of different devices: /device:TPU:10 before, /device:TPU:4 now
where the time goes in v1:
time: 304 us
  waiting for transfers between devices  179 us (59%)
  Pallas kernels  43.9 us (14%)
  blocking collectives  23.2 us (8%)
  other arithmetic  22.8 us (8%)
  starting transfers between devices  21.3 us (7%)
  local copies, waits for them, and re-layouts  12.1 us (4%)
    all_to_all x1, waiting for transfers between devices, body(): lax.all_to_all(picked, 'node', split_axis=0, concat_axis=0, tiled=True)  179 us
    pallas_call x1, Pallas kernels, edge_scores(): pl.pallas_call(functools.partial(score_kernel, edges), grid_spec=grid_spe...  43.9 us
    unnamed x1, blocking collectives  23.2 us
    convert_element_type x1, other arithmetic, body(): arrived.reshape(node_count * block_rows, feature_width).astype(jnp.float32)  11.5 us
    all_to_all x1, starting transfers between devices, body(): lax.all_to_all(picked, 'node', split_axis=0, concat_axis=0, tiled=True)  10.6 us
    all_to_all x1, starting transfers between devices, body(): lax.all_to_all(labels, 'node', split_axis=0, concat_axis=0, tiled=True)  10.6 us
    select_n x2, other arithmetic, body(): picked = jnp.take(embedding, jnp.clip(wanted, 0, blocks_here - 1), axis=0)  8.13 us
  transfers between devices with their start and end apart: 2, of which 1 were waited for; matrix products, arithmetic and copies ran while one was open for 7% of the time, Pallas kernels for 0%

profile of v1, /device:TPU:4, one launch (start us, length us, event | category | flops | bytes accessed | tf_op | source)
XLA Modules:
  0.0 303.8 jit_solution(12624579837322042243)
XLA Ops:
  0.6 0.0 copy-start
  0.6 0.7 fusion.3
  1.4 0.7 copy.14
  2.1 10.6 %all-to-all-start = ((s32[64,1,1]{2,1,0:T(1,128)}), s32[64,1,1]{2,1,0:T(1,128)S(1)}, u32[]{:S(2)}, u32[]{:S(2)}) async-start(s32[64,1,1]{2,1,0:T(1,128)} %copy.14), calls=%async_computation | async-start | bytes 65536 | tf_op jit(solution)/shard_map/all_to_all | solution.py:121
  12.7 0.7 fusion.4
  13.4 0.7 compare_and_fusion
  14.1 0.0 copy-done
  14.1 5.5 %gather_fusion = bf16[64,128,512]{2,1,0:T(8,128)(2,1)} fusion(bf16[8,128,512]{2,1,0:T(8,128)(2,1)S(1)} %copy-done, s32[1024]{0:T(1024)S(1)} %pad_clamp_fusion), kind=kCustom, calls=%fused_computation | custom fusion | bytes 16777472 | tf_op jit(solution)/shard_map/jit(_take)/gather | solution.py:117
  19.6 7.5 %broadcast_select_fusion = bf16[64,128,512]{2,1,0:T(8,128)(2,1)} fusion(bf16[64,128,512]{2,1,0:T(8,128)(2,1)} %gather_fusion, pred[64]{0:T(512)(128)(4,1)S(1)} %compare_and_fusion), kind=kLoop, calls=%fused_computation.2 | loop fusion | flops 4194304 | bytes 16777280 | tf_op jit(solution)/shard_map/jit(_take)/select_n | solution.py:117
  27.0 0.0 copy-start.2
  27.0 0.0 copy-start.1
  27.0 0.0 all-to-all-done
  27.0 10.6 %all-to-all-start.1 = ((bf16[64,128,512]{2,1,0:T(8,128)(2,1)}), bf16[64,128,512]{2,1,0:T(8,128)(2,1)}, u32[]{:S(2)}, u32[]{:S(2)}) async-start(bf16[64,128,512]{2,1,0:T(8,128)(2,1)} %broadcast_select_fusion), calls=%async_computation.1 | async-start | bytes 16777216 | tf_op jit(solution)/shard_map/all_to_all | solution.py:120
  37.7 0.0 copy-done.2
  37.7 1.3 copy.16.pid_ref
  39.1 1.3 dynamic-slice
  41.0 0.0 copy-done.1
  41.0 1.2 reduce
  42.3 0.2 fusion
  42.5 0.6 copy.17
  43.1 0.2 compare_reduce_fusion
  43.3 1.4 copy.15
  44.8 0.0 copy-start.3
  44.8 179.3 %all-to-all-done.1 = bf16[64,128,512]{2,1,0:T(8,128)(2,1)} async-done(((bf16[64,128,512]{2,1,0:T(8,128)(2,1)}), bf16[64,128,512]{2,1,0:T(8,128)(2,1)}, u32[]{:S(2)}, u32[]{:S(2)}) %all-to-all-start.1) | async-done | bytes 8388640 | tf_op jit(solution)/shard_map/all_to_all | solution.py:120
  224.1 11.5 %bitcast_convert_fusion.table = f32[8192,512]{1,0:T(8,128)} fusion(bf16[64,128,512]{2,1,0:T(8,128)(2,1)} %all-to-all-done.1), kind=kLoop, calls=%fused_computation.1 | loop fusion | flops 4194304 | bytes 25165824 | tf_op jit(solution)/shard_map/convert_element_type | solution.py:123
  235.6 0.0 copy-done.3
  235.6 0.6 broadcast_in_dim.35.wo_ref
  236.2 43.9 %shard_map.86 = (f32[1,2048]{1,0:T(1,128)}, f32[1,1024]{1,0:T(1,128)}) custom-call(s32[4096]{0:T(1024)} %bitcast.21, f32[8192,512]{1,0:T(8,128)} %bitcast_convert_fusion.table, f32[2048,2]{1,0:T(8,128)} %bitcast.20, bf16[1024,512]{1,0:T(8,128)(2,1)} %wb_ref.1, bf16[1024,512]{1,0:T(8,128)(2,1)} %wb_ref.1, f32[1,512]{1,0:T(1,128)} %bitcast.24, ...), custom_call_target="tpu_custom_call" | custom-call | flops 2147483648 | bytes 8388608 | tf_op jit(solution)/shard_map/pallas_call | solution.py:95
  280.1 23.2 %all-reduce = f32[1024]{0:T(1024)S(1)} all-reduce(f32[1024]{0:T(1024)} %bitcast.23), channel_id=2, replica_groups=mesh['node'=64,'edge'=8] {'edge'}, use_global_device_ids=true, to_apply=%region_2.3.clone | all-reduce | flops 1024 | bytes 8192
  303.2 0.6 dynamic-slice.1
  (5 shorter events, 0.1 us)
Async XLA Ops:
  0.6 13.4 %copy-start = (bf16[8,128,512]{2,1,0:T(8,128)(2,1)S(1)}, bf16[8,128,512]{2,1,0:T(8,128)(2,1)}, u32[]{:S(2)}) copy-start(bf16[8,128,512]{2,1,0:T(8,128)(2,1)} %param.7) | copy-start | bytes 3145732
  2.1 24.9 %all-to-all-start = ((s32[64,1,1]{2,1,0:T(1,128)}), s32[64,1,1]{2,1,0:T(1,128)S(1)}, u32[]{:S(2)}, u32[]{:S(2)}) async-start(s32[64,1,1]{2,1,0:T(1,128)} %copy.14), calls=%async_computation | async-start | bytes 65536 | tf_op jit(solution)/shard_map/all_to_all | solution.py:121
  27.0 10.7 %copy-start.2 = (s32[2048]{0:T(1024)S(1)}, s32[2048]{0:T(1024)}, u32[]{:S(2)}) copy-start(s32[2048]{0:T(1024)} %param.10) | copy-start | bytes 24580
  27.0 13.9 %copy-start.1 = (s32[2,2048]{1,0:T(2,128)S(1)}, s32[2,2048]{1,0:T(2,128)}, u32[]{:S(2)}) copy-start(s32[2,2048]{1,0:T(2,128)} %param.9) | copy-start | bytes 49156
  27.0 197.0 %all-to-all-start.1 = ((bf16[64,128,512]{2,1,0:T(8,128)(2,1)}), bf16[64,128,512]{2,1,0:T(8,128)(2,1)}, u32[]{:S(2)}, u32[]{:S(2)}) async-start(bf16[64,128,512]{2,1,0:T(8,128)(2,1)} %broadcast_select_fusion), calls=%async_computation.1 | async-start | bytes 16777216 | tf_op jit(solution)/shard_map/all_to_all | solution.py:120
  44.8 190.8 %copy-start.3 = (bf16[512]{0:T(512)(128)(2,1)S(1)}, bf16[512]{0:T(512)(128)(2,1)}, u32[]{:S(2)}) copy-start(bf16[512]{0:T(512)(128)(2,1)} %param.13) | copy-start | bytes 3076

commit v2 on v1

--- a/solution.py
+++ b/solution.py
@@ -16,18 +16,19 @@
 
 
 def score_kernel(edges, pos_ref, table, mask_ref, wt_ref, wb_ref, bias_ref, wo_ref, pid_ref,
-                 score_ref, pool_ref, buf, sems):
+                 score_ref, pool_ref, buf, wide, sems):
     step = pl.program_id(0)
     steps = pl.num_programs(0)
+    parts = buf.shape[2] // TILE
 
     def fetch(tile, slot):
         base = tile * TILE
 
         def one(r, carry):
-            p0 = pos_ref[base + r]
-            p1 = pos_ref[edges + base + r]
-            pltpu.make_async_copy(table.at[pl.ds(p0, 1)], buf.at[0, slot, pl.ds(r, 1)], sems.at[0, slot]).start()
-            pltpu.make_async_copy(table.at[pl.ds(p1, 1)], buf.at[1, slot, pl.ds(r, 1)], sems.at[1, slot]).start()
+            dst = pl.ds(pl.multiple_of(r * parts, parts), parts)
+            for end in range(2):
+                src = pl.ds(pl.multiple_of(pos_ref[end * edges + base + r], parts), parts)
+                pltpu.make_async_copy(table.at[src], buf.at[end, slot, dst], sems.at[end, slot]).start()
             return carry
 
         lax.fori_loop(0, TILE, one, 0, unroll=8)
@@ -44,15 +45,19 @@
         fetch(step + 1, 1 - slot)
 
     for end in range(2):
-        pltpu.make_async_copy(table.at[pl.ds(0, TILE)], buf.at[end, slot], sems.at[end, slot]).wait()
+        pltpu.make_async_copy(table.at[pl.ds(0, TILE * parts)], buf.at[end, slot], sems.at[end, slot]).wait()
 
     mask = mask_ref[...]
-    rows0 = buf[0, slot].astype(jnp.bfloat16)
-    rows1 = buf[1, slot].astype(jnp.bfloat16)
-    rows0 = jnp.where(mask[:, 0:1] > 0, rows0, jnp.zeros_like(rows0))
-    rows1 = jnp.where(mask[:, 1:2] > 0, rows1, jnp.zeros_like(rows1))
-    preact = jnp.dot(rows0, wt_ref[...], preferred_element_type=jnp.float32)
-    preact = preact + jnp.dot(rows1, wb_ref[...], preferred_element_type=jnp.float32) + bias_ref[...]
+    lanes = buf.shape[3]
+    preact = bias_ref[...]
+    for end, w_ref in ((0, wt_ref), (1, wb_ref)):
+        wide[...] = buf[end, slot].astype(jnp.float32)
+        keep = mask[:, end:end + 1] > 0
+        for q in range(parts):
+            piece = wide[pl.ds(q, TILE, stride=parts), :]
+            piece = jnp.where(keep, piece, jnp.zeros_like(piece)).astype(jnp.bfloat16)
+            preact = preact + jnp.dot(piece, w_ref[q * lanes:(q + 1) * lanes, :],
+                                      preferred_element_type=jnp.float32)
     hidden = gelu_tanh(preact)
     scores = lax.dot_general(wo_ref[...], hidden, (((1,), (1,)), ((), ())),
                              precision=lax.Precision.HIGHEST, preferred_element_type=jnp.float32)
@@ -65,7 +70,9 @@
 
 def edge_scores(position, located, pair_ids, table, w_first, b_first, w_second):
     edges = position.shape[1]
-    width = table.shape[1]
+    lanes = table.shape[1]
+    width = w_first.shape[0] // 2
+    parts = width // lanes
     hid = w_first.shape[1]
     tiles = edges // TILE
     pos_flat = position.reshape(2 * edges)
@@ -88,7 +95,8 @@
             pl.BlockSpec((1, PAIRS_ROW), lambda i, p: (0, 0)),
         ],
         scratch_shapes=[
-            pltpu.VMEM((2, 2, TILE, width), table.dtype),
+            pltpu.VMEM((2, 2, TILE * parts, lanes), table.dtype),
+            pltpu.VMEM((TILE * parts, lanes), jnp.float32),
             pltpu.SemaphoreType.DMA((2, 2)),
         ],
     )
@@ -113,20 +121,23 @@
     blocks_here = embedding.shape[0]
     block_rows = embedding.shape[1]
     feature_width = embedding.shape[2]
+    lanes = 128
+    parts = feature_width // lanes
+    block_len = block_rows * parts
+    slot_len = block_len + 8
     wanted = send_list[0, 0]
-    picked = jnp.take(embedding, jnp.clip(wanted, 0, blocks_here - 1), axis=0)
-    labels = jnp.where(wanted >= 0, node_self * blocks_here + wanted, -1)
-    arrived, slot_ids = (
-        lax.all_to_all(picked, "node", split_axis=0, concat_axis=0, tiled=True),
-        lax.all_to_all(labels, "node", split_axis=0, concat_axis=0, tiled=True),
-    )
-    table = arrived.reshape(node_count * block_rows, feature_width).astype(jnp.float32)
-    target = edge_ends // block_rows
-    within = edge_ends % block_rows
-    matches = target[..., None] == slot_ids
-    located = jnp.any(matches, axis=-1)
-    slot_index = jnp.sum(jnp.where(matches, jnp.arange(node_count, dtype=jnp.int32), 0), axis=-1)
-    position = slot_index * block_rows + within
+    narrow = embedding.reshape(blocks_here, block_len, lanes)
+    picked = jnp.take(narrow, jnp.clip(wanted, 0, blocks_here - 1), axis=0, mode="clip")
+    label_rows = jnp.broadcast_to(wanted.astype(embedding.dtype)[:, None, None], (node_count, 8, lanes))
+    picked = jnp.concatenate([picked, label_rows], axis=1)
+    arrived = lax.all_to_all(picked, "node", split_axis=0, concat_axis=0, tiled=True)
+    table = arrived.reshape(node_count * slot_len, lanes)
+    source = edge_ends // (blocks_here * block_rows)
+    block_of = (edge_ends // block_rows) % blocks_here
+    position = source * slot_len + (edge_ends % block_rows) * parts
+    sent = arrived[:, block_len, 0].astype(jnp.int32)
+    located = jnp.any((source[..., None] == jnp.arange(node_count, dtype=jnp.int32))
+                      & (block_of[..., None] == sent), axis=-1)
     pair_ids = pair_index - node_self * PAIRS_ROW
     edge_score, pooled_sum = edge_scores(position, located, pair_ids, table, w_first, b_first, w_second)
     pair_cost = lax.psum_scatter(pooled_sum, "edge", scatter_dimension=0, tiled=True)

time: 304 us -> 298 us (0.980)
  the two profiles are of different devices: /device:TPU:4 before, /device:TPU:2 now
where the time goes in v2:
time: 298 us; the launch traced here: 297 us
  waiting for transfers between devices  184 us (62%)
  Pallas kernels  52.8 us (18%)
  blocking collectives  24.1 us (8%)
  local copies, waits for them, and re-layouts  13.1 us (4%)
  starting transfers between devices  11.1 us (4%)
  other arithmetic  10.7 us (4%)
    all_to_all x1, waiting for transfers between devices, body(): lax.all_to_all(picked, 'node', split_axis=0, concat_axis=0, tiled=True)  184 us
    pallas_call x1, Pallas kernels, edge_scores(): pl.pallas_call(functools.partial(score_kernel, edges), grid_spec=grid_spe...  52.8 us
    unnamed x1, blocking collectives  24.1 us
    all_to_all x1, starting transfers between devices, body(): lax.all_to_all(picked, 'node', split_axis=0, concat_axis=0, tiled=True)  11.1 us
    concatenate x1, other arithmetic, body(): picked = jnp.concatenate([picked, label_rows], axis=1)  7.35 us
  transfers between devices with their start and end apart: 1, of which 1 were waited for; matrix products, arithmetic and copies ran while one was open for 1% of the time, Pallas kernels for 0%

profile of v2, /device:TPU:2, one launch (start us, length us, event | category | flops | bytes accessed | tf_op | source)
XLA Modules:
  0.0 297.3 jit_solution(3183948082369191944)
XLA Ops:
  0.6 0.7 clamp_bitcast_fusion
  1.4 1.7 reshape.55
  3.1 5.5 %gather_fusion = bf16[64,512,128]{2,1,0:T(8,128)(2,1)} fusion(bf16[8,512,128]{2,1,0:T(8,128)(2,1)S(1)} %reshape.55, s32[1024]{0:T(1024)S(1)} %pad_clamp_fusion), kind=kCustom, calls=%fused_computation | custom fusion | bytes 16777472 | tf_op jit(solution)/shard_map/jit(_take)/gather | solution.py:130
  8.5 0.1 broadcast_in_dim.6
  8.7 7.4 %pad_maximum_fusion = bf16[64,520,128]{2,1,0:T(8,128)(2,1)} fusion(bf16[64,8,128]{2,1,0:T(8,128)(2,1)S(1)} %broadcast_in_dim.6, bf16[64,512,128]{2,1,0:T(8,128)(2,1)} %gather_fusion), kind=kLoop, calls=%fused_computation.1 | loop fusion | flops 17039360 | bytes 17039360 | tf_op jit(solution)/shard_map/concatenate | solution.py:132
  16.0 0.0 copy-start
  16.0 0.0 copy-start.1
  16.0 0.0 copy-start.2
  16.0 11.1 %all-to-all-start = ((bf16[64,520,128]{2,1,0:T(8,128)(2,1)}), bf16[64,520,128]{2,1,0:T(8,128)(2,1)}, u32[]{:S(2)}, u32[]{:S(2)}) async-start(bf16[64,520,128]{2,1,0:T(8,128)(2,1)} %pad_maximum_fusion), calls=%async_computation | async-start | bytes 17039360 | tf_op jit(solution)/shard_map/all_to_all | solution.py:133
  27.2 0.0 copy-done
  27.2 0.1 fusion.6
  27.3 0.6 copy.15
  27.9 0.0 copy-done.1
  27.9 1.4 copy.14.pid_ref
  29.3 1.3 dynamic-slice
  31.2 184.1 %all-to-all-done = bf16[64,520,128]{2,1,0:T(8,128)(2,1)} async-done(((bf16[64,520,128]{2,1,0:T(8,128)(2,1)}), bf16[64,520,128]{2,1,0:T(8,128)(2,1)}, u32[]{:S(2)}, u32[]{:S(2)}) %all-to-all-start) | async-done | bytes 8519712 | tf_op jit(solution)/shard_map/all_to_all | solution.py:133
  215.3 2.1 fusion.2
  217.4 0.4 fusion.1
  217.8 1.4 copy.13
  219.2 0.0 copy-done.2
  219.2 0.6 broadcast_in_dim.7.wo_ref
  219.8 52.8 %shard_map.86 = (f32[1,2048]{1,0:T(1,128)}, f32[1,1024]{1,0:T(1,128)}) custom-call(s32[4096]{0:T(1024)} %bitcast.15, bf16[33280,128]{1,0:T(8,128)(2,1)} %bitcast.2.table, f32[2048,2]{1,0:T(8,128)} %bitcast.14, bf16[1024,512]{1,0:T(8,128)(2,1)} %wb_ref.1, bf16[1024,512]{1,0:T(8,128)(2,1)} %wb_ref.1, f32[1,512]{1,0:T(1,128)} %bitcast.18, ...), custom_call_target="tpu_custom_call" | custom-call | flops 2147483648 | bytes 4194304 | tf_op jit(solution)/shard_map/pallas_call | solution.py:103
  272.6 24.1 %all-reduce = f32[1024]{0:T(1024)S(1)} all-reduce(f32[1024]{0:T(1024)} %bitcast.17), channel_id=2, replica_groups=mesh['node'=64,'edge'=8] {'edge'}, use_global_device_ids=true, to_apply=%region_1.2.clone | all-reduce | flops 1024 | bytes 8192
  296.7 0.6 dynamic-slice.1
  (3 shorter events, 0.0 us)
Async XLA Ops:
  16.0 11.2 %copy-start = (s32[2,2048]{1,0:T(2,128)S(1)}, s32[2,2048]{1,0:T(2,128)}, u32[]{:S(2)}) copy-start(s32[2,2048]{1,0:T(2,128)} %param.9) | copy-start | bytes 49156
  16.0 11.9 %copy-start.1 = (s32[2048]{0:T(1024)S(1)}, s32[2048]{0:T(1024)}, u32[]{:S(2)}) copy-start(s32[2048]{0:T(1024)} %param.10) | copy-start | bytes 24580
  16.0 203.2 %copy-start.2 = (bf16[512]{0:T(512)(128)(2,1)S(1)}, bf16[512]{0:T(512)(128)(2,1)}, u32[]{:S(2)}) copy-start(bf16[512]{0:T(512)(128)(2,1)} %param.13) | copy-start | bytes 3076
  16.0 199.2 %all-to-all-start = ((bf16[64,520,128]{2,1,0:T(8,128)(2,1)}), bf16[64,520,128]{2,1,0:T(8,128)(2,1)}, u32[]{:S(2)}, u32[]{:S(2)}) async-start(bf16[64,520,128]{2,1,0:T(8,128)(2,1)} %pad_maximum_fusion), calls=%async_computation | async-start | bytes 17039360 | tf_op jit(solution)/shard_map/all_to_all | solution.py:133

commit v3 on v2

--- a/solution.py
+++ b/solution.py
@@ -59,13 +59,11 @@
             preact = preact + jnp.dot(piece, w_ref[q * lanes:(q + 1) * lanes, :],
                                       preferred_element_type=jnp.float32)
     hidden = gelu_tanh(preact)
-    scores = lax.dot_general(wo_ref[...], hidden, (((1,), (1,)), ((), ())),
-                             precision=lax.Precision.HIGHEST, preferred_element_type=jnp.float32)
-    score_ref[...] = scores[0:1]
+    scores = jnp.sum(hidden * wo_ref[0:1, :], axis=1, keepdims=True)
+    score_ref[...] = scores
     pair_range = lax.broadcasted_iota(jnp.int32, (TILE, PAIRS_ROW), 1)
-    onehot = (pid_ref[...] == pair_range).astype(jnp.float32)
-    pooled = jnp.dot(scores, onehot, precision=lax.Precision.HIGHEST, preferred_element_type=jnp.float32)
-    pool_ref[...] += pooled[0:1]
+    picked = jnp.where(pid_ref[...] == pair_range, scores, 0.0)
+    pool_ref[...] += jnp.sum(picked, axis=0, keepdims=True)
 
 
 def edge_scores(position, located, pair_ids, table, w_first, b_first, w_second):
@@ -91,7 +89,7 @@
             pl.BlockSpec((TILE, 1), lambda i, p: (i, 0)),
         ],
         out_specs=[
-            pl.BlockSpec((1, TILE), lambda i, p: (0, i)),
+            pl.BlockSpec((TILE, 1), lambda i, p: (i, 0)),
             pl.BlockSpec((1, PAIRS_ROW), lambda i, p: (0, 0)),
         ],
         scratch_shapes=[
@@ -104,7 +102,7 @@
         functools.partial(score_kernel, edges),
         grid_spec=grid_spec,
         out_shape=[
-            jax.ShapeDtypeStruct((1, edges), jnp.float32),
+            jax.ShapeDtypeStruct((edges, 1), jnp.float32),
             jax.ShapeDtypeStruct((1, PAIRS_ROW), jnp.float32),
         ],
         compiler_params=pltpu.CompilerParams(dimension_semantics=("arbitrary",)),
@@ -127,9 +125,12 @@
     slot_len = block_len + 8
     wanted = send_list[0, 0]
     narrow = embedding.reshape(blocks_here, block_len, lanes)
-    picked = jnp.take(narrow, jnp.clip(wanted, 0, blocks_here - 1), axis=0, mode="clip")
-    label_rows = jnp.broadcast_to(wanted.astype(embedding.dtype)[:, None, None], (node_count, 8, lanes))
-    picked = jnp.concatenate([picked, label_rows], axis=1)
+    narrow = jnp.concatenate([narrow, jnp.zeros((1, block_len, lanes), embedding.dtype)], axis=0)
+    marks = jnp.arange(blocks_here + 1, dtype=jnp.int32)
+    marks = jnp.where(marks < blocks_here, marks, -1).astype(embedding.dtype)
+    marks = jnp.broadcast_to(marks[:, None, None], (blocks_here + 1, 8, lanes))
+    source_blocks = jnp.concatenate([narrow, marks], axis=1)
+    picked = jnp.take(source_blocks, jnp.where(wanted >= 0, wanted, blocks_here), axis=0, mode="clip")
     arrived = lax.all_to_all(picked, "node", split_axis=0, concat_axis=0, tiled=True)
     table = arrived.reshape(node_count * slot_len, lanes)
     source = edge_ends // (blocks_here * block_rows)

time: 298 us -> 280 us (0.940)
  Pallas kernels: 52.8 us -> 39.8 us
  other arithmetic: 10.7 us -> 5.55 us
    pallas_call x1, Pallas kernels: 52.8 us -> 39.8 us  [edge_scores(): pl.pallas_call(functools.partial(score_kernel, edges), grid_spec=grid_spe...]
    concatenate x1, other arithmetic: 7.35 us -> 0.09 us  [body(): source_blocks = jnp.concatenate([narrow, marks], axis=1)]
where the time goes in v3:
time: 280 us; the launch traced here: 279 us
  waiting for transfers between devices  184 us (66%)
  Pallas kernels  39.8 us (14%)
  blocking collectives  24.3 us (9%)
  local copies, waits for them, and re-layouts  13.2 us (5%)
  starting transfers between devices  11.1 us (4%)
  other arithmetic  5.55 us (2%)
    all_to_all x1, waiting for transfers between devices, body(): lax.all_to_all(picked, 'node', split_axis=0, concat_axis=0, tiled=True)  184 us
    pallas_call x1, Pallas kernels, edge_scores(): pl.pallas_call(functools.partial(score_kernel, edges), grid_spec=grid_spe...  39.8 us
    unnamed x1, blocking collectives  24.3 us
    all_to_all x1, starting transfers between devices, body(): lax.all_to_all(picked, 'node', split_axis=0, concat_axis=0, tiled=True)  11.1 us
    gather x1, local copies, waits for them, and re-layouts, body(): jnp.take(source_blocks, jnp.where(wanted >= 0, wanted, blocks_here), axis...  5.6 us
  transfers between devices with their start and end apart: 1, of which 1 were waited for; matrix products, arithmetic and copies ran while one was open for 1% of the time, Pallas kernels for 0%

profile of v3, /device:TPU:2, one launch (start us, length us, event | category | flops | bytes accessed | tf_op | source)
XLA Modules:
  0.0 279.4 jit_solution(17667474172696832586)
XLA Ops:
  0.6 1.7 reshape.62
  2.4 0.7 fusion.10
  3.0 0.1 broadcast_in_dim.15
  3.1 0.1 fusion.1
  3.2 5.6 %gather_fusion = bf16[64,520,128]{2,1,0:T(8,128)(2,1)} fusion(bf16[9,520,128]{2,1,0:T(8,128)(2,1)S(1)} %fusion.1, s32[1024]{0:T(1024)S(1)} %pad_clamp_fusion), kind=kCustom, calls=%fused_computation | custom fusion | bytes 17039616 | tf_op jit(solution)/shard_map/jit(_take)/gather | solution.py:133
  8.8 0.0 copy-start
  8.8 0.0 copy-start.1
  8.8 0.0 copy-start.2
  8.8 11.1 %all-to-all-start = ((bf16[64,520,128]{2,1,0:T(8,128)(2,1)}), bf16[64,520,128]{2,1,0:T(8,128)(2,1)}, u32[]{:S(2)}, u32[]{:S(2)}) async-start(bf16[64,520,128]{2,1,0:T(8,128)(2,1)} %gather_fusion), calls=%async_computation | async-start | bytes 17039360 | tf_op jit(solution)/shard_map/all_to_all | solution.py:134
  19.9 0.0 copy-done
  20.0 0.1 fusion.8
  20.1 0.6 copy.15
  20.7 0.0 copy-done.1
  20.7 1.4 copy.14.pid_ref
  22.0 1.3 dynamic-slice
  24.0 184.1 %all-to-all-done = bf16[64,520,128]{2,1,0:T(8,128)(2,1)} async-done(((bf16[64,520,128]{2,1,0:T(8,128)(2,1)}), bf16[64,520,128]{2,1,0:T(8,128)(2,1)}, u32[]{:S(2)}, u32[]{:S(2)}) %all-to-all-start) | async-done | bytes 8519712 | tf_op jit(solution)/shard_map/all_to_all | solution.py:134
  208.0 2.1 fusion.4
  210.1 0.4 fusion.3
  210.5 1.4 copy.13
  212.0 0.0 copy-done.2
  212.0 0.6 broadcast_in_dim.17.wo_ref
  212.6 39.8 %shard_map.86 = (f32[2048,1]{1,0:T(8,128)}, f32[1,1024]{1,0:T(1,128)}) custom-call(s32[4096]{0:T(1024)} %bitcast.14, bf16[33280,128]{1,0:T(8,128)(2,1)} %bitcast.2.table, f32[2048,2]{1,0:T(8,128)} %bitcast.13, bf16[1024,512]{1,0:T(8,128)(2,1)} %wb_ref.1, bf16[1024,512]{1,0:T(8,128)(2,1)} %wb_ref.1, f32[1,512]{1,0:T(1,128)} %bitcast.17, ...), custom_call_target="tpu_custom_call" | custom-call | flops 2147483648 | bytes 4194304 | tf_op jit(solution)/shard_map/pallas_call | solution.py:101
  252.3 24.3 %all-reduce.1 = f32[1024]{0:T(1024)S(1)} all-reduce(f32[1024]{0:T(1024)} %bitcast.16), channel_id=2, replica_groups=mesh['node'=64,'edge'=8] {'edge'}, use_global_device_ids=true, to_apply=%region_1.2.clone | all-reduce | flops 1024 | bytes 8192
  276.6 0.6 dynamic-slice.1
  277.2 2.2 reduce.1
  (4 shorter events, 0.0 us)
Async XLA Ops:
  8.8 11.1 %copy-start = (s32[2,2048]{1,0:T(2,128)S(1)}, s32[2,2048]{1,0:T(2,128)}, u32[]{:S(2)}) copy-start(s32[2,2048]{1,0:T(2,128)} %param.9) | copy-start | bytes 49156
  8.8 11.9 %copy-start.1 = (s32[2048]{0:T(1024)S(1)}, s32[2048]{0:T(1024)}, u32[]{:S(2)}) copy-start(s32[2048]{0:T(1024)} %param.10) | copy-start | bytes 24580
  8.8 203.2 %copy-start.2 = (bf16[512]{0:T(512)(128)(2,1)S(1)}, bf16[512]{0:T(512)(128)(2,1)}, u32[]{:S(2)}) copy-start(bf16[512]{0:T(512)(128)(2,1)} %param.13) | copy-start | bytes 3076
  8.8 199.2 %all-to-all-start = ((bf16[64,520,128]{2,1,0:T(8,128)(2,1)}), bf16[64,520,128]{2,1,0:T(8,128)(2,1)}, u32[]{:S(2)}, u32[]{:S(2)}) async-start(bf16[64,520,128]{2,1,0:T(8,128)(2,1)} %gather_fusion), calls=%async_computation | async-start | bytes 17039360 | tf_op jit(solution)/shard_map/all_to_all | solution.py:134

commit v4 on v3

--- a/solution.py
+++ b/solution.py
@@ -16,45 +16,39 @@
 
 
 def score_kernel(edges, pos_ref, table, mask_ref, wt_ref, wb_ref, bias_ref, wo_ref, pid_ref,
-                 score_ref, pool_ref, buf, wide, sems):
+                 score_ref, pool_ref, buf):
     step = pl.program_id(0)
-    steps = pl.num_programs(0)
-    parts = buf.shape[2] // TILE
-
-    def fetch(tile, slot):
-        base = tile * TILE
-
-        def one(r, carry):
-            dst = pl.ds(pl.multiple_of(r * parts, parts), parts)
-            for end in range(2):
-                src = pl.ds(pl.multiple_of(pos_ref[end * edges + base + r], parts), parts)
-                pltpu.make_async_copy(table.at[src], buf.at[end, slot, dst], sems.at[end, slot]).start()
-            return carry
-
-        lax.fori_loop(0, TILE, one, 0, unroll=8)
+    parts = buf.shape[1] // TILE
+    base = step * TILE
 
     @pl.when(step == 0)
     def _():
-        fetch(0, 0)
         pool_ref[...] = jnp.zeros_like(pool_ref)
 
-    slot = step % 2
+    half_rows = lax.broadcasted_iota(jnp.int32, (2 * parts, buf.shape[2]), 0) < parts
 
-    @pl.when(step + 1 < steps)
-    def _():
-        fetch(step + 1, 1 - slot)
+    def near(end, r, half):
+        p = pos_ref[end * edges + base + r]
+        group = table[pl.ds(pl.multiple_of((p // (2 * parts)) * (2 * parts), 2 * parts), 2 * parts), :]
+        group = group.astype(jnp.float32)
+        turned = pltpu.roll(group, parts, 0)
+        return jnp.where((p // parts) % 2 == half, group, turned)
 
-    for end in range(2):
-        pltpu.make_async_copy(table.at[pl.ds(0, TILE * parts)], buf.at[end, slot], sems.at[end, slot]).wait()
+    def pair(s, carry):
+        dst = pl.ds(pl.multiple_of(s * 2 * parts, 2 * parts), 2 * parts)
+        for end in range(2):
+            buf[end, dst, :] = jnp.where(half_rows, near(end, 2 * s, 0), near(end, 2 * s + 1, 1))
+        return carry
+
+    lax.fori_loop(0, TILE // 2, pair, 0, unroll=4)
 
     mask = mask_ref[...]
-    lanes = buf.shape[3]
+    lanes = buf.shape[2]
     preact = bias_ref[...]
     for end, w_ref in ((0, wt_ref), (1, wb_ref)):
-        wide[...] = buf[end, slot].astype(jnp.float32)
         keep = mask[:, end:end + 1] > 0
         for q in range(parts):
-            piece = wide[pl.ds(q, TILE, stride=parts), :]
+            piece = buf[end, pl.ds(q, TILE, stride=parts), :]
             piece = jnp.where(keep, piece, jnp.zeros_like(piece)).astype(jnp.bfloat16)
             preact = preact + jnp.dot(piece, w_ref[q * lanes:(q + 1) * lanes, :],
                                       preferred_element_type=jnp.float32)
@@ -80,7 +74,7 @@
         num_scalar_prefetch=1,
         grid=(tiles,),
         in_specs=[
-            pl.BlockSpec(memory_space=pl.ANY),
+            pl.BlockSpec(memory_space=pltpu.VMEM),
             pl.BlockSpec((TILE, 2), lambda i, p: (i, 0)),
             pl.BlockSpec((width, hid), lambda i, p: (0, 0)),
             pl.BlockSpec((width, hid), lambda i, p: (1, 0)),
@@ -93,9 +87,7 @@
             pl.BlockSpec((1, PAIRS_ROW), lambda i, p: (0, 0)),
         ],
         scratch_shapes=[
-            pltpu.VMEM((2, 2, TILE * parts, lanes), table.dtype),
-            pltpu.VMEM((TILE * parts, lanes), jnp.float32),
-            pltpu.SemaphoreType.DMA((2, 2)),
+            pltpu.VMEM((2, TILE * parts, lanes), jnp.float32),
         ],
     )
     scores, pooled = pl.pallas_call(
@@ -105,7 +97,7 @@
             jax.ShapeDtypeStruct((edges, 1), jnp.float32),
             jax.ShapeDtypeStruct((1, PAIRS_ROW), jnp.float32),
         ],
-        compiler_params=pltpu.CompilerParams(dimension_semantics=("arbitrary",)),
+        compiler_params=pltpu.CompilerParams(dimension_semantics=("arbitrary",), vmem_limit_bytes=48 * 1024 * 1024),
         cost_estimate=pl.CostEstimate(
             flops=2 * edges * 2 * width * hid, transcendentals=edges * hid,
             bytes_accessed=2 * edges * width * table.dtype.itemsize),

time: 280 us -> 302 us (1.079)
  Pallas kernels: 39.8 us -> 63 us
    pallas_call x1, Pallas kernels: 39.8 us -> 63 us  [edge_scores(): pl.pallas_call(functools.partial(score_kernel, edges), grid_spec=grid_spe...]
where the time goes in v4:
time: 302 us
  waiting for transfers between devices  186 us (62%)
  Pallas kernels  63 us (21%)
  blocking collectives  24 us (8%)
  starting transfers between devices  11.2 us (4%)
  local copies, waits for them, and re-layouts  11 us (4%)
  other arithmetic  5.55 us (2%)
    all_to_all x1, waiting for transfers between devices, body(): lax.all_to_all(picked, 'node', split_axis=0, concat_axis=0, tiled=True)  186 us
    pallas_call x1, Pallas kernels, edge_scores(): pl.pallas_call(functools.partial(score_kernel, edges), grid_spec=grid_spe...  63 us
    unnamed x1, blocking collectives  24 us
    all_to_all x1, starting transfers between devices, body(): lax.all_to_all(picked, 'node', split_axis=0, concat_axis=0, tiled=True)  11.2 us
  transfers between devices with their start and end apart: 1, of which 1 were waited for; matrix products, arithmetic and copies ran while one was open for 1% of the time, Pallas kernels for 0%

profile of v4, /device:TPU:2, one launch (start us, length us, event | category | flops | bytes accessed | tf_op | source)
XLA Modules:
  0.0 301.7 jit_solution(14871301118119629457)
XLA Ops:
  0.6 1.7 reshape.62
  2.4 0.7 fusion.10
  3.0 0.1 broadcast_in_dim.15
  3.1 0.1 fusion.1
  3.2 5.6 %gather_fusion = bf16[64,520,128]{2,1,0:T(8,128)(2,1)} fusion(bf16[9,520,128]{2,1,0:T(8,128)(2,1)S(1)} %fusion.1, s32[1024]{0:T(1024)S(1)} %pad_clamp_fusion), kind=kCustom, calls=%fused_computation | custom fusion | bytes 17039616 | tf_op jit(solution)/shard_map/jit(_take)/gather | solution.py:125
  8.8 0.0 copy-start.3
  8.8 0.0 copy-start.4
  8.8 0.0 copy-start.5
  8.8 11.2 %all-to-all-start = ((bf16[64,520,128]{2,1,0:T(8,128)(2,1)}), bf16[64,520,128]{2,1,0:T(8,128)(2,1)}, u32[]{:S(2)}, u32[]{:S(2)}) async-start(bf16[64,520,128]{2,1,0:T(8,128)(2,1)} %gather_fusion), calls=%async_computation | async-start | bytes 17039360 | tf_op jit(solution)/shard_map/all_to_all | solution.py:126
  20.0 0.0 copy-start
  20.0 0.0 copy-start.2
  20.0 0.0 copy-done.3
  20.0 0.1 fusion.8
  20.2 0.0 copy-done.4
  20.2 0.4 copy.14.pid_ref
  20.6 1.3 dynamic-slice
  22.5 185.6 %all-to-all-done = bf16[64,520,128]{2,1,0:T(8,128)(2,1)} async-done(((bf16[64,520,128]{2,1,0:T(8,128)(2,1)}), bf16[64,520,128]{2,1,0:T(8,128)(2,1)}, u32[]{:S(2)}, u32[]{:S(2)}) %all-to-all-start) | async-done | bytes 8519712 | tf_op jit(solution)/shard_map/all_to_all | solution.py:126
  208.1 2.1 fusion.4
  210.2 0.4 fusion.3
  210.6 0.4 copy.13
  211.0 0.0 copy-done.5
  211.0 0.0 copy-done
  211.0 0.0 copy-done.2
  211.0 63.0 %shard_map.86 = (f32[2048,1]{1,0:T(8,128)S(1)}, f32[1,1024]{1,0:T(1,128)S(1)}) custom-call(s32[4096]{0:T(1024)S(1)} %bitcast.14, bf16[33280,128]{1,0:T(8,128)(2,1)} %bitcast.2.table, f32[2048,2]{1,0:T(8,128)S(1)} %bitcast.13, bf16[1024,512]{1,0:T(8,128)(2,1)S(1)} %copy-done, bf16[1024,512]{1,0:T(8,128)(2,1)S(1)} %copy-done, f32[1,512]{1,0:T(1,128)S(1)} %bitcast.16, ...), custom_call_target="tpu_custom_call" | custom-call | flops 2147483648 | bytes 4194304 | tf_op jit(solution)/shard_map/pallas_call | solution.py:93
  274.0 0.0 copy-start.1
  274.0 1.0 copy-done.1
  275.0 24.0 %all-reduce.1 = f32[1024]{0:T(1024)S(1)} all-reduce(f32[1024]{0:T(1024)S(1)} %bitcast.15), channel_id=2, replica_groups=mesh['node'=64,'edge'=8] {'edge'}, use_global_device_ids=true, to_apply=%region_1.2.clone | all-reduce | flops 1024 | bytes 8192
  299.0 0.6 dynamic-slice.1
  299.6 2.2 reduce.1
  (6 shorter events, 0.0 us)
Async XLA Ops:
  8.8 11.2 %copy-start.3 = (s32[2,2048]{1,0:T(2,128)S(1)}, s32[2,2048]{1,0:T(2,128)}, u32[]{:S(2)}) copy-start(s32[2,2048]{1,0:T(2,128)} %param.9) | copy-start | bytes 49156
  8.8 11.4 %copy-start.4 = (s32[2048]{0:T(1024)S(1)}, s32[2048]{0:T(1024)}, u32[]{:S(2)}) copy-start(s32[2048]{0:T(1024)} %param.10) | copy-start | bytes 24580
  8.8 202.2 %copy-start.5 = (bf16[512]{0:T(512)(128)(2,1)S(1)}, bf16[512]{0:T(512)(128)(2,1)}, u32[]{:S(2)}) copy-start(bf16[512]{0:T(512)(128)(2,1)} %param.13) | copy-start | bytes 3076
  8.8 199.3 %all-to-all-start = ((bf16[64,520,128]{2,1,0:T(8,128)(2,1)}), bf16[64,520,128]{2,1,0:T(8,128)(2,1)}, u32[]{:S(2)}, u32[]{:S(2)}) async-start(bf16[64,520,128]{2,1,0:T(8,128)(2,1)} %gather_fusion), calls=%async_computation | async-start | bytes 17039360 | tf_op jit(solution)/shard_map/all_to_all | solution.py:126
  20.0 191.0 %copy-start = (bf16[1024,512]{1,0:T(8,128)(2,1)S(1)}, bf16[1024,512]{1,0:T(8,128)(2,1)}, u32[]{:S(2)}) copy-start(bf16[1024,512]{1,0:T(8,128)(2,1)} %wb_ref.1) | copy-start | bytes 3145732
  20.0 191.0 %copy-start.2 = (f32[512]{0:T(512)S(1)}, f32[512]{0:T(512)}, u32[]{:S(2)}) copy-start(f32[512]{0:T(512)} %param.12) | copy-start | bytes 6148
  274.0 1.0 copy-start.1

commit v5 on v3

v5 whole, which is shorter than its diff:
```python
import functools

import jax
import jax.numpy as jnp
from jax import lax
from jax.experimental import pallas as pl
from jax.experimental.pallas import tpu as pltpu
from jax.sharding import PartitionSpec as P

PAIRS_ROW = 1024
TILE = 256
LATE_TILE = 128
EARLY_ROWS = 96


def gelu_tanh(x):
    return x * (0.5 * (1.0 + jnp.tanh(0.7978845608028654 * (x + 0.044715 * (x * x * x)))))


def early_kernel(edges, pos_ref, table, mask_ref, wt_ref, wb_ref, part_ref, buf, wide, sems):
    step = pl.program_id(0)
    steps = pl.num_programs(0)
    parts = buf.shape[2] // TILE
    lanes = buf.shape[3]

    def fetch(tile, slot):
        base = tile * TILE

        def one(r, carry):
            dst = pl.ds(pl.multiple_of(r * parts, parts), parts)
            for end in range(2):
                src = pl.ds(pl.multiple_of(pos_ref[end * edges + base + r], parts), parts)
                pltpu.make_async_copy(table.at[src], buf.at[end, slot, dst], sems.at[end, slot]).start()
            return carry

        lax.fori_loop(0, TILE, one, 0, unroll=8)

    @pl.when(step == 0)
    def _():
        fetch(0, 0)

    slot = step % 2

    @pl.when(step + 1 < steps)
    def _():
        fetch(step + 1, 1 - slot)

    for end in range(2):
        pltpu.make_async_copy(table.at[pl.ds(0, TILE * parts)], buf.at[end, slot], sems.at[end, slot]).wait()

    mask = mask_ref[...]
    total = None
    for end, w_ref in ((0, wt_ref), (1, wb_ref)):
        wide[...] = buf[end, slot].astype(jnp.float32)
        keep = mask[:, end:end + 1] > 0
        for q in range(parts):
            piece = wide[pl.ds(q, TILE, stride=parts), :]
            piece = jnp.where(keep, piece, jnp.zeros_like(piece)).astype(jnp.bfloat16)
            term = jnp.dot(piece, w_ref[q * lanes:(q + 1) * lanes, :], preferred_element_type=jnp.float32)
            total = term if total is None else total + term
    part_ref[...] = total


def late_kernel(edges, pos_ref, table, mask_ref, part_ref, wt_ref, wb_ref, bias_ref, wo_ref, pid_ref,
                score_ref, pool_ref, buf, wide, sems):
    step = pl.program_id(0)
    parts = buf.shape[1] // LATE_TILE
    lanes = buf.shape[2]
    base = step * LATE_TILE

    @pl.when(step == 0)
    def _():
        pool_ref[...] = jnp.zeros_like(pool_ref)

    def copy(end, r):
        src = pl.ds(pl.multiple_of(jnp.maximum(pos_ref[end * edges + base + r], 0), parts), parts)
        dst = pl.ds(pl.multiple_of(r * parts, parts), parts)
        return pltpu.make_async_copy(table.at[src], buf.at[end, dst], sems.at[end, r])

    def start(r, carry):
        for end in range(2):
            @pl.when(pos_ref[end * edges + base + r] >= 0)
            def _():
                copy(end, r).start()
        return carry

    def finish(r, carry):
        for end in range(2):
            @pl.when(pos_ref[end * edges + base + r] >= 0)
            def _():
                copy(end, r).wait()
        return carry

    lax.fori_loop(0, LATE_TILE, start, 0, unroll=8)
    lax.fori_loop(0, LATE_TILE, finish, 0, unroll=8)

    mask = mask_ref[...]
    preact = part_ref[...]
    for end, w_ref in ((0, wt_ref), (1, wb_ref)):
        wide[...] = buf[end].astype(jnp.float32)
        keep = mask[:, end:end + 1] > 0
        for q in range(parts):
            piece = wide[pl.ds(q, LATE_TILE, stride=parts), :]
            piece = jnp.where(keep, piece, jnp.zeros_like(piece)).astype(jnp.bfloat16)
            preact = preact + jnp.dot(piece, w_ref[q * lanes:(q + 1) * lanes, :],
                                      preferred_element_type=jnp.float32)
    hidden = gelu_tanh(preact + bias_ref[...])
    scores = jnp.sum(hidden * wo_ref[0:1, :], axis=1, keepdims=True)
    score_ref[...] = scores
    pair_range = lax.broadcasted_iota(jnp.int32, (LATE_TILE, PAIRS_ROW), 1)
    picked = jnp.where(pid_ref[...] == pair_range, scores, 0.0)
    pool_ref[...] += jnp.sum(picked, axis=0, keepdims=True)


def early_products(position, mask, table, w_first):
    edges = position.shape[1]
    lanes = table.shape[1]
    width = w_first.shape[0] // 2
    parts = width // lanes
    hid = w_first.shape[1]
    grid_spec = pltpu.PrefetchScalarGridSpec(
        num_scalar_prefetch=1,
        grid=(edges // TILE,),
        in_specs=[
            pl.BlockSpec(memory_space=pl.ANY),
            pl.BlockSpec((TILE, 2), lambda i, p: (i, 0)),
            pl.BlockSpec((width, hid), lambda i, p: (0, 0)),
            pl.BlockSpec((width, hid), lambda i, p: (1, 0)),
        ],
        out_specs=pl.BlockSpec((TILE, hid), lambda i, p: (i, 0)),
        scratch_shapes=[
            pltpu.VMEM((2, 2, TILE * parts, lanes), table.dtype),
            pltpu.VMEM((TILE * parts, lanes), jnp.float32),
            pltpu.SemaphoreType.DMA((2, 2)),
        ],
    )
    return pl.pallas_call(
        functools.partial(early_kernel, edges),
        grid_spec=grid_spec,
        out_shape=jax.ShapeDtypeStruct((edges, hid), jnp.float32),
        compiler_params=pltpu.CompilerParams(dimension_semantics=("arbitrary",)),
        cost_estimate=pl.CostEstimate(
            flops=2 * edges * 2 * width * hid, transcendentals=0,
            bytes_accessed=2 * edges * width * table.dtype.itemsize + edges * hid * 4),
    )(position.reshape(2 * edges), table, mask, w_first, w_first)


def late_scores(position, mask, partial, pair_ids, table, w_first, b_first, w_second):
    edges = position.shape[1]
    lanes = table.shape[1]
    width = w_first.shape[0] // 2
    parts = width // lanes
    hid = w_first.shape[1]
    wo8 = jnp.broadcast_to(w_second.astype(jnp.float32)[None, :], (8, hid))
    grid_spec = pltpu.PrefetchScalarGridSpec(
        num_scalar_prefetch=1,
        grid=(edges // LATE_TILE,),
        in_specs=[
            pl.BlockSpec(memory_space=pl.ANY),
            pl.BlockSpec((LATE_TILE, 2), lambda i, p: (i, 0)),
            pl.BlockSpec((LATE_TILE, hid), lambda i, p: (i, 0)),
            pl.BlockSpec((width, hid), lambda i, p: (0, 0)),
            pl.BlockSpec((width, hid), lambda i, p: (1, 0)),
            pl.BlockSpec((1, hid), lambda i, p: (0, 0)),
            pl.BlockSpec((8, hid), lambda i, p: (0, 0)),
            pl.BlockSpec((LATE_TILE, 1), lambda i, p: (i, 0)),
        ],
        out_specs=[
            pl.BlockSpec((LATE_TILE, 1), lambda i, p: (i, 0)),
            pl.BlockSpec((1, PAIRS_ROW), lambda i, p: (0, 0)),
        ],
        scratch_shapes=[
            pltpu.VMEM((2, LATE_TILE * parts, lanes), table.dtype),
            pltpu.VMEM((LATE_TILE * parts, lanes), jnp.float32),
            pltpu.SemaphoreType.DMA((2, LATE_TILE)),
        ],
    )
    scores, pooled = pl.pallas_call(
        functools.partial(late_kernel, edges),
        grid_spec=grid_spec,
        out_shape=[
            jax.ShapeDtypeStruct((edges, 1), jnp.float32),
            jax.ShapeDtypeStruct((1, PAIRS_ROW), jnp.float32),
        ],
        compiler_params=pltpu.CompilerParams(dimension_semantics=("arbitrary",)),
        cost_estimate=pl.CostEstimate(
            flops=2 * edges * 2 * width * hid, transcendentals=edges * hid,
            bytes_accessed=edges * width * table.dtype.itemsize + edges * hid * 4),
    )(position.reshape(2 * edges), table, mask, partial, w_first, w_first, b_first.reshape(1, hid), wo8,
      pair_ids.reshape(edges, 1))
    return scores.reshape(edges), pooled.reshape(PAIRS_ROW)


def body(embedding, send_list, edge_ends, pair_index, w_first, b_first, w_second):
    node_count = lax.axis_size("node")
    node_self = lax.axis_index("node")
    blocks_here = embedding.shape[0]
    block_rows = embedding.shape[1]
    feature_width = embedding.shape[2]
    lanes = 128
    parts = feature_width // lanes
    early_len = EARLY_ROWS * parts
    late_len = (block_rows - EARLY_ROWS) * parts
    slot_len = early_len + 8
    wanted = send_list[0, 0]
    pick = jnp.where(wanted >= 0, wanted, blocks_here)
    narrow = embedding.reshape(blocks_here, block_rows * parts, lanes)
    narrow = jnp.concatenate([narrow, jnp.zeros((1, block_rows * parts, lanes), embedding.dtype)], axis=0)
    marks = jnp.arange(blocks_here + 1, dtype=jnp.int32)
    marks = jnp.where(marks < blocks_here, marks, -1).astype(embedding.dtype)
    marks = jnp.broadcast_to(marks[:, None, None], (blocks_here + 1, 8, lanes))
    early_source = jnp.concatenate([narrow[:, :early_len], marks], axis=1)
    late_source = narrow[:, early_len:]
    early_picked = jnp.take(early_source, pick, axis=0, mode="clip")
    late_picked = jnp.take(late_source, pick, axis=0, mode="clip")
    early_arrived = lax.all_to_all(early_picked, "node", split_axis=0, concat_axis=0, tiled=True)
    late_picked, early_arrived = lax.optimization_barrier((late_picked, early_arrived))
    late_arrived = lax.all_to_all(late_picked, "node", split_axis=0, concat_axis=0, tiled=True)
    early_table = early_arrived.reshape(node_count * slot_len, lanes)
    late_table = late_arrived.reshape(node_count * late_len, lanes)
    source = edge_ends // (blocks_here * block_rows)
    block_of = (edge_ends // block_rows) % blocks_here
    within = edge_ends % block_rows
    early = within < EARLY_ROWS
    early_position = source * slot_len + jnp.where(early, within, 0) * parts
    late_position = jnp.where(early, -1, source * late_len + (within - EARLY_ROWS) * parts)
    sent = early_arrived[:, early_len, 0].astype(jnp.int32)
    located = jnp.any((source[..., None] == jnp.arange(node_count, dtype=jnp.int32))
                      & (block_of[..., None] == sent), axis=-1)
    early_mask = (located & early).T.astype(jnp.float32)
    late_mask = (located & ~early).T.astype(jnp.float32)
    partial = early_products(early_position, early_mask, early_table, w_first)
    pair_ids = pair_index - node_self * PAIRS_ROW
    edge_score, pooled_sum = late_scores(late_position, late_mask, partial, pair_ids, late_table,
                                         w_first, b_first, w_second)
    pair_cost = lax.psum_scatter(pooled_sum, "edge", scatter_dimension=0, tiled=True)
    return (edge_score, pair_cost)


def solution(mesh):
    return jax.shard_map(
        body,
        mesh=mesh,
        in_specs=(
            P("node", None, None),
            P("edge", "node", None),
            P(None, ("node", "edge")),
            P(("node", "edge")),
            P(),
            P(),
            P(),
        ),
        out_specs=(P(("node", "edge")), P(("node", "edge"))),
        check_vma=False,
    )
```

time: 280 us -> 325 us (1.16)
  the two profiles are of different devices: /device:TPU:2 before, /device:TPU:10 now
where the time goes in v5:
time: 325 us; the launch traced here: 324 us
  waiting for transfers between devices  141 us (43%)
  Pallas kernels  113 us (35%)
  blocking collectives  23.1 us (7%)
  starting transfers between devices  17.5 us (5%)
  local copies, waits for them, and re-layouts  17.1 us (5%)
  other arithmetic  10.9 us (3%)
    all_to_all x1, waiting for transfers between devices, body(): lax.all_to_all(early_picked, 'node', split_axis=0, concat_axis=0, tiled=T...  141 us
    pallas_call x1, Pallas kernels, late_scores(): pl.pallas_call(functools.partial(late_kernel, edges), grid_spec=grid_spec...  75.5 us
    pallas_call x1, Pallas kernels, early_products(): pl.pallas_call(functools.partial(early_kernel, edges), grid_spec=grid_spe...  37.3 us
    unnamed x1, blocking collectives  23.1 us
    all_to_all x1, starting transfers between devices, body(): lax.all_to_all(early_picked, 'node', split_axis=0, concat_axis=0, tiled=T...  10.9 us
    all_to_all x1, starting transfers between devices, body(): lax.all_to_all(late_picked, 'node', split_axis=0, concat_axis=0, tiled=True)  6.52 us
  transfers between devices with their start and end apart: 2, of which 1 were waited for; matrix products, arithmetic and copies ran while one was open for 6% of the time, Pallas kernels for 12%

profile of v5, /device:TPU:10, one launch (start us, length us, event | category | flops | bytes accessed | tf_op | source)
XLA Modules:
  0.0 324.0 jit_solution(5647346722941500480)
XLA Ops:
  0.6 0.7 fusion.6
  1.3 1.7 reshape.68
  3.0 0.1 pad_slice_fusion
  3.1 0.1 broadcast_in_dim.38
  3.2 0.1 pad_maximum_fusion
  3.2 4.1 %gather_fusion.1 = bf16[64,392,128]{2,1,0:T(8,128)(2,1)} fusion(bf16[9,392,128]{2,1,0:T(8,128)(2,1)S(1)} %pad_maximum_fusion, s32[1024]{0:T(1024)S(1)} %pad_clamp_fusion), kind=kCustom, calls=%fused_computation.1 | custom fusion | bytes 12845312 | tf_op jit(solution)/shard_map/jit(_take)/gather | solution.py:214
  7.3 10.9 %all-to-all-start = ((bf16[64,392,128]{2,1,0:T(8,128)(2,1)}), bf16[64,392,128]{2,1,0:T(8,128)(2,1)}, u32[]{:S(2)}, u32[]{:S(2)}) async-start(bf16[64,392,128]{2,1,0:T(8,128)(2,1)} %gather_fusion.1), calls=%async_computation | async-start | bytes 12845056 | tf_op jit(solution)/shard_map/all_to_all | solution.py:216
  18.3 2.2 gather_fusion
  20.5 0.0 copy-start
  20.5 0.0 copy-start.1
  20.5 141.2 %all-to-all-done = bf16[64,392,128]{2,1,0:T(8,128)(2,1)} async-done(((bf16[64,392,128]{2,1,0:T(8,128)(2,1)}), bf16[64,392,128]{2,1,0:T(8,128)(2,1)}, u32[]{:S(2)}, u32[]{:S(2)}) %all-to-all-start) | async-done | bytes 6422560 | tf_op jit(solution)/shard_map/all_to_all | solution.py:216
  161.7 6.5 %all-to-all-start.1 = ((bf16[64,128,128]{2,1,0:T(8,128)(2,1)}), bf16[64,128,128]{2,1,0:T(8,128)(2,1)}, u32[]{:S(2)}, u32[]{:S(2)}) async-start(bf16[64,128,128]{2,1,0:T(8,128)(2,1)} %gather_fusion), calls=%async_computation.1 | async-start | bytes 4194304 | tf_op jit(solution)/shard_map/all_to_all | solution.py:218
  168.3 0.0 copy-done
  168.3 0.4 copy.80
  168.7 0.5 copy.83
  169.2 0.0 copy-done.1
  169.2 1.4 copy.95.pid_ref
  170.5 2.9 multiply_add_fusion
  173.4 1.6 copy.93
  175.0 0.6 copy.97
  175.6 0.3 copy.90
  175.9 0.3 copy.88
  176.3 0.6 add_select_fusion.4
  176.9 0.3 copy.87
  177.2 0.6 copy.96
  177.8 1.3 dynamic-slice
  179.8 2.1 convert_reduce_fusion
  181.9 0.4 fusion.3
  182.2 0.5 copy.91
  182.7 2.0 convert_bitcast_fusion
  184.7 0.0 copy-start.2
  184.7 37.3 %shard_map.86.part_ref = f32[2048,512]{1,0:T(8,128)} custom-call(s32[4096]{0:T(1024)} %bitcast.19, bf16[25088,128]{1,0:T(8,128)(2,1)} %bitcast.4.table, f32[2048,2]{1,0:T(8,128)} %get-tuple-element.12.mask_ref, bf16[1024,512]{1,0:T(8,128)(2,1)} %wb_ref.3, bf16[1024,512]{1,0:T(8,128)(2,1)} %wb_ref.3), custom_call_target="tpu_custom_call" | custom-call | flops 2147483648 | bytes 8388608 | tf_op jit(solution)/shard_map/pallas_call | solution.py:137
  222.0 0.0 all-to-all-done.1
  222.0 0.0 copy-done.2
  222.0 0.6 broadcast_in_dim.39.wo_ref
  222.6 75.5 %shard_map.87 = (f32[2048,1]{1,0:T(8,128)}, f32[1,1024]{1,0:T(1,128)}) custom-call(s32[4096]{0:T(1024)} %bitcast.18, bf16[8192,128]{1,0:T(8,128)(2,1)} %bitcast.2.table, f32[2048,2]{1,0:T(8,128)} %get-tuple-element.13.mask_ref, f32[2048,512]{1,0:T(8,128)} %shard_map.86.part_ref, bf16[1024,512]{1,0:T(8,128)(2,1)} %wb_ref.3, bf16[1024,512]{1,0:T(8,128)(2,1)} %wb_ref.3, ...), custom_call_target="tpu_custom_call" | custom-call | flops 2147483648 | bytes 6291456 | tf_op jit(solution)/shard_map/pallas_call | solution.py:178
  298.2 23.1 %all-reduce.1 = f32[1024]{0:T(1024)S(1)} all-reduce(f32[1024]{0:T(1024)} %bitcast.23), channel_id=2, replica_groups=mesh['node'=64,'edge'=8] {'edge'}, use_global_device_ids=true, to_apply=%region_1.2.clone | all-reduce | flops 1024 | bytes 8192
  321.2 2.2 reduce.1
  323.4 0.6 dynamic-slice.1
  (5 shorter events, 0.1 us)
Async XLA Ops:
  7.3 154.4 %all-to-all-start = ((bf16[64,392,128]{2,1,0:T(8,128)(2,1)}), bf16[64,392,128]{2,1,0:T(8,128)(2,1)}, u32[]{:S(2)}, u32[]{:S(2)}) async-start(bf16[64,392,128]{2,1,0:T(8,128)(2,1)} %gather_fusion.1), calls=%async_computation | async-start | bytes 12845056 | tf_op jit(solution)/shard_map/all_to_all | solution.py:216
  20.5 147.8 %copy-start = (s32[2,2048]{1,0:T(2,128)S(1)}, s32[2,2048]{1,0:T(2,128)}, u32[]{:S(2)}) copy-start(s32[2,2048]{1,0:T(2,128)} %param.9) | copy-start | bytes 49156
  20.5 148.7 %copy-start.1 = (s32[2048]{0:T(1024)S(1)}, s32[2048]{0:T(1024)}, u32[]{:S(2)}) copy-start(s32[2048]{0:T(1024)} %param.10) | copy-start | bytes 24580
  161.7 60.3 %all-to-all-start.1 = ((bf16[64,128,128]{2,1,0:T(8,128)(2,1)}), bf16[64,128,128]{2,1,0:T(8,128)(2,1)}, u32[]{:S(2)}, u32[]{:S(2)}) async-start(bf16[64,128,128]{2,1,0:T(8,128)(2,1)} %gather_fusion), calls=%async_computation.1 | async-start | bytes 4194304 | tf_op jit(solution)/shard_map/all_to_all | solution.py:218
  184.7 37.3 %copy-start.2 = (bf16[512]{0:T(512)(128)(2,1)S(1)}, bf16[512]{0:T(512)(128)(2,1)}, u32[]{:S(2)}) copy-start(bf16[512]{0:T(512)(128)(2,1)} %param.13) | copy-start | bytes 3076

commit v6 on v5

--- a/solution.py
+++ b/solution.py
@@ -9,7 +9,7 @@
 
 PAIRS_ROW = 1024
 TILE = 256
-LATE_TILE = 128
+LATE_TILE = 256
 EARLY_ROWS = 96
 
 
@@ -61,55 +61,27 @@
     part_ref[...] = total
 
 
-def late_kernel(edges, pos_ref, table, mask_ref, part_ref, wt_ref, wb_ref, bias_ref, wo_ref, pid_ref,
-                score_ref, pool_ref, buf, wide, sems):
+def late_kernel(idx_ref, part_ref, table_ref, wt_ref, wb_ref, bias_ref, wo_ref, pid_ref, score_ref, pool_ref):
     step = pl.program_id(0)
-    parts = buf.shape[1] // LATE_TILE
-    lanes = buf.shape[2]
-    base = step * LATE_TILE
 
     @pl.when(step == 0)
     def _():
         pool_ref[...] = jnp.zeros_like(pool_ref)
 
-    def copy(end, r):
-        src = pl.ds(pl.multiple_of(jnp.maximum(pos_ref[end * edges + base + r], 0), parts), parts)
-        dst = pl.ds(pl.multiple_of(r * parts, parts), parts)
-        return pltpu.make_async_copy(table.at[src], buf.at[end, dst], sems.at[end, r])
-
-    def start(r, carry):
-        for end in range(2):
-            @pl.when(pos_ref[end * edges + base + r] >= 0)
-            def _():
-                copy(end, r).start()
-        return carry
-
-    def finish(r, carry):
-        for end in range(2):
-            @pl.when(pos_ref[end * edges + base + r] >= 0)
-            def _():
-                copy(end, r).wait()
-        return carry
-
-    lax.fori_loop(0, LATE_TILE, start, 0, unroll=8)
-    lax.fori_loop(0, LATE_TILE, finish, 0, unroll=8)
-
-    mask = mask_ref[...]
+    idx = idx_ref[...]
+    rows = table_ref.shape[0]
+    slots = lax.broadcasted_iota(jnp.int32, (LATE_TILE, rows), 1)
     preact = part_ref[...]
     for end, w_ref in ((0, wt_ref), (1, wb_ref)):
-        wide[...] = buf[end].astype(jnp.float32)
-        keep = mask[:, end:end + 1] > 0
-        for q in range(parts):
-            piece = wide[pl.ds(q, LATE_TILE, stride=parts), :]
-            piece = jnp.where(keep, piece, jnp.zeros_like(piece)).astype(jnp.bfloat16)
-            preact = preact + jnp.dot(piece, w_ref[q * lanes:(q + 1) * lanes, :],
-                                      preferred_element_type=jnp.float32)
+        onehot = (idx[:, end:end + 1] == slots).astype(table_ref.dtype)
+        picked = jnp.dot(onehot, table_ref[...], preferred_element_type=jnp.float32).astype(table_ref.dtype)
+        preact = preact + jnp.dot(picked, w_ref[...], preferred_element_type=jnp.float32)
     hidden = gelu_tanh(preact + bias_ref[...])
     scores = jnp.sum(hidden * wo_ref[0:1, :], axis=1, keepdims=True)
     score_ref[...] = scores
     pair_range = lax.broadcasted_iota(jnp.int32, (LATE_TILE, PAIRS_ROW), 1)
-    picked = jnp.where(pid_ref[...] == pair_range, scores, 0.0)
-    pool_ref[...] += jnp.sum(picked, axis=0, keepdims=True)
+    pooled = jnp.where(pid_ref[...] == pair_range, scores, 0.0)
+    pool_ref[...] += jnp.sum(pooled, axis=0, keepdims=True)
 
 
 def early_products(position, mask, table, w_first):
@@ -145,49 +117,37 @@
     )(position.reshape(2 * edges), table, mask, w_first, w_first)
 
 
-def late_scores(position, mask, partial, pair_ids, table, w_first, b_first, w_second):
-    edges = position.shape[1]
-    lanes = table.shape[1]
-    width = w_first.shape[0] // 2
-    parts = width // lanes
+def late_scores(late_index, partial, pair_ids, table, w_first, b_first, w_second):
+    edges = late_index.shape[1]
+    rows, width = table.shape
     hid = w_first.shape[1]
     wo8 = jnp.broadcast_to(w_second.astype(jnp.float32)[None, :], (8, hid))
-    grid_spec = pltpu.PrefetchScalarGridSpec(
-        num_scalar_prefetch=1,
+    scores, pooled = pl.pallas_call(
+        late_kernel,
         grid=(edges // LATE_TILE,),
         in_specs=[
-            pl.BlockSpec(memory_space=pl.ANY),
-            pl.BlockSpec((LATE_TILE, 2), lambda i, p: (i, 0)),
-            pl.BlockSpec((LATE_TILE, hid), lambda i, p: (i, 0)),
-            pl.BlockSpec((width, hid), lambda i, p: (0, 0)),
-            pl.BlockSpec((width, hid), lambda i, p: (1, 0)),
-            pl.BlockSpec((1, hid), lambda i, p: (0, 0)),
-            pl.BlockSpec((8, hid), lambda i, p: (0, 0)),
-            pl.BlockSpec((LATE_TILE, 1), lambda i, p: (i, 0)),
+            pl.BlockSpec((LATE_TILE, 2), lambda i: (i, 0)),
+            pl.BlockSpec((LATE_TILE, hid), lambda i: (i, 0)),
+            pl.BlockSpec((rows, width), lambda i: (0, 0)),
+            pl.BlockSpec((width, hid), lambda i: (0, 0)),
+            pl.BlockSpec((width, hid), lambda i: (1, 0)),
+            pl.BlockSpec((1, hid), lambda i: (0, 0)),
+            pl.BlockSpec((8, hid), lambda i: (0, 0)),
+            pl.BlockSpec((LATE_TILE, 1), lambda i: (i, 0)),
         ],
         out_specs=[
-            pl.BlockSpec((LATE_TILE, 1), lambda i, p: (i, 0)),
-            pl.BlockSpec((1, PAIRS_ROW), lambda i, p: (0, 0)),
-        ],
-        scratch_shapes=[
-            pltpu.VMEM((2, LATE_TILE * parts, lanes), table.dtype),
-            pltpu.VMEM((LATE_TILE * parts, lanes), jnp.float32),
-            pltpu.SemaphoreType.DMA((2, LATE_TILE)),
-        ],
-    )
-    scores, pooled = pl.pallas_call(
-        functools.partial(late_kernel, edges),
-        grid_spec=grid_spec,
+            pl.BlockSpec((LATE_TILE, 1), lambda i: (i, 0)),
+            pl.BlockSpec((1, PAIRS_ROW), lambda i: (0, 0)),
+        ],
         out_shape=[
             jax.ShapeDtypeStruct((edges, 1), jnp.float32),
             jax.ShapeDtypeStruct((1, PAIRS_ROW), jnp.float32),
         ],
         compiler_params=pltpu.CompilerParams(dimension_semantics=("arbitrary",)),
         cost_estimate=pl.CostEstimate(
-            flops=2 * edges * 2 * width * hid, transcendentals=edges * hid,
-            bytes_accessed=edges * width * table.dtype.itemsize + edges * hid * 4),
-    )(position.reshape(2 * edges), table, mask, partial, w_first, w_first, b_first.reshape(1, hid), wo8,
-      pair_ids.reshape(edges, 1))
+            flops=2 * edges * 2 * (rows + hid) * width, transcendentals=edges * hid,
+            bytes_accessed=rows * width * 2 + edges * hid * 4),
+    )(late_index.T, partial, table, w_first, w_first, b_first.reshape(1, hid), wo8, pair_ids.reshape(edges, 1))
     return scores.reshape(edges), pooled.reshape(PAIRS_ROW)
 
 
@@ -200,7 +160,6 @@
     lanes = 128
     parts = feature_width // lanes
     early_len = EARLY_ROWS * parts
-    late_len = (block_rows - EARLY_ROWS) * parts
     slot_len = early_len + 8
     wanted = send_list[0, 0]
     pick = jnp.where(wanted >= 0, wanted, blocks_here)
@@ -210,29 +169,28 @@
     marks = jnp.where(marks < blocks_here, marks, -1).astype(embedding.dtype)
     marks = jnp.broadcast_to(marks[:, None, None], (blocks_here + 1, 8, lanes))
     early_source = jnp.concatenate([narrow[:, :early_len], marks], axis=1)
-    late_source = narrow[:, early_len:]
+    late_rows = block_rows - EARLY_ROWS
+    late_source = jnp.concatenate([embedding[:, EARLY_ROWS:], jnp.zeros((1, late_rows, feature_width), embedding.dtype)], axis=0)
     early_picked = jnp.take(early_source, pick, axis=0, mode="clip")
     late_picked = jnp.take(late_source, pick, axis=0, mode="clip")
     early_arrived = lax.all_to_all(early_picked, "node", split_axis=0, concat_axis=0, tiled=True)
     late_picked, early_arrived = lax.optimization_barrier((late_picked, early_arrived))
     late_arrived = lax.all_to_all(late_picked, "node", split_axis=0, concat_axis=0, tiled=True)
     early_table = early_arrived.reshape(node_count * slot_len, lanes)
-    late_table = late_arrived.reshape(node_count * late_len, lanes)
+    late_table = late_arrived.reshape(node_count * late_rows, feature_width)
     source = edge_ends // (blocks_here * block_rows)
     block_of = (edge_ends // block_rows) % blocks_here
     within = edge_ends % block_rows
     early = within < EARLY_ROWS
     early_position = source * slot_len + jnp.where(early, within, 0) * parts
-    late_position = jnp.where(early, -1, source * late_len + (within - EARLY_ROWS) * parts)
     sent = early_arrived[:, early_len, 0].astype(jnp.int32)
     located = jnp.any((source[..., None] == jnp.arange(node_count, dtype=jnp.int32))
                       & (block_of[..., None] == sent), axis=-1)
     early_mask = (located & early).T.astype(jnp.float32)
-    late_mask = (located & ~early).T.astype(jnp.float32)
+    late_index = jnp.where(located & ~early, source * late_rows + within - EARLY_ROWS, -1)
     partial = early_products(early_position, early_mask, early_table, w_first)
     pair_ids = pair_index - node_self * PAIRS_ROW
-    edge_score, pooled_sum = late_scores(late_position, late_mask, partial, pair_ids, late_table,
-                                         w_first, b_first, w_second)
+    edge_score, pooled_sum = late_scores(late_index, partial, pair_ids, late_table, w_first, b_first, w_second)
     pair_cost = lax.psum_scatter(pooled_sum, "edge", scatter_dimension=0, tiled=True)
     return (edge_score, pair_cost)
 

time: 325 us -> 269 us (0.83)
  the two profiles are of different devices: /device:TPU:10 before, /device:TPU:2 now
where the time goes in v6:
time: 269 us; the launch traced here: 268 us
  waiting for transfers between devices  140 us (52%)
  Pallas kernels  56.8 us (21%)
  blocking collectives  23 us (9%)
  starting transfers between devices  18.7 us (7%)
  local copies, waits for them, and re-layouts  16 us (6%)
  other arithmetic  11.6 us (4%)
    all_to_all x1, waiting for transfers between devices, body(): lax.all_to_all(early_picked, 'node', split_axis=0, concat_axis=0, tiled=T...  140 us
    pallas_call x1, Pallas kernels, early_products(): pl.pallas_call(functools.partial(early_kernel, edges), grid_spec=grid_spe...  37.1 us
    unnamed x1, blocking collectives  23 us
    pallas_call x1, Pallas kernels, late_scores(): pl.pallas_call(late_kernel, grid=(edges // LATE_TILE,), in_specs=[pl.Bloc...  19.7 us
    all_to_all x1, starting transfers between devices, body(): lax.all_to_all(early_picked, 'node', split_axis=0, concat_axis=0, tiled=T...  11.1 us
    all_to_all x1, starting transfers between devices, body(): lax.all_to_all(late_picked, 'node', split_axis=0, concat_axis=0, tiled=True)  7.61 us
  transfers between devices with their start and end apart: 2, of which 1 were waited for; matrix products, arithmetic and copies ran while one was open for 7% of the time, Pallas kernels for 14%

profile of v6, /device:TPU:2, one launch (start us, length us, event | category | flops | bytes accessed | tf_op | source)
XLA Modules:
  0.0 267.9 jit_solution(694608053719036321)
XLA Ops:
  0.6 0.7 fusion.6
  1.3 1.7 reshape.64
  3.0 0.1 pad_slice_fusion
  3.1 0.1 broadcast_in_dim.21
  3.2 0.1 pad_maximum_fusion
  3.2 4.1 %gather_fusion.1 = bf16[64,392,128]{2,1,0:T(8,128)(2,1)} fusion(bf16[9,392,128]{2,1,0:T(8,128)(2,1)S(1)} %pad_maximum_fusion, s32[1024]{0:T(1024)S(1)} %pad_clamp_fusion), kind=kCustom, calls=%fused_computation.1 | custom fusion | bytes 12845312 | tf_op jit(solution)/shard_map/jit(_take)/gather | solution.py:174
  7.3 0.0 slice-start
  7.3 11.1 %all-to-all-start = ((bf16[64,392,128]{2,1,0:T(8,128)(2,1)}), bf16[64,392,128]{2,1,0:T(8,128)(2,1)}, u32[]{:S(2)}, u32[]{:S(2)}) async-start(bf16[64,392,128]{2,1,0:T(8,128)(2,1)} %gather_fusion.1), calls=%async_computation | async-start | bytes 12845056 | tf_op jit(solution)/shard_map/all_to_all | solution.py:176
  18.4 0.0 slice-done
  18.5 2.0 gather_fusion
  20.5 0.0 copy-start
  20.5 140.4 %all-to-all-done = bf16[64,392,128]{2,1,0:T(8,128)(2,1)} async-done(((bf16[64,392,128]{2,1,0:T(8,128)(2,1)}), bf16[64,392,128]{2,1,0:T(8,128)(2,1)}, u32[]{:S(2)}, u32[]{:S(2)}) %all-to-all-start) | async-done | bytes 6422560 | tf_op jit(solution)/shard_map/all_to_all | solution.py:176
  160.9 7.6 %all-to-all-start.1 = ((bf16[64,32,512]{2,1,0:T(8,128)(2,1)}), bf16[64,32,512]{2,1,0:T(8,128)(2,1)}, u32[]{:S(2)}, u32[]{:S(2)}) async-start(bf16[64,32,512]{2,1,0:T(8,128)(2,1)} %gather_fusion), calls=%async_computation.1 | async-start | bytes 4194304 | tf_op jit(solution)/shard_map/all_to_all | solution.py:178
  168.5 0.0 copy-done
  168.5 0.4 copy.75
  168.9 0.5 copy.80
  169.4 2.9 %multiply_add_fusion = (s32[2,2048]{0,1:T(8,128)S(1)}, s32[2,2048]{0,1:T(8,128)S(1)}, s32[2,2048]{0,1:T(8,128)}) fusion(pred[2,2048]{0,1:T(8,128)(4,1)S(1)} %copy.80, s32[2,2048]{0,1:T(8,128)S(1)} %copy.75), kind=kLoop, calls=%fused_computation.17 | loop fusion | flops 180224 | bytes 69632 | tf_op jit(solution)/shard_map/add | solution.py:185
  172.3 0.0 copy-start.1
  172.3 0.3 copy.82
  172.6 1.6 copy.85
  174.2 0.3 copy.88
  174.5 0.6 copy.91
  175.1 0.0 copy-done.1
  175.1 1.4 copy.90.pid_ref
  176.5 1.3 dynamic-slice
  178.4 2.1 convert_reduce_fusion
  180.5 0.4 fusion.3
  180.9 0.5 copy.86
  181.4 1.6 convert_bitcast_fusion.mask_ref
  183.0 37.1 %shard_map.86.part_ref = f32[2048,512]{1,0:T(8,128)} custom-call(s32[4096]{0:T(1024)} %bitcast.16, bf16[25088,128]{1,0:T(8,128)(2,1)} %bitcast.3.table, f32[2048,2]{1,0:T(8,128)} %convert_bitcast_fusion.mask_ref, bf16[1024,512]{1,0:T(8,128)(2,1)} %wb_ref.3, bf16[1024,512]{1,0:T(8,128)(2,1)} %wb_ref.3), custom_call_target="tpu_custom_call" | custom-call | flops 2147483648 | bytes 8388608 | tf_op jit(solution)/shard_map/pallas_call | solution.py:109
  220.1 0.0 copy-start.2
  220.1 1.7 select_bitcast_fusion.idx_ref
  221.9 0.0 all-to-all-done.1
  221.9 0.0 copy-done.2
  221.9 0.6 broadcast_in_dim.22.wo_ref
  222.5 19.7 %shard_map.87 = (f32[2048,1]{1,0:T(8,128)}, f32[1,1024]{1,0:T(1,128)}) custom-call(s32[2048,2]{1,0:T(8,128)} %select_bitcast_fusion.idx_ref, f32[2048,512]{1,0:T(8,128)} %shard_map.86.part_ref, bf16[2048,512]{1,0:T(8,128)(2,1)} %bitcast.5.table_ref, bf16[1024,512]{1,0:T(8,128)(2,1)} %wb_ref.3, bf16[1024,512]{1,0:T(8,128)(2,1)} %wb_ref.3, f32[1,512]{1,0:T(1,128)} %bitcast.20, ...), custom_call_target="tpu_custom_call" | custom-call | flops 10737418240 | bytes 6291456 | tf_op jit(solution)/shard_map/pallas_call | solution.py:125
  242.2 23.0 %all-reduce.2 = f32[1024]{0:T(1024)S(1)} all-reduce(f32[1024]{0:T(1024)} %bitcast.19), channel_id=2, replica_groups=mesh['node'=64,'edge'=8] {'edge'}, use_global_device_ids=true, to_apply=%region_1.2.clone | all-reduce | flops 1024 | bytes 8192
  265.2 0.6 dynamic-slice.1
  265.8 2.2 reduce.1
  (5 shorter events, 0.1 us)
Async XLA Ops:
  7.3 11.1 %slice-start = ((bf16[8,128,512]{2,1,0:T(8,128)(2,1)}), bf16[8,32,512]{2,1,0:T(8,128)(2,1)S(1)}, s32[]{:S(2)}) async-start(bf16[8,128,512]{2,1,0:T(8,128)(2,1)} %param.7), calls=%async_computation.2 | async-start | bytes 524288 | tf_op jit(solution)/shard_map/slice | solution.py:173
  7.3 153.6 %all-to-all-start = ((bf16[64,392,128]{2,1,0:T(8,128)(2,1)}), bf16[64,392,128]{2,1,0:T(8,128)(2,1)}, u32[]{:S(2)}, u32[]{:S(2)}) async-start(bf16[64,392,128]{2,1,0:T(8,128)(2,1)} %gather_fusion.1), calls=%async_computation | async-start | bytes 12845056 | tf_op jit(solution)/shard_map/all_to_all | solution.py:176
  20.5 148.0 %copy-start = (s32[2,2048]{1,0:T(2,128)S(1)}, s32[2,2048]{1,0:T(2,128)}, u32[]{:S(2)}) copy-start(s32[2,2048]{1,0:T(2,128)} %param.9) | copy-start | bytes 49156
  160.9 61.0 %all-to-all-start.1 = ((bf16[64,32,512]{2,1,0:T(8,128)(2,1)}), bf16[64,32,512]{2,1,0:T(8,128)(2,1)}, u32[]{:S(2)}, u32[]{:S(2)}) async-start(bf16[64,32,512]{2,1,0:T(8,128)(2,1)} %gather_fusion), calls=%async_computation.1 | async-start | bytes 4194304 | tf_op jit(solution)/shard_map/all_to_all | solution.py:178
  172.3 2.9 %copy-start.1 = (s32[2048]{0:T(1024)S(1)}, s32[2048]{0:T(1024)}, u32[]{:S(2)}) copy-start(s32[2048]{0:T(1024)} %param.10) | copy-start | bytes 24580
  220.1 1.8 copy-start.2

commit v7 on v6

--- a/solution.py
+++ b/solution.py
@@ -82,6 +82,58 @@
     pair_range = lax.broadcasted_iota(jnp.int32, (LATE_TILE, PAIRS_ROW), 1)
     pooled = jnp.where(pid_ref[...] == pair_range, scores, 0.0)
     pool_ref[...] += jnp.sum(pooled, axis=0, keepdims=True)
+
+
+def exchange_kernel(src_ref, dst_ref, send_sems, recv_sems, own_sem):
+    count = src_ref.shape[0]
+    me = lax.axis_index("node")
+    lane = lax.axis_index("edge")
+    barrier = pltpu.get_barrier_semaphore()
+
+    def greet(k, carry):
+        pl.semaphore_signal(barrier, 1, device_id=((me + k) % count, lane), device_id_type=pl.DeviceIdType.MESH)
+        return carry
+
+    lax.fori_loop(1, count, greet, 0)
+    pl.semaphore_wait(barrier, count - 1)
+    own = pltpu.make_async_copy(src_ref.at[me], dst_ref.at[me], own_sem)
+    own.start()
+
+    def remote(target, slot):
+        return pltpu.make_async_remote_copy(
+            src_ref.at[target], dst_ref.at[slot], send_sems.at[target], recv_sems.at[slot],
+            device_id=(target, lane), device_id_type=pl.DeviceIdType.MESH)
+
+    def send(k, carry):
+        remote((me + k) % count, me).start()
+        return carry
+
+    lax.fori_loop(1, count, send, 0)
+
+    def finish(k, carry):
+        remote((me + k) % count, me).wait_send()
+        source = (me + count - k) % count
+        remote(source, source).wait_recv()
+        return carry
+
+    lax.fori_loop(1, count, finish, 0)
+    own.wait()
+
+
+def exchange(picked):
+    count = picked.shape[0]
+    return pl.pallas_call(
+        exchange_kernel,
+        in_specs=[pl.BlockSpec(memory_space=pl.ANY)],
+        out_specs=pl.BlockSpec(memory_space=pl.ANY),
+        out_shape=jax.ShapeDtypeStruct(picked.shape, picked.dtype),
+        scratch_shapes=[
+            pltpu.SemaphoreType.DMA((count,)),
+            pltpu.SemaphoreType.DMA((count,)),
+            pltpu.SemaphoreType.DMA(()),
+        ],
+        compiler_params=pltpu.CompilerParams(collective_id=0, has_side_effects=True),
+    )(picked)
 
 
 def early_products(position, mask, table, w_first):
@@ -173,7 +225,7 @@
     late_source = jnp.concatenate([embedding[:, EARLY_ROWS:], jnp.zeros((1, late_rows, feature_width), embedding.dtype)], axis=0)
     early_picked = jnp.take(early_source, pick, axis=0, mode="clip")
     late_picked = jnp.take(late_source, pick, axis=0, mode="clip")
-    early_arrived = lax.all_to_all(early_picked, "node", split_axis=0, concat_axis=0, tiled=True)
+    early_arrived = exchange(early_picked)
     late_picked, early_arrived = lax.optimization_barrier((late_picked, early_arrived))
     late_arrived = lax.all_to_all(late_picked, "node", split_axis=0, concat_axis=0, tiled=True)
     early_table = early_arrived.reshape(node_count * slot_len, lanes)

time: 269 us -> 299 us (1.11)
  Pallas kernels: 56.8 us -> 219 us
  waiting for transfers between devices: 140 us -> 0.01 us
  starting transfers between devices: 18.7 us -> 26 us
    pallas_call x0 -> x1, Pallas kernels: none -> 162 us  [exchange(): pl.pallas_call(exchange_kernel, in_specs=[pl.BlockSpec(memory_space=pl.AN...]
    all_to_all x1 -> x0, waiting for transfers between devices: 140 us -> none  [body(): lax.all_to_all(early_picked, 'node', split_axis=0, concat_axis=0, tiled=T...]
    all_to_all x1, starting transfers between devices: 7.61 us -> 26 us  [body(): lax.all_to_all(late_picked, 'node', split_axis=0, concat_axis=0, tiled=True)]
    all_to_all x1 -> x0, starting transfers between devices: 11.1 us -> none  [body(): lax.all_to_all(early_picked, 'node', split_axis=0, concat_axis=0, tiled=T...]
  transfers between devices with their start and end apart: 2 -> 1, of which waited for: 1 -> 0; matrix products, arithmetic and copies ran while one was open for 7% -> 6% of each run, Pallas kernels for 14% -> 12%
where the time goes in v7:
time: 299 us
  Pallas kernels  219 us (73%)
  starting transfers between devices  26 us (9%)
  blocking collectives  24.3 us (8%)
  local copies, waits for them, and re-layouts  16.6 us (6%)
  other arithmetic  11.9 us (4%)
    pallas_call x1, Pallas kernels, exchange(): pl.pallas_call(exchange_kernel, in_specs=[pl.BlockSpec(memory_space=pl.AN...  162 us
    pallas_call x1, Pallas kernels, early_products(): pl.pallas_call(functools.partial(early_kernel, edges), grid_spec=grid_spe...  37.3 us
    all_to_all x1, starting transfers between devices, body(): lax.all_to_all(late_picked, 'node', split_axis=0, concat_axis=0, tiled=True)  26 us
    unnamed x1, blocking collectives  24.3 us
    pallas_call x1, Pallas kernels, late_scores(): pl.pallas_call(late_kernel, grid=(edges // LATE_TILE,), in_specs=[pl.Bloc...  19.7 us
  transfers between devices with their start and end apart: 1, of which 0 were waited for; matrix products, arithmetic and copies ran while one was open for 6% of the time, Pallas kernels for 12%

profile of v7, /device:TPU:2, one launch (start us, length us, event | category | flops | bytes accessed | tf_op | source)
XLA Modules:
  0.0 298.8 jit_solution(1381489889171241292)
XLA Ops:
  0.6 0.0 copy-start.4
  0.7 1.7 reshape.64
  2.4 0.0 copy-done.4
  2.4 0.1 pad_slice_fusion
  2.5 0.1 broadcast_in_dim.21
  2.5 0.1 pad_maximum_fusion
  2.6 4.1 %gather_fusion.1 = bf16[64,392,128]{2,1,0:T(8,128)(2,1)} fusion(bf16[9,392,128]{2,1,0:T(8,128)(2,1)S(1)} %pad_maximum_fusion, s32[1024]{0:T(1024)S(1)} %pad_clamp_fusion), kind=kCustom, calls=%fused_computation.1 | custom fusion | bytes 12845312 | tf_op jit(solution)/shard_map/jit(_take)/gather | solution.py:226
  6.7 0.0 slice-start
  6.7 161.6 %shard_map.86 = bf16[64,392,128]{2,1,0:T(8,128)(2,1)} custom-call(bf16[64,392,128]{2,1,0:T(8,128)(2,1)} %gather_fusion.1), custom_call_target="tpu_custom_call" | custom-call | tf_op jit(solution)/shard_map/pallas_call | solution.py:125
  168.3 0.0 slice-done
  168.4 2.0 gather_fusion
  170.4 0.0 copy-start.1
  170.4 26.0 %all-to-all-start = ((bf16[64,32,512]{2,1,0:T(8,128)(2,1)}), bf16[64,32,512]{2,1,0:T(8,128)(2,1)}, u32[]{:S(2)}, u32[]{:S(2)}) async-start(bf16[64,32,512]{2,1,0:T(8,128)(2,1)} %gather_fusion), calls=%async_computation | async-start | bytes 4194304 | tf_op jit(solution)/shard_map/all_to_all | solution.py:230
  196.4 0.0 copy-done.1
  196.4 0.4 copy.61
  196.8 0.5 copy.66
  197.3 2.9 multiply_add_fusion
  200.1 0.0 copy-start.2
  200.2 0.3 copy.68
  200.5 1.6 copy.71
  202.0 2.1 convert_reduce_fusion
  204.2 0.4 fusion.3
  204.5 1.1 copy.72
  205.6 0.3 copy.74
  206.0 0.6 copy.77
  206.6 0.0 copy-done.2
  206.6 1.4 copy.76.pid_ref
  208.0 1.3 dynamic-slice
  209.9 2.5 convert_bitcast_fusion.mask_ref
  212.4 0.0 copy-start
  212.4 37.3 %shard_map.87.part_ref = f32[2048,512]{1,0:T(8,128)} custom-call(s32[4096]{0:T(1024)} %bitcast.17, bf16[25088,128]{1,0:T(8,128)(2,1)} %bitcast.16, f32[2048,2]{1,0:T(8,128)} %convert_bitcast_fusion.mask_ref, bf16[1024,512]{1,0:T(8,128)(2,1)} %wb_ref.3, bf16[1024,512]{1,0:T(8,128)(2,1)} %wb_ref.3), custom_call_target="tpu_custom_call" | custom-call | flops 2147483648 | bytes 8388608 | tf_op jit(solution)/shard_map/pallas_call | solution.py:161
  249.7 0.0 copy-done
  249.7 0.0 copy-start.3
  249.7 1.7 select_bitcast_fusion.idx_ref
  251.4 0.0 all-to-all-done
  251.4 0.0 copy-done.3
  251.4 0.6 broadcast_in_dim.22.wo_ref
  252.0 19.7 %shard_map.88 = (f32[2048,1]{1,0:T(8,128)}, f32[1,1024]{1,0:T(1,128)}) custom-call(s32[2048,2]{1,0:T(8,128)} %select_bitcast_fusion.idx_ref, f32[2048,512]{1,0:T(8,128)} %shard_map.87.part_ref, bf16[2048,512]{1,0:T(8,128)(2,1)} %bitcast.5.table_ref, bf16[1024,512]{1,0:T(8,128)(2,1)} %wb_ref.3, bf16[1024,512]{1,0:T(8,128)(2,1)} %wb_ref.3, f32[1,512]{1,0:T(1,128)} %bitcast.21, ...), custom_call_target="tpu_custom_call" | custom-call | flops 10737418240 | bytes 6291456 | tf_op jit(solution)/shard_map/pallas_call | solution.py:177
  271.7 24.3 %all-reduce.2 = f32[1024]{0:T(1024)S(1)} all-reduce(f32[1024]{0:T(1024)} %bitcast.20), channel_id=2, replica_groups=mesh['node'=64,'edge'=8] {'edge'}, use_global_device_ids=true, to_apply=%region_1.2.clone | all-reduce | flops 1024 | bytes 8192
  296.1 0.6 dynamic-slice.1
  296.7 2.2 reduce.1
  (6 shorter events, 0.1 us)
Async XLA Ops:
  0.6 1.7 copy-start.4
  6.7 161.6 %slice-start = ((bf16[8,128,512]{2,1,0:T(8,128)(2,1)}), bf16[8,32,512]{2,1,0:T(8,128)(2,1)S(1)}, s32[]{:S(2)}) async-start(bf16[8,128,512]{2,1,0:T(8,128)(2,1)} %param.7), calls=%async_computation.1 | async-start | bytes 524288 | tf_op jit(solution)/shard_map/slice | solution.py:225
  170.4 26.0 %copy-start.1 = (s32[2,2048]{1,0:T(2,128)S(1)}, s32[2,2048]{1,0:T(2,128)}, u32[]{:S(2)}) copy-start(s32[2,2048]{1,0:T(2,128)} %param.9) | copy-start | bytes 49156
  170.4 81.1 %all-to-all-start = ((bf16[64,32,512]{2,1,0:T(8,128)(2,1)}), bf16[64,32,512]{2,1,0:T(8,128)(2,1)}, u32[]{:S(2)}, u32[]{:S(2)}) async-start(bf16[64,32,512]{2,1,0:T(8,128)(2,1)} %gather_fusion), calls=%async_computation | async-start | bytes 4194304 | tf_op jit(solution)/shard_map/all_to_all | solution.py:230
  200.1 6.4 %copy-start.2 = (s32[2048]{0:T(1024)S(1)}, s32[2048]{0:T(1024)}, u32[]{:S(2)}) copy-start(s32[2048]{0:T(1024)} %param.10) | copy-start | bytes 24580
  212.4 37.3 %copy-start = (pred[2,2048]{0,1:T(8,128)(4,1)S(1)}, pred[2,2048]{0,1:T(8,128)(4,1)}, u32[]{:S(2)}) copy-start(pred[2,2048]{0,1:T(8,128)(4,1)} %copy.72) | copy-start | bytes 12292
  249.7 1.8 copy-start.3

commit v8 on v6

--- a/solution.py
+++ b/solution.py
@@ -10,7 +10,7 @@
 PAIRS_ROW = 1024
 TILE = 256
 LATE_TILE = 256
-EARLY_ROWS = 96
+EARLY_ROWS = 88
 
 
 def gelu_tanh(x):
@@ -149,6 +149,58 @@
             bytes_accessed=rows * width * 2 + edges * hid * 4),
     )(late_index.T, partial, table, w_first, w_first, b_first.reshape(1, hid), wo8, pair_ids.reshape(edges, 1))
     return scores.reshape(edges), pooled.reshape(PAIRS_ROW)
+
+
+def scatter_kernel(part_ref, out_ref, recv, send_sems, recv_sems):
+    count = part_ref.shape[0]
+    me = lax.axis_index("edge")
+    node = lax.axis_index("node")
+    barrier = pltpu.get_barrier_semaphore()
+
+    def greet(k, carry):
+        pl.semaphore_signal(barrier, 1, device_id=(node, (me + k) % count), device_id_type=pl.DeviceIdType.MESH)
+        return carry
+
+    lax.fori_loop(1, count, greet, 0)
+    pl.semaphore_wait(barrier, count - 1)
+
+    def remote(target, slot):
+        return pltpu.make_async_remote_copy(
+            part_ref.at[pl.ds(target, 1)], recv.at[pl.ds(slot, 1)], send_sems.at[target], recv_sems.at[slot],
+            device_id=(node, target), device_id_type=pl.DeviceIdType.MESH)
+
+    def send(k, carry):
+        remote((me + k) % count, me).start()
+        return carry
+
+    lax.fori_loop(1, count, send, 0)
+
+    def finish(k, carry):
+        remote((me + k) % count, me).wait_send()
+        source = (me + count - k) % count
+        remote(source, source).wait_recv()
+        return carry
+
+    lax.fori_loop(1, count, finish, 0)
+    rows = lax.broadcasted_iota(jnp.int32, part_ref.shape, 0)
+    out_ref[...] = jnp.sum(jnp.where(rows == me, part_ref[...], recv[...]), axis=0, keepdims=True)
+
+
+def reduce_scatter(pooled, count):
+    width = pooled.shape[0] // count
+    out = pl.pallas_call(
+        scatter_kernel,
+        in_specs=[pl.BlockSpec(memory_space=pltpu.VMEM)],
+        out_specs=pl.BlockSpec(memory_space=pltpu.VMEM),
+        out_shape=jax.ShapeDtypeStruct((1, width), pooled.dtype),
+        scratch_shapes=[
+            pltpu.VMEM((count, width), pooled.dtype),
+            pltpu.SemaphoreType.DMA((count,)),
+            pltpu.SemaphoreType.DMA((count,)),
+        ],
+        compiler_params=pltpu.CompilerParams(collective_id=0, has_side_effects=True),
+    )(pooled.reshape(count, width))
+    return out.reshape(width)
 
 
 def body(embedding, send_list, edge_ends, pair_index, w_first, b_first, w_second):
@@ -191,7 +243,7 @@
     partial = early_products(early_position, early_mask, early_table, w_first)
     pair_ids = pair_index - node_self * PAIRS_ROW
     edge_score, pooled_sum = late_scores(late_index, partial, pair_ids, late_table, w_first, b_first, w_second)
-    pair_cost = lax.psum_scatter(pooled_sum, "edge", scatter_dimension=0, tiled=True)
+    pair_cost = reduce_scatter(pooled_sum, lax.axis_size("edge"))
     return (edge_score, pair_cost)
 
 

time: 269 us -> 262 us (0.974)
  blocking collectives: 23 us -> 0 us
  Pallas kernels: 56.8 us -> 74.9 us
    unnamed x1 -> x0, blocking collectives: 23 us -> none
    pallas_call x0 -> x1, Pallas kernels: none -> 15.7 us  [reduce_scatter(): pl.pallas_call(scatter_kernel, in_specs=[pl.BlockSpec(memory_space=pltpu....]
    all_to_all x1, waiting for transfers between devices: 0.01 us -> 10.9 us  [body(): lax.all_to_all(late_picked, 'node', split_axis=0, concat_axis=0, tiled=True)]
    all_to_all x1, waiting for transfers between devices: 140 us -> 131 us  [body(): lax.all_to_all(early_picked, 'node', split_axis=0, concat_axis=0, tiled=T...]
  transfers between devices with their start and end apart: 2 -> 2, of which waited for: 1 -> 2; matrix products, arithmetic and copies ran while one was open for 7% -> 6% of each run, Pallas kernels for 14% -> 14%
where the time goes in v8:
time: 262 us; the launch traced here: 261 us
  waiting for transfers between devices  142 us (54%)
  Pallas kernels  74.9 us (29%)
  starting transfers between devices  16.9 us (6%)
  local copies, waits for them, and re-layouts  15.3 us (6%)
  other arithmetic  11.6 us (4%)
    all_to_all x1, waiting for transfers between devices, body(): lax.all_to_all(early_picked, 'node', split_axis=0, concat_axis=0, tiled=T...  131 us
    pallas_call x1, Pallas kernels, early_products(): pl.pallas_call(functools.partial(early_kernel, edges), grid_spec=grid_spe...  37.2 us
    pallas_call x1, Pallas kernels, late_scores(): pl.pallas_call(late_kernel, grid=(edges // LATE_TILE,), in_specs=[pl.Bloc...  22 us
    pallas_call x1, Pallas kernels, reduce_scatter(): pl.pallas_call(scatter_kernel, in_specs=[pl.BlockSpec(memory_space=pltpu....  15.7 us
    all_to_all x1, starting transfers between devices, body(): lax.all_to_all(early_picked, 'node', split_axis=0, concat_axis=0, tiled=T...  11.1 us
    all_to_all x1, waiting for transfers between devices, body(): lax.all_to_all(late_picked, 'node', split_axis=0, concat_axis=0, tiled=True)  10.9 us
    all_to_all x1, starting transfers between devices, body(): lax.all_to_all(late_picked, 'node', split_axis=0, concat_axis=0, tiled=True)  5.76 us
  transfers between devices with their start and end apart: 2, of which 2 were waited for; matrix products, arithmetic and copies ran while one was open for 6% of the time, Pallas kernels for 14%

profile of v8, /device:TPU:2, one launch (start us, length us, event | category | flops | bytes accessed | tf_op | source)
XLA Modules:
  0.0 261.0 jit_solution(5275638831334128455)
XLA Ops:
  0.6 0.7 fusion.6
  1.3 1.7 reshape.64
  3.0 0.1 pad_slice_fusion
  3.1 0.1 broadcast_in_dim.21
  3.2 0.1 pad_maximum_fusion
  3.2 3.9 %gather_fusion.1 = bf16[64,360,128]{2,1,0:T(8,128)(2,1)} fusion(bf16[9,360,128]{2,1,0:T(8,128)(2,1)S(1)} %pad_maximum_fusion, s32[1024]{0:T(1024)S(1)} %pad_clamp_fusion), kind=kCustom, calls=%fused_computation.1 | custom fusion | bytes 11796736 | tf_op jit(solution)/shard_map/jit(_take)/gather | solution.py:226
  7.1 0.0 slice-start
  7.1 11.1 %all-to-all-start = ((bf16[64,360,128]{2,1,0:T(8,128)(2,1)}), bf16[64,360,128]{2,1,0:T(8,128)(2,1)}, u32[]{:S(2)}, u32[]{:S(2)}) async-start(bf16[64,360,128]{2,1,0:T(8,128)(2,1)} %gather_fusion.1), calls=%async_computation | async-start | bytes 11796480 | tf_op jit(solution)/shard_map/all_to_all | solution.py:228
  18.2 0.0 slice-done
  18.3 2.2 gather_fusion
  20.5 0.0 copy-start
  20.5 130.6 %all-to-all-done = bf16[64,360,128]{2,1,0:T(8,128)(2,1)} async-done(((bf16[64,360,128]{2,1,0:T(8,128)(2,1)}), bf16[64,360,128]{2,1,0:T(8,128)(2,1)}, u32[]{:S(2)}, u32[]{:S(2)}) %all-to-all-start) | async-done | bytes 5898272 | tf_op jit(solution)/shard_map/all_to_all | solution.py:228
  151.1 5.8 %all-to-all-start.1 = ((bf16[64,40,512]{2,1,0:T(8,128)(2,1)}), bf16[64,40,512]{2,1,0:T(8,128)(2,1)}, u32[]{:S(2)}, u32[]{:S(2)}) async-start(bf16[64,40,512]{2,1,0:T(8,128)(2,1)} %gather_fusion), calls=%async_computation.1 | async-start | bytes 5242880 | tf_op jit(solution)/shard_map/all_to_all | solution.py:230
  156.9 0.0 copy-done
  156.9 0.4 copy.62
  157.3 0.5 copy.67
  157.7 2.9 %multiply_add_fusion = (s32[2,2048]{0,1:T(8,128)S(1)}, s32[2,2048]{0,1:T(8,128)S(1)}, s32[2,2048]{0,1:T(8,128)}) fusion(pred[2,2048]{0,1:T(8,128)(4,1)S(1)} %copy.67, s32[2,2048]{0,1:T(8,128)S(1)} %copy.62), kind=kLoop, calls=%fused_computation.17 | loop fusion | flops 180224 | bytes 69632 | tf_op jit(solution)/shard_map/add | solution.py:237
  160.6 0.0 copy-start.1
  160.6 0.3 copy.69
  161.0 1.6 copy.72
  162.5 0.3 copy.75
  162.9 0.6 copy.78
  163.5 0.0 copy-done.1
  163.5 1.4 copy.77.pid_ref
  164.9 2.1 convert_reduce_fusion
  167.0 0.4 fusion.3
  167.4 0.5 copy.73
  167.9 1.6 convert_bitcast_fusion.mask_ref
  169.4 37.2 %shard_map.86.part_ref = f32[2048,512]{1,0:T(8,128)} custom-call(s32[4096]{0:T(1024)} %bitcast.16, bf16[23040,128]{1,0:T(8,128)(2,1)} %bitcast.3.table, f32[2048,2]{1,0:T(8,128)} %convert_bitcast_fusion.mask_ref, bf16[1024,512]{1,0:T(8,128)(2,1)} %wb_ref.3, bf16[1024,512]{1,0:T(8,128)(2,1)} %wb_ref.3), custom_call_target="tpu_custom_call" | custom-call | flops 2147483648 | bytes 8388608 | tf_op jit(solution)/shard_map/pallas_call | solution.py:109
  206.6 0.0 copy-start.2
  206.6 1.7 select_bitcast_fusion.idx_ref
  208.3 10.9 %all-to-all-done.1 = bf16[64,40,512]{2,1,0:T(8,128)(2,1)} async-done(((bf16[64,40,512]{2,1,0:T(8,128)(2,1)}), bf16[64,40,512]{2,1,0:T(8,128)(2,1)}, u32[]{:S(2)}, u32[]{:S(2)}) %all-to-all-start.1) | async-done | bytes 2621472 | tf_op jit(solution)/shard_map/all_to_all | solution.py:230
  219.3 0.0 copy-done.2
  219.3 0.6 broadcast_in_dim.22.wo_ref
  219.9 22.0 %shard_map.87 = (f32[2048,1]{1,0:T(8,128)}, f32[1,1024]{1,0:T(1,128)}) custom-call(s32[2048,2]{1,0:T(8,128)} %select_bitcast_fusion.idx_ref, f32[2048,512]{1,0:T(8,128)} %shard_map.86.part_ref, bf16[2560,512]{1,0:T(8,128)(2,1)} %bitcast.5.table_ref, bf16[1024,512]{1,0:T(8,128)(2,1)} %wb_ref.3, bf16[1024,512]{1,0:T(8,128)(2,1)} %wb_ref.3, f32[1,512]{1,0:T(1,128)} %bitcast.21, ...), custom_call_target="tpu_custom_call" | custom-call | flops 12884901888 | bytes 6815744 | tf_op jit(solution)/shard_map/pallas_call | solution.py:125
  241.9 15.7 %shard_map.88 = f32[1,128]{1,0:T(1,128)} custom-call(f32[8,128]{1,0:T(8,128)} %bitcast.19), custom_call_target="tpu_custom_call" | custom-call | tf_op jit(solution)/shard_map/pallas_call | solution.py:191
  257.6 2.2 reduce.1
  259.8 1.2 copy.80
  (5 shorter events, 0.1 us)
Async XLA Ops:
  7.1 11.1 %slice-start = ((bf16[8,128,512]{2,1,0:T(8,128)(2,1)}), bf16[8,40,512]{2,1,0:T(8,128)(2,1)S(1)}, s32[]{:S(2)}) async-start(bf16[8,128,512]{2,1,0:T(8,128)(2,1)} %param.7), calls=%async_computation.2 | async-start | bytes 655360 | tf_op jit(solution)/shard_map/slice | solution.py:225
  7.1 144.0 %all-to-all-start = ((bf16[64,360,128]{2,1,0:T(8,128)(2,1)}), bf16[64,360,128]{2,1,0:T(8,128)(2,1)}, u32[]{:S(2)}, u32[]{:S(2)}) async-start(bf16[64,360,128]{2,1,0:T(8,128)(2,1)} %gather_fusion.1), calls=%async_computation | async-start | bytes 11796480 | tf_op jit(solution)/shard_map/all_to_all | solution.py:228
  20.5 136.4 %copy-start = (s32[2,2048]{1,0:T(2,128)S(1)}, s32[2,2048]{1,0:T(2,128)}, u32[]{:S(2)}) copy-start(s32[2,2048]{1,0:T(2,128)} %param.9) | copy-start | bytes 49156
  151.1 68.2 %all-to-all-start.1 = ((bf16[64,40,512]{2,1,0:T(8,128)(2,1)}), bf16[64,40,512]{2,1,0:T(8,128)(2,1)}, u32[]{:S(2)}, u32[]{:S(2)}) async-start(bf16[64,40,512]{2,1,0:T(8,128)(2,1)} %gather_fusion), calls=%async_computation.1 | async-start | bytes 5242880 | tf_op jit(solution)/shard_map/all_to_all | solution.py:230
  160.6 2.9 %copy-start.1 = (s32[2048]{0:T(1024)S(1)}, s32[2048]{0:T(1024)}, u32[]{:S(2)}) copy-start(s32[2048]{0:T(1024)} %param.10) | copy-start | bytes 24580
  206.6 12.7 %copy-start.2 = (bf16[512]{0:T(512)(128)(2,1)S(1)}, bf16[512]{0:T(512)(128)(2,1)}, u32[]{:S(2)}) copy-start(bf16[512]{0:T(512)(128)(2,1)} %param.13) | copy-start | bytes 3076

commit v9 on v8

--- a/solution.py
+++ b/solution.py
@@ -10,7 +10,7 @@
 PAIRS_ROW = 1024
 TILE = 256
 LATE_TILE = 256
-EARLY_ROWS = 88
+EARLY_ROWS = 96
 
 
 def gelu_tanh(x):
@@ -212,6 +212,7 @@
     lanes = 128
     parts = feature_width // lanes
     early_len = EARLY_ROWS * parts
+    late_rows = block_rows - EARLY_ROWS
     slot_len = early_len + 8
     wanted = send_list[0, 0]
     pick = jnp.where(wanted >= 0, wanted, blocks_here)
@@ -221,27 +222,29 @@
     marks = jnp.where(marks < blocks_here, marks, -1).astype(embedding.dtype)
     marks = jnp.broadcast_to(marks[:, None, None], (blocks_here + 1, 8, lanes))
     early_source = jnp.concatenate([narrow[:, :early_len], marks], axis=1)
-    late_rows = block_rows - EARLY_ROWS
     late_source = jnp.concatenate([embedding[:, EARLY_ROWS:], jnp.zeros((1, late_rows, feature_width), embedding.dtype)], axis=0)
     early_picked = jnp.take(early_source, pick, axis=0, mode="clip")
     late_picked = jnp.take(late_source, pick, axis=0, mode="clip")
     early_arrived = lax.all_to_all(early_picked, "node", split_axis=0, concat_axis=0, tiled=True)
-    late_picked, early_arrived = lax.optimization_barrier((late_picked, early_arrived))
-    late_arrived = lax.all_to_all(late_picked, "node", split_axis=0, concat_axis=0, tiled=True)
-    early_table = early_arrived.reshape(node_count * slot_len, lanes)
-    late_table = late_arrived.reshape(node_count * late_rows, feature_width)
     source = edge_ends // (blocks_here * block_rows)
     block_of = (edge_ends // block_rows) % blocks_here
     within = edge_ends % block_rows
     early = within < EARLY_ROWS
     early_position = source * slot_len + jnp.where(early, within, 0) * parts
+    late_rows = block_rows - EARLY_ROWS
+    late_spot = source * late_rows + within - EARLY_ROWS
+    pair_ids = (pair_index - node_self * PAIRS_ROW).reshape(-1, 1)
+    late_picked, early_arrived, early_position, late_spot, pair_ids = lax.optimization_barrier(
+        (late_picked, early_arrived, early_position, late_spot, pair_ids))
+    late_arrived = lax.all_to_all(late_picked, "node", split_axis=0, concat_axis=0, tiled=True)
+    early_table = early_arrived.reshape(node_count * slot_len, lanes)
+    late_table = late_arrived.reshape(node_count * late_rows, feature_width)
     sent = early_arrived[:, early_len, 0].astype(jnp.int32)
     located = jnp.any((source[..., None] == jnp.arange(node_count, dtype=jnp.int32))
                       & (block_of[..., None] == sent), axis=-1)
     early_mask = (located & early).T.astype(jnp.float32)
-    late_index = jnp.where(located & ~early, source * late_rows + within - EARLY_ROWS, -1)
+    late_index = jnp.where(located & ~early, late_spot, -1)
     partial = early_products(early_position, early_mask, early_table, w_first)
-    pair_ids = pair_index - node_self * PAIRS_ROW
     edge_score, pooled_sum = late_scores(late_index, partial, pair_ids, late_table, w_first, b_first, w_second)
     pair_cost = reduce_scatter(pooled_sum, lax.axis_size("edge"))
     return (edge_score, pair_cost)

time: 262 us -> 259 us (0.989)
  waiting for transfers between devices: 142 us -> 137 us
    all_to_all x1, waiting for transfers between devices: 10.9 us -> 1.81 us  [body(): lax.all_to_all(late_picked, 'node', split_axis=0, concat_axis=0, tiled=True)]
    all_to_all x1, waiting for transfers between devices: 131 us -> 135 us  [body(): lax.all_to_all(early_picked, 'node', split_axis=0, concat_axis=0, tiled=T...]
    sub x1 -> x2, other arithmetic: 0.01 us -> 2.81 us  [the longest x1 2.8 us: body(): late_spot = source * late_rows + within - EARLY_ROWS]
  transfers between devices with their start and end apart: 2 -> 2, of which waited for: 2 -> 2; matrix products, arithmetic and copies ran while one was open for 6% -> 7% of each run, Pallas kernels for 14% -> 14%
where the time goes in v9:
time: 259 us
  waiting for transfers between devices  137 us (53%)
  Pallas kernels  72.6 us (28%)
  starting transfers between devices  18.7 us (7%)
  local copies, waits for them, and re-layouts  15.9 us (6%)
  other arithmetic  13.9 us (5%)
    all_to_all x1, waiting for transfers between devices, body(): lax.all_to_all(early_picked, 'node', split_axis=0, concat_axis=0, tiled=T...  135 us
    pallas_call x1, Pallas kernels, early_products(): pl.pallas_call(functools.partial(early_kernel, edges), grid_spec=grid_spe...  37.3 us
    pallas_call x1, Pallas kernels, late_scores(): pl.pallas_call(late_kernel, grid=(edges // LATE_TILE,), in_specs=[pl.Bloc...  19.7 us
    pallas_call x1, Pallas kernels, reduce_scatter(): pl.pallas_call(scatter_kernel, in_specs=[pl.BlockSpec(memory_space=pltpu....  15.6 us
    all_to_all x1, starting transfers between devices, body(): lax.all_to_all(early_picked, 'node', split_axis=0, concat_axis=0, tiled=T...  11.1 us
    all_to_all x1, starting transfers between devices, body(): lax.all_to_all(late_picked, 'node', split_axis=0, concat_axis=0, tiled=True)  7.61 us
  transfers between devices with their start and end apart: 2, of which 2 were waited for; matrix products, arithmetic and copies ran while one was open for 7% of the time, Pallas kernels for 14%

profile of v9, /device:TPU:2, one launch (start us, length us, event | category | flops | bytes accessed | tf_op | source)
XLA Modules:
  0.0 258.8 jit_solution(716735769527405678)
XLA Ops:
  0.6 0.7 fusion.6
  1.3 1.7 reshape.64
  3.0 0.1 pad_slice_fusion
  3.1 0.1 broadcast_in_dim.21
  3.2 0.1 pad_maximum_fusion
  3.2 4.0 %gather_fusion.1 = bf16[64,392,128]{2,1,0:T(8,128)(2,1)} fusion(bf16[9,392,128]{2,1,0:T(8,128)(2,1)S(1)} %pad_maximum_fusion, s32[1024]{0:T(1024)S(1)} %pad_clamp_fusion), kind=kCustom, calls=%fused_computation.1 | custom fusion | bytes 12845312 | tf_op jit(solution)/shard_map/jit(_take)/gather | solution.py:226
  7.3 0.0 slice-start
  7.3 11.1 %all-to-all-start = ((bf16[64,392,128]{2,1,0:T(8,128)(2,1)}), bf16[64,392,128]{2,1,0:T(8,128)(2,1)}, u32[]{:S(2)}, u32[]{:S(2)}) async-start(bf16[64,392,128]{2,1,0:T(8,128)(2,1)} %gather_fusion.1), calls=%async_computation | async-start | bytes 12845056 | tf_op jit(solution)/shard_map/all_to_all | solution.py:228
  18.4 0.0 slice-done
  18.5 0.0 copy-start.2
  18.5 0.0 copy-start.3
  18.5 2.0 gather_fusion
  20.5 0.0 copy-done.2
  20.5 0.4 copy.47
  20.9 0.5 copy.52
  21.4 0.0 copy-done.3
  21.4 2.8 %add_add_fusion = (s32[2,2048]{0,1:T(8,128)S(1)}, s32[2,2048]{0,1:T(8,128)S(1)}, s32[2,2048]{0,1:T(8,128)}) fusion(pred[2,2048]{0,1:T(8,128)(4,1)S(1)} %copy.52, s32[2,2048]{0,1:T(8,128)S(1)} %copy.47), kind=kLoop, calls=%fused_computation.18 | loop fusion | flops 172032 | bytes 69632 | tf_op jit(solution)/shard_map/sub | solution.py:235
  24.2 1.6 multiply_add_fusion
  25.8 135.1 %all-to-all-done = bf16[64,392,128]{2,1,0:T(8,128)(2,1)} async-done(((bf16[64,392,128]{2,1,0:T(8,128)(2,1)}), bf16[64,392,128]{2,1,0:T(8,128)(2,1)}, u32[]{:S(2)}, u32[]{:S(2)}) %all-to-all-start) | async-done | bytes 6422560 | tf_op jit(solution)/shard_map/all_to_all | solution.py:228
  160.8 7.6 %all-to-all-start.1 = ((bf16[64,32,512]{2,1,0:T(8,128)(2,1)}), bf16[64,32,512]{2,1,0:T(8,128)(2,1)}, u32[]{:S(2)}, u32[]{:S(2)}) async-start(bf16[64,32,512]{2,1,0:T(8,128)(2,1)} %gather_fusion), calls=%async_computation.1 | async-start | bytes 4194304 | tf_op jit(solution)/shard_map/all_to_all | solution.py:239
  168.5 0.3 copy.54
  168.8 0.0 copy-start
  168.8 1.7 copy.57
  170.4 2.1 convert_reduce_fusion
  172.6 0.4 fusion.3
  172.9 1.1 copy.58
  174.0 0.0 copy-done
  174.0 0.3 copy.59
  174.4 0.6 copy.62
  175.0 1.4 copy.61.pid_ref
  176.4 2.5 convert_bitcast_fusion.mask_ref
  178.9 0.0 copy-start.1
  178.9 37.3 %shard_map.86.part_ref = f32[2048,512]{1,0:T(8,128)} custom-call(s32[4096]{0:T(1024)} %bitcast.16, bf16[25088,128]{1,0:T(8,128)(2,1)} %bitcast.4.table, f32[2048,2]{1,0:T(8,128)} %convert_bitcast_fusion.mask_ref, bf16[1024,512]{1,0:T(8,128)(2,1)} %wb_ref.3, bf16[1024,512]{1,0:T(8,128)(2,1)} %wb_ref.3), custom_call_target="tpu_custom_call" | custom-call | flops 2147483648 | bytes 8388608 | tf_op jit(solution)/shard_map/pallas_call | solution.py:109
  216.2 0.0 copy-done.1
  216.2 0.0 copy-start.4
  216.2 1.6 select_bitcast_fusion.idx_ref
  217.8 1.8 all-to-all-done.1
  219.6 0.0 copy-done.4
  219.6 0.6 broadcast_in_dim.22.wo_ref
  220.2 19.7 %shard_map.87 = (f32[2048,1]{1,0:T(8,128)}, f32[1,1024]{1,0:T(1,128)}) custom-call(s32[2048,2]{1,0:T(8,128)} %select_bitcast_fusion.idx_ref, f32[2048,512]{1,0:T(8,128)} %shard_map.86.part_ref, bf16[2048,512]{1,0:T(8,128)(2,1)} %bitcast.6.table_ref, bf16[1024,512]{1,0:T(8,128)(2,1)} %wb_ref.3, bf16[1024,512]{1,0:T(8,128)(2,1)} %wb_ref.3, f32[1,512]{1,0:T(1,128)} %bitcast.21, ...), custom_call_target="tpu_custom_call" | custom-call | flops 10737418240 | bytes 6291456 | tf_op jit(solution)/shard_map/pallas_call | solution.py:125
  239.9 15.6 %shard_map.88 = f32[1,128]{1,0:T(1,128)} custom-call(f32[8,128]{1,0:T(8,128)} %bitcast.19), custom_call_target="tpu_custom_call" | custom-call | tf_op jit(solution)/shard_map/pallas_call | solution.py:191
  255.5 2.2 reduce.1
  257.7 1.1 copy.64
  (5 shorter events, 0.1 us)
Async XLA Ops:
  7.3 11.1 %slice-start = ((bf16[8,128,512]{2,1,0:T(8,128)(2,1)}), bf16[8,32,512]{2,1,0:T(8,128)(2,1)S(1)}, s32[]{:S(2)}) async-start(bf16[8,128,512]{2,1,0:T(8,128)(2,1)} %param.7), calls=%async_computation.2 | async-start | bytes 524288 | tf_op jit(solution)/shard_map/slice | solution.py:225
  7.3 153.6 %all-to-all-start = ((bf16[64,392,128]{2,1,0:T(8,128)(2,1)}), bf16[64,392,128]{2,1,0:T(8,128)(2,1)}, u32[]{:S(2)}, u32[]{:S(2)}) async-start(bf16[64,392,128]{2,1,0:T(8,128)(2,1)} %gather_fusion.1), calls=%async_computation | async-start | bytes 12845056 | tf_op jit(solution)/shard_map/all_to_all | solution.py:228
  18.5 2.1 copy-start.2
  18.5 2.9 %copy-start.3 = (s32[2048]{0:T(1024)S(1)}, s32[2048]{0:T(1024)}, u32[]{:S(2)}) copy-start(s32[2048]{0:T(1024)} %param.10) | copy-start | bytes 24580
  160.8 58.8 %all-to-all-start.1 = ((bf16[64,32,512]{2,1,0:T(8,128)(2,1)}), bf16[64,32,512]{2,1,0:T(8,128)(2,1)}, u32[]{:S(2)}, u32[]{:S(2)}) async-start(bf16[64,32,512]{2,1,0:T(8,128)(2,1)} %gather_fusion), calls=%async_computation.1 | async-start | bytes 4194304 | tf_op jit(solution)/shard_map/all_to_all | solution.py:239
  168.8 5.2 %copy-start = (s32[2,2048]{0,1:T(8,128)S(1)}, s32[2,2048]{0,1:T(8,128)}, u32[]{:S(2)}) copy-start(s32[2,2048]{0,1:T(8,128)} %multiply_add_fusion) | copy-start | bytes 49156
  178.9 37.3 %copy-start.1 = (pred[2,2048]{0,1:T(8,128)(4,1)S(1)}, pred[2,2048]{0,1:T(8,128)(4,1)}, u32[]{:S(2)}) copy-start(pred[2,2048]{0,1:T(8,128)(4,1)} %copy.58) | copy-start | bytes 12292
  216.2 3.4 %copy-start.4 = (bf16[512]{0:T(512)(128)(2,1)S(1)}, bf16[512]{0:T(512)(128)(2,1)}, u32[]{:S(2)}) copy-start(bf16[512]{0:T(512)(128)(2,1)} %param.13) | copy-start | bytes 3076

commit v10 on v9

--- a/solution.py
+++ b/solution.py
@@ -78,7 +78,7 @@
         preact = preact + jnp.dot(picked, w_ref[...], preferred_element_type=jnp.float32)
     hidden = gelu_tanh(preact + bias_ref[...])
     scores = jnp.sum(hidden * wo_ref[0:1, :], axis=1, keepdims=True)
-    score_ref[...] = scores
+    score_ref[...] = jnp.broadcast_to(scores, (LATE_TILE, 128)).T[0:1, :]
     pair_range = lax.broadcasted_iota(jnp.int32, (LATE_TILE, PAIRS_ROW), 1)
     pooled = jnp.where(pid_ref[...] == pair_range, scores, 0.0)
     pool_ref[...] += jnp.sum(pooled, axis=0, keepdims=True)
@@ -136,11 +136,11 @@
             pl.BlockSpec((LATE_TILE, 1), lambda i: (i, 0)),
         ],
         out_specs=[
-            pl.BlockSpec((LATE_TILE, 1), lambda i: (i, 0)),
+            pl.BlockSpec((1, LATE_TILE), lambda i: (0, i)),
             pl.BlockSpec((1, PAIRS_ROW), lambda i: (0, 0)),
         ],
         out_shape=[
-            jax.ShapeDtypeStruct((edges, 1), jnp.float32),
+            jax.ShapeDtypeStruct((1, edges), jnp.float32),
             jax.ShapeDtypeStruct((1, PAIRS_ROW), jnp.float32),
         ],
         compiler_params=pltpu.CompilerParams(dimension_semantics=("arbitrary",)),
@@ -183,7 +183,7 @@
 
     lax.fori_loop(1, count, finish, 0)
     rows = lax.broadcasted_iota(jnp.int32, part_ref.shape, 0)
-    out_ref[...] = jnp.sum(jnp.where(rows == me, part_ref[...], recv[...]), axis=0, keepdims=True)
+    out_ref[...] = jnp.sum(jnp.where(rows == me, part_ref[...], recv[...]), axis=0)
 
 
 def reduce_scatter(pooled, count):
@@ -192,7 +192,7 @@
         scatter_kernel,
         in_specs=[pl.BlockSpec(memory_space=pltpu.VMEM)],
         out_specs=pl.BlockSpec(memory_space=pltpu.VMEM),
-        out_shape=jax.ShapeDtypeStruct((1, width), pooled.dtype),
+        out_shape=jax.ShapeDtypeStruct((width,), pooled.dtype),
         scratch_shapes=[
             pltpu.VMEM((count, width), pooled.dtype),
             pltpu.SemaphoreType.DMA((count,)),
@@ -200,7 +200,7 @@
         ],
         compiler_params=pltpu.CompilerParams(collective_id=0, has_side_effects=True),
     )(pooled.reshape(count, width))
-    return out.reshape(width)
+    return out
 
 
 def body(embedding, send_list, edge_ends, pair_index, w_first, b_first, w_second):

time: 259 us -> 258 us (level)
  transfers between devices with their start and end apart: 2 -> 2, of which waited for: 2 -> 2; matrix products, arithmetic and copies ran while one was open for 7% -> 7% of each run, Pallas kernels for 14% -> 15%
where the time goes in v10:
time: 258 us; the launch traced here: 257 us
  waiting for transfers between devices  137 us (53%)
  Pallas kernels  73.2 us (28%)
  starting transfers between devices  18.7 us (7%)
  local copies, waits for them, and re-layouts  15.9 us (6%)
  other arithmetic  11.7 us (5%)
    all_to_all x1, waiting for transfers between devices, body(): lax.all_to_all(early_picked, 'node', split_axis=0, concat_axis=0, tiled=T...  135 us
    pallas_call x1, Pallas kernels, early_products(): pl.pallas_call(functools.partial(early_kernel, edges), grid_spec=grid_spe...  37.3 us
    pallas_call x1, Pallas kernels, late_scores(): pl.pallas_call(late_kernel, grid=(edges // LATE_TILE,), in_specs=[pl.Bloc...  20.3 us
    pallas_call x1, Pallas kernels, reduce_scatter(): pl.pallas_call(scatter_kernel, in_specs=[pl.BlockSpec(memory_space=pltpu....  15.6 us
    all_to_all x1, starting transfers between devices, body(): lax.all_to_all(early_picked, 'node', split_axis=0, concat_axis=0, tiled=T...  11.1 us
    all_to_all x1, starting transfers between devices, body(): lax.all_to_all(late_picked, 'node', split_axis=0, concat_axis=0, tiled=True)  7.61 us
  transfers between devices with their start and end apart: 2, of which 2 were waited for; matrix products, arithmetic and copies ran while one was open for 7% of the time, Pallas kernels for 15%

profile of v10, /device:TPU:2, one launch (start us, length us, event | category | flops | bytes accessed | tf_op | source)
XLA Modules:
  0.0 257.2 jit_solution(16547996804475532087)
XLA Ops:
  0.6 0.7 fusion.6
  1.3 1.7 reshape.61
  3.0 0.1 pad_slice_fusion
  3.1 0.1 broadcast_in_dim.21
  3.2 0.1 pad_maximum_fusion
  3.2 4.0 %gather_fusion.1 = bf16[64,392,128]{2,1,0:T(8,128)(2,1)} fusion(bf16[9,392,128]{2,1,0:T(8,128)(2,1)S(1)} %pad_maximum_fusion, s32[1024]{0:T(1024)S(1)} %pad_clamp_fusion), kind=kCustom, calls=%fused_computation.1 | custom fusion | bytes 12845312 | tf_op jit(solution)/shard_map/jit(_take)/gather | solution.py:226
  7.3 0.0 slice-start
  7.3 11.1 %all-to-all-start = ((bf16[64,392,128]{2,1,0:T(8,128)(2,1)}), bf16[64,392,128]{2,1,0:T(8,128)(2,1)}, u32[]{:S(2)}, u32[]{:S(2)}) async-start(bf16[64,392,128]{2,1,0:T(8,128)(2,1)} %gather_fusion.1), calls=%async_computation | async-start | bytes 12845056 | tf_op jit(solution)/shard_map/all_to_all | solution.py:228
  18.4 0.0 slice-done
  18.4 0.0 copy-start.2
  18.4 0.0 copy-start.3
  18.5 2.0 gather_fusion
  20.5 0.0 copy-done.2
  20.5 0.4 copy.47
  20.9 0.5 copy.52
  21.3 0.0 copy-done.3
  21.4 2.8 %add_add_fusion = (s32[2,2048]{0,1:T(8,128)S(1)}, s32[2,2048]{0,1:T(8,128)S(1)}, s32[2,2048]{0,1:T(8,128)}) fusion(pred[2,2048]{0,1:T(8,128)(4,1)S(1)} %copy.52, s32[2,2048]{0,1:T(8,128)S(1)} %copy.47), kind=kLoop, calls=%fused_computation.18 | loop fusion | flops 172032 | bytes 69632 | tf_op jit(solution)/shard_map/sub | solution.py:235
  24.2 1.6 multiply_add_fusion
  25.7 135.1 %all-to-all-done = bf16[64,392,128]{2,1,0:T(8,128)(2,1)} async-done(((bf16[64,392,128]{2,1,0:T(8,128)(2,1)}), bf16[64,392,128]{2,1,0:T(8,128)(2,1)}, u32[]{:S(2)}, u32[]{:S(2)}) %all-to-all-start) | async-done | bytes 6422560 | tf_op jit(solution)/shard_map/all_to_all | solution.py:228
  160.8 7.6 %all-to-all-start.1 = ((bf16[64,32,512]{2,1,0:T(8,128)(2,1)}), bf16[64,32,512]{2,1,0:T(8,128)(2,1)}, u32[]{:S(2)}, u32[]{:S(2)}) async-start(bf16[64,32,512]{2,1,0:T(8,128)(2,1)} %gather_fusion), calls=%async_computation.1 | async-start | bytes 4194304 | tf_op jit(solution)/shard_map/all_to_all | solution.py:239
  168.4 0.3 copy.54
  168.8 0.0 copy-start
  168.8 1.7 copy.57
  170.4 2.1 convert_reduce_fusion
  172.6 0.4 fusion.3
  172.9 1.1 copy.58
  174.0 0.0 copy-done
  174.0 0.3 copy.59
  174.4 0.6 copy.62
  175.0 1.4 copy.61.pid_ref
  176.3 2.5 convert_bitcast_fusion.mask_ref
  178.8 0.0 copy-start.1
  178.8 37.3 %shard_map.86.part_ref = f32[2048,512]{1,0:T(8,128)} custom-call(s32[4096]{0:T(1024)} %bitcast.16, bf16[25088,128]{1,0:T(8,128)(2,1)} %bitcast.4.table, f32[2048,2]{1,0:T(8,128)} %convert_bitcast_fusion.mask_ref, bf16[1024,512]{1,0:T(8,128)(2,1)} %wb_ref.3, bf16[1024,512]{1,0:T(8,128)(2,1)} %wb_ref.3), custom_call_target="tpu_custom_call" | custom-call | flops 2147483648 | bytes 8388608 | tf_op jit(solution)/shard_map/pallas_call | solution.py:109
  216.1 0.0 copy-done.1
  216.2 0.0 copy-start.4
  216.2 1.6 select_bitcast_fusion.idx_ref
  217.8 1.8 all-to-all-done.1
  219.6 0.0 copy-done.4
  219.6 0.6 broadcast_in_dim.22.wo_ref
  220.2 20.3 %shard_map.87 = (f32[1,2048]{1,0:T(1,128)}, f32[1,1024]{1,0:T(1,128)}) custom-call(s32[2048,2]{1,0:T(8,128)} %select_bitcast_fusion.idx_ref, f32[2048,512]{1,0:T(8,128)} %shard_map.86.part_ref, bf16[2048,512]{1,0:T(8,128)(2,1)} %bitcast.6.table_ref, bf16[1024,512]{1,0:T(8,128)(2,1)} %wb_ref.3, bf16[1024,512]{1,0:T(8,128)(2,1)} %wb_ref.3, f32[1,512]{1,0:T(1,128)} %bitcast.20, ...), custom_call_target="tpu_custom_call" | custom-call | flops 10737418240 | bytes 6291456 | tf_op jit(solution)/shard_map/pallas_call | solution.py:125
  240.5 15.6 %shard_map.88 = f32[128]{0:T(128)} custom-call(f32[8,128]{1,0:T(8,128)} %bitcast.19), custom_call_target="tpu_custom_call" | custom-call | tf_op jit(solution)/shard_map/pallas_call | solution.py:191
  256.1 1.1 copy.64
  (5 shorter events, 0.1 us)
Async XLA Ops:
  7.3 11.1 %slice-start = ((bf16[8,128,512]{2,1,0:T(8,128)(2,1)}), bf16[8,32,512]{2,1,0:T(8,128)(2,1)S(1)}, s32[]{:S(2)}) async-start(bf16[8,128,512]{2,1,0:T(8,128)(2,1)} %param.7), calls=%async_computation.2 | async-start | bytes 524288 | tf_op jit(solution)/shard_map/slice | solution.py:225
  7.3 153.6 %all-to-all-start = ((bf16[64,392,128]{2,1,0:T(8,128)(2,1)}), bf16[64,392,128]{2,1,0:T(8,128)(2,1)}, u32[]{:S(2)}, u32[]{:S(2)}) async-start(bf16[64,392,128]{2,1,0:T(8,128)(2,1)} %gather_fusion.1), calls=%async_computation | async-start | bytes 12845056 | tf_op jit(solution)/shard_map/all_to_all | solution.py:228
  18.4 2.0 copy-start.2
  18.4 2.9 %copy-start.3 = (s32[2048]{0:T(1024)S(1)}, s32[2048]{0:T(1024)}, u32[]{:S(2)}) copy-start(s32[2048]{0:T(1024)} %param.10) | copy-start | bytes 24580
  160.8 58.8 %all-to-all-start.1 = ((bf16[64,32,512]{2,1,0:T(8,128)(2,1)}), bf16[64,32,512]{2,1,0:T(8,128)(2,1)}, u32[]{:S(2)}, u32[]{:S(2)}) async-start(bf16[64,32,512]{2,1,0:T(8,128)(2,1)} %gather_fusion), calls=%async_computation.1 | async-start | bytes 4194304 | tf_op jit(solution)/shard_map/all_to_all | solution.py:239
  168.8 5.3 %copy-start = (s32[2,2048]{0,1:T(8,128)S(1)}, s32[2,2048]{0,1:T(8,128)}, u32[]{:S(2)}) copy-start(s32[2,2048]{0,1:T(8,128)} %multiply_add_fusion) | copy-start | bytes 49156
  178.8 37.3 %copy-start.1 = (pred[2,2048]{0,1:T(8,128)(4,1)S(1)}, pred[2,2048]{0,1:T(8,128)(4,1)}, u32[]{:S(2)}) copy-start(pred[2,2048]{0,1:T(8,128)(4,1)} %copy.58) | copy-start | bytes 12292
  216.2 3.5 %copy-start.4 = (bf16[512]{0:T(512)(128)(2,1)S(1)}, bf16[512]{0:T(512)(128)(2,1)}, u32[]{:S(2)}) copy-start(bf16[512]{0:T(512)(128)(2,1)} %param.13) | copy-start | bytes 3076

commit v11 on v6

--- a/solution.py
+++ b/solution.py
@@ -61,12 +61,24 @@
     part_ref[...] = total
 
 
-def late_kernel(idx_ref, part_ref, table_ref, wt_ref, wb_ref, bias_ref, wo_ref, pid_ref, score_ref, pool_ref):
+def late_kernel(idx_ref, part_ref, table_ref, wt_ref, wb_ref, bias_ref, wo_ref, pid_ref, score_ref, cost_ref,
+                pool, chunks, recv, send_sems, recv_sems):
     step = pl.program_id(0)
+    steps = pl.num_programs(0)
+    count = recv.shape[0]
+    width = recv.shape[1]
+    me = lax.axis_index("edge")
+    node = lax.axis_index("node")
+    barrier = pltpu.get_barrier_semaphore()
 
     @pl.when(step == 0)
     def _():
-        pool_ref[...] = jnp.zeros_like(pool_ref)
+        def greet(k, carry):
+            pl.semaphore_signal(barrier, 1, device_id=(node, (me + k) % count), device_id_type=pl.DeviceIdType.MESH)
+            return carry
+
+        lax.fori_loop(1, count, greet, 0)
+        pool[...] = jnp.zeros_like(pool)
 
     idx = idx_ref[...]
     rows = table_ref.shape[0]
@@ -78,10 +90,37 @@
         preact = preact + jnp.dot(picked, w_ref[...], preferred_element_type=jnp.float32)
     hidden = gelu_tanh(preact + bias_ref[...])
     scores = jnp.sum(hidden * wo_ref[0:1, :], axis=1, keepdims=True)
-    score_ref[...] = scores
+    score_ref[...] = jnp.broadcast_to(scores, (LATE_TILE, 128)).T[0:1, :]
     pair_range = lax.broadcasted_iota(jnp.int32, (LATE_TILE, PAIRS_ROW), 1)
     pooled = jnp.where(pid_ref[...] == pair_range, scores, 0.0)
-    pool_ref[...] += jnp.sum(pooled, axis=0, keepdims=True)
+    pool[...] += jnp.sum(pooled, axis=0, keepdims=True)
+
+    @pl.when(step == steps - 1)
+    def _():
+        for t in range(count):
+            chunks[t:t + 1, :] = pool[:, t * width:(t + 1) * width]
+        pl.semaphore_wait(barrier, count - 1)
+
+        def remote(target, slot):
+            return pltpu.make_async_remote_copy(
+                chunks.at[pl.ds(target, 1)], recv.at[pl.ds(slot, 1)], send_sems.at[target], recv_sems.at[slot],
+                device_id=(node, target), device_id_type=pl.DeviceIdType.MESH)
+
+        def send(k, carry):
+            remote((me + k) % count, me).start()
+            return carry
+
+        lax.fori_loop(1, count, send, 0)
+
+        def finish(k, carry):
+            remote((me + k) % count, me).wait_send()
+            source = (me + count - k) % count
+            remote(source, source).wait_recv()
+            return carry
+
+        lax.fori_loop(1, count, finish, 0)
+        here = lax.broadcasted_iota(jnp.int32, (count, width), 0)
+        cost_ref[...] = jnp.sum(jnp.where(here == me, chunks[...], recv[...]), axis=0)
 
 
 def early_products(position, mask, table, w_first):
@@ -117,12 +156,13 @@
     )(position.reshape(2 * edges), table, mask, w_first, w_first)
 
 
-def late_scores(late_index, partial, pair_ids, table, w_first, b_first, w_second):
+def late_scores(late_index, partial, pair_ids, table, w_first, b_first, w_second, count):
     edges = late_index.shape[1]
     rows, width = table.shape
     hid = w_first.shape[1]
+    share = PAIRS_ROW // count
     wo8 = jnp.broadcast_to(w_second.astype(jnp.float32)[None, :], (8, hid))
-    scores, pooled = pl.pallas_call(
+    scores, cost = pl.pallas_call(
         late_kernel,
         grid=(edges // LATE_TILE,),
         in_specs=[
@@ -136,19 +176,27 @@
             pl.BlockSpec((LATE_TILE, 1), lambda i: (i, 0)),
         ],
         out_specs=[
-            pl.BlockSpec((LATE_TILE, 1), lambda i: (i, 0)),
-            pl.BlockSpec((1, PAIRS_ROW), lambda i: (0, 0)),
+            pl.BlockSpec((1, LATE_TILE), lambda i: (0, i)),
+            pl.BlockSpec((share,), lambda i: (0,)),
         ],
         out_shape=[
-            jax.ShapeDtypeStruct((edges, 1), jnp.float32),
-            jax.ShapeDtypeStruct((1, PAIRS_ROW), jnp.float32),
-        ],
-        compiler_params=pltpu.CompilerParams(dimension_semantics=("arbitrary",)),
+            jax.ShapeDtypeStruct((1, edges), jnp.float32),
+            jax.ShapeDtypeStruct((share,), jnp.float32),
+        ],
+        scratch_shapes=[
+            pltpu.VMEM((1, PAIRS_ROW), jnp.float32),
+            pltpu.VMEM((count, share), jnp.float32),
+            pltpu.VMEM((count, share), jnp.float32),
+            pltpu.SemaphoreType.DMA((count,)),
+            pltpu.SemaphoreType.DMA((count,)),
+        ],
+        compiler_params=pltpu.CompilerParams(
+            dimension_semantics=("arbitrary",), collective_id=0, has_side_effects=True),
         cost_estimate=pl.CostEstimate(
             flops=2 * edges * 2 * (rows + hid) * width, transcendentals=edges * hid,
             bytes_accessed=rows * width * 2 + edges * hid * 4),
-    )(late_index.T, partial, table, w_first, w_first, b_first.reshape(1, hid), wo8, pair_ids.reshape(edges, 1))
-    return scores.reshape(edges), pooled.reshape(PAIRS_ROW)
+    )(late_index.T, partial, table, w_first, w_first, b_first.reshape(1, hid), wo8, pair_ids)
+    return scores.reshape(edges), cost
 
 
 def body(embedding, send_list, edge_ends, pair_index, w_first, b_first, w_second):
@@ -160,6 +208,7 @@
     lanes = 128
     parts = feature_width // lanes
     early_len = EARLY_ROWS * parts
+    late_rows = block_rows - EARLY_ROWS
     slot_len = early_len + 8
     wanted = send_list[0, 0]
     pick = jnp.where(wanted >= 0, wanted, blocks_here)
@@ -169,29 +218,31 @@
     marks = jnp.where(marks < blocks_here, marks, -1).astype(embedding.dtype)
     marks = jnp.broadcast_to(marks[:, None, None], (blocks_here + 1, 8, lanes))
     early_source = jnp.concatenate([narrow[:, :early_len], marks], axis=1)
-    late_rows = block_rows - EARLY_ROWS
     late_source = jnp.concatenate([embedding[:, EARLY_ROWS:], jnp.zeros((1, late_rows, feature_width), embedding.dtype)], axis=0)
     early_picked = jnp.take(early_source, pick, axis=0, mode="clip")
     late_picked = jnp.take(late_source, pick, axis=0, mode="clip")
     early_arrived = lax.all_to_all(early_picked, "node", split_axis=0, concat_axis=0, tiled=True)
-    late_picked, early_arrived = lax.optimization_barrier((late_picked, early_arrived))
-    late_arrived = lax.all_to_all(late_picked, "node", split_axis=0, concat_axis=0, tiled=True)
-    early_table = early_arrived.reshape(node_count * slot_len, lanes)
-    late_table = late_arrived.reshape(node_count * late_rows, feature_width)
     source = edge_ends // (blocks_here * block_rows)
     block_of = (edge_ends // block_rows) % blocks_here
     within = edge_ends % block_rows
     early = within < EARLY_ROWS
     early_position = source * slot_len + jnp.where(early, within, 0) * parts
+    late_rows = block_rows - EARLY_ROWS
+    late_spot = source * late_rows + within - EARLY_ROWS
+    pair_ids = (pair_index - node_self * PAIRS_ROW).reshape(-1, 1)
+    late_picked, early_arrived, early_position, late_spot, pair_ids = lax.optimization_barrier(
+        (late_picked, early_arrived, early_position, late_spot, pair_ids))
+    late_arrived = lax.all_to_all(late_picked, "node", split_axis=0, concat_axis=0, tiled=True)
+    early_table = early_arrived.reshape(node_count * slot_len, lanes)
+    late_table = late_arrived.reshape(node_count * late_rows, feature_width)
     sent = early_arrived[:, early_len, 0].astype(jnp.int32)
     located = jnp.any((source[..., None] == jnp.arange(node_count, dtype=jnp.int32))
                       & (block_of[..., None] == sent), axis=-1)
     early_mask = (located & early).T.astype(jnp.float32)
-    late_index = jnp.where(located & ~early, source * late_rows + within - EARLY_ROWS, -1)
+    late_index = jnp.where(located & ~early, late_spot, -1)
     partial = early_products(early_position, early_mask, early_table, w_first)
-    pair_ids = pair_index - node_self * PAIRS_ROW
-    edge_score, pooled_sum = late_scores(late_index, partial, pair_ids, late_table, w_first, b_first, w_second)
-    pair_cost = lax.psum_scatter(pooled_sum, "edge", scatter_dimension=0, tiled=True)
+    edge_score, pair_cost = late_scores(late_index, partial, pair_ids, late_table, w_first, b_first, w_second,
+                                        lax.axis_size("edge"))
     return (edge_score, pair_cost)
 
 

time: 269 us -> 255 us (0.948)
  blocking collectives: 23 us -> 0 us
  Pallas kernels: 56.8 us -> 68.9 us
  waiting for transfers between devices: 140 us -> 137 us
    unnamed x1 -> x0, blocking collectives: 23 us -> none
    pallas_call x1, Pallas kernels: 19.7 us -> 31.6 us  [late_scores(): pl.pallas_call(late_kernel, grid=(edges // LATE_TILE,), in_specs=[pl.Bloc...]
    all_to_all x1, waiting for transfers between devices: 140 us -> 135 us  [body(): lax.all_to_all(early_picked, 'node', split_axis=0, concat_axis=0, tiled=T...]
    sub x1 -> x2, other arithmetic: 0.01 us -> 2.8 us  [the longest x1 2.79 us: body(): late_spot = source * late_rows + within - EARLY_ROWS]
  transfers between devices with their start and end apart: 2 -> 2, of which waited for: 1 -> 2; matrix products, arithmetic and copies ran while one was open for 7% -> 8% of each run, Pallas kernels for 14% -> 15%
where the time goes in v11:
time: 255 us; the launch traced here: 254 us
  waiting for transfers between devices  137 us (54%)
  Pallas kernels  68.9 us (27%)
  starting transfers between devices  18.7 us (7%)
  local copies, waits for them, and re-layouts  17.2 us (7%)
  other arithmetic  11.7 us (5%)
    all_to_all x1, waiting for transfers between devices, body(): lax.all_to_all(early_picked, 'node', split_axis=0, concat_axis=0, tiled=T...  135 us
    pallas_call x1, Pallas kernels, early_products(): pl.pallas_call(functools.partial(early_kernel, edges), grid_spec=grid_spe...  37.3 us
    pallas_call x1, Pallas kernels, late_scores(): pl.pallas_call(late_kernel, grid=(edges // LATE_TILE,), in_specs=[pl.Bloc...  31.6 us
    all_to_all x1, starting transfers between devices, body(): lax.all_to_all(early_picked, 'node', split_axis=0, concat_axis=0, tiled=T...  11.1 us
    all_to_all x1, starting transfers between devices, body(): lax.all_to_all(late_picked, 'node', split_axis=0, concat_axis=0, tiled=True)  7.61 us
  transfers between devices with their start and end apart: 2, of which 2 were waited for; matrix products, arithmetic and copies ran while one was open for 8% of the time, Pallas kernels for 15%

profile of v11, /device:TPU:2, one launch (start us, length us, event | category | flops | bytes accessed | tf_op | source)
XLA Modules:
  0.0 254.3 jit_solution(10070446975098220254)
XLA Ops:
  0.6 0.7 fusion.6
  1.3 1.7 reshape.61
  3.0 0.1 pad_slice_fusion
  3.1 0.1 broadcast_in_dim.21
  3.2 0.1 pad_maximum_fusion
  3.2 4.0 %gather_fusion.1 = bf16[64,392,128]{2,1,0:T(8,128)(2,1)} fusion(bf16[9,392,128]{2,1,0:T(8,128)(2,1)S(1)} %pad_maximum_fusion, s32[1024]{0:T(1024)S(1)} %pad_clamp_fusion), kind=kCustom, calls=%fused_computation.1 | custom fusion | bytes 12845312 | tf_op jit(solution)/shard_map/jit(_take)/gather | solution.py:222
  7.3 0.0 slice-start
  7.3 11.1 %all-to-all-start = ((bf16[64,392,128]{2,1,0:T(8,128)(2,1)}), bf16[64,392,128]{2,1,0:T(8,128)(2,1)}, u32[]{:S(2)}, u32[]{:S(2)}) async-start(bf16[64,392,128]{2,1,0:T(8,128)(2,1)} %gather_fusion.1), calls=%async_computation | async-start | bytes 12845056 | tf_op jit(solution)/shard_map/all_to_all | solution.py:224
  18.4 0.0 slice-done
  18.4 0.0 copy-start.2
  18.4 0.0 copy-start.3
  18.5 2.0 gather_fusion
  20.5 0.0 copy-done.2
  20.5 0.4 copy.47
  20.9 0.5 copy.52
  21.3 0.0 copy-done.3
  21.4 2.8 %add_add_fusion = (s32[2,2048]{0,1:T(8,128)S(1)}, s32[2,2048]{0,1:T(8,128)S(1)}, s32[2,2048]{0,1:T(8,128)}) fusion(pred[2,2048]{0,1:T(8,128)(4,1)S(1)} %copy.52, s32[2,2048]{0,1:T(8,128)S(1)} %copy.47), kind=kLoop, calls=%fused_computation.18 | loop fusion | flops 172032 | bytes 69632 | tf_op jit(solution)/shard_map/sub | solution.py:231
  24.2 1.6 multiply_add_fusion
  25.7 135.1 %all-to-all-done = bf16[64,392,128]{2,1,0:T(8,128)(2,1)} async-done(((bf16[64,392,128]{2,1,0:T(8,128)(2,1)}), bf16[64,392,128]{2,1,0:T(8,128)(2,1)}, u32[]{:S(2)}, u32[]{:S(2)}) %all-to-all-start) | async-done | bytes 6422560 | tf_op jit(solution)/shard_map/all_to_all | solution.py:224
  160.8 7.6 %all-to-all-start.1 = ((bf16[64,32,512]{2,1,0:T(8,128)(2,1)}), bf16[64,32,512]{2,1,0:T(8,128)(2,1)}, u32[]{:S(2)}, u32[]{:S(2)}) async-start(bf16[64,32,512]{2,1,0:T(8,128)(2,1)} %gather_fusion), calls=%async_computation.1 | async-start | bytes 4194304 | tf_op jit(solution)/shard_map/all_to_all | solution.py:235
  168.4 0.3 copy.54
  168.8 0.0 copy-start
  168.8 1.7 copy.57
  170.4 2.1 convert_reduce_fusion
  172.6 0.4 fusion.3
  172.9 1.1 copy.58
  174.0 0.0 copy-done
  174.0 0.3 copy.59
  174.4 0.6 copy.62
  175.0 1.4 copy.61.pid_ref
  176.3 2.5 convert_bitcast_fusion.mask_ref
  178.8 0.0 copy-start.1
  178.8 37.3 %shard_map.86.part_ref = f32[2048,512]{1,0:T(8,128)} custom-call(s32[4096]{0:T(1024)} %bitcast.15, bf16[25088,128]{1,0:T(8,128)(2,1)} %bitcast.4.table, f32[2048,2]{1,0:T(8,128)} %convert_bitcast_fusion.mask_ref, bf16[1024,512]{1,0:T(8,128)(2,1)} %wb_ref.3, bf16[1024,512]{1,0:T(8,128)(2,1)} %wb_ref.3), custom_call_target="tpu_custom_call" | custom-call | flops 2147483648 | bytes 8388608 | tf_op jit(solution)/shard_map/pallas_call | solution.py:148
  216.1 0.0 copy-done.1
  216.2 0.0 copy-start.4
  216.2 1.6 select_bitcast_fusion.idx_ref
  217.8 1.8 all-to-all-done.1
  219.6 0.0 copy-done.4
  219.6 0.6 broadcast_in_dim.22.wo_ref
  220.2 31.6 %shard_map.87 = (f32[1,2048]{1,0:T(1,128)}, f32[128]{0:T(128)}) custom-call(s32[2048,2]{1,0:T(8,128)} %select_bitcast_fusion.idx_ref, f32[2048,512]{1,0:T(8,128)} %shard_map.86.part_ref, bf16[2048,512]{1,0:T(8,128)(2,1)} %bitcast.6.table_ref, bf16[1024,512]{1,0:T(8,128)(2,1)} %wb_ref.3, bf16[1024,512]{1,0:T(8,128)(2,1)} %wb_ref.3, f32[1,512]{1,0:T(1,128)} %bitcast.19, ...), custom_call_target="tpu_custom_call" | custom-call | flops 10737418240 | bytes 6291456 | tf_op jit(solution)/shard_map/pallas_call | solution.py:165
  251.8 1.3 copy.65
  253.1 1.2 copy.66
  (5 shorter events, 0.1 us)
Async XLA Ops:
  7.3 11.1 %slice-start = ((bf16[8,128,512]{2,1,0:T(8,128)(2,1)}), bf16[8,32,512]{2,1,0:T(8,128)(2,1)S(1)}, s32[]{:S(2)}) async-start(bf16[8,128,512]{2,1,0:T(8,128)(2,1)} %param.7), calls=%async_computation.2 | async-start | bytes 524288 | tf_op jit(solution)/shard_map/slice | solution.py:221
  7.3 153.6 %all-to-all-start = ((bf16[64,392,128]{2,1,0:T(8,128)(2,1)}), bf16[64,392,128]{2,1,0:T(8,128)(2,1)}, u32[]{:S(2)}, u32[]{:S(2)}) async-start(bf16[64,392,128]{2,1,0:T(8,128)(2,1)} %gather_fusion.1), calls=%async_computation | async-start | bytes 12845056 | tf_op jit(solution)/shard_map/all_to_all | solution.py:224
  18.4 2.0 copy-start.2
  18.4 2.9 %copy-start.3 = (s32[2048]{0:T(1024)S(1)}, s32[2048]{0:T(1024)}, u32[]{:S(2)}) copy-start(s32[2048]{0:T(1024)} %param.10) | copy-start | bytes 24580
  160.8 58.8 %all-to-all-start.1 = ((bf16[64,32,512]{2,1,0:T(8,128)(2,1)}), bf16[64,32,512]{2,1,0:T(8,128)(2,1)}, u32[]{:S(2)}, u32[]{:S(2)}) async-start(bf16[64,32,512]{2,1,0:T(8,128)(2,1)} %gather_fusion), calls=%async_computation.1 | async-start | bytes 4194304 | tf_op jit(solution)/shard_map/all_to_all | solution.py:235
  168.8 5.3 %copy-start = (s32[2,2048]{0,1:T(8,128)S(1)}, s32[2,2048]{0,1:T(8,128)}, u32[]{:S(2)}) copy-start(s32[2,2048]{0,1:T(8,128)} %multiply_add_fusion) | copy-start | bytes 49156
  178.8 37.3 %copy-start.1 = (pred[2,2048]{0,1:T(8,128)(4,1)S(1)}, pred[2,2048]{0,1:T(8,128)(4,1)}, u32[]{:S(2)}) copy-start(pred[2,2048]{0,1:T(8,128)(4,1)} %copy.58) | copy-start | bytes 12292
  216.2 3.5 %copy-start.4 = (bf16[512]{0:T(512)(128)(2,1)S(1)}, bf16[512]{0:T(512)(128)(2,1)}, u32[]{:S(2)}) copy-start(bf16[512]{0:T(512)(128)(2,1)} %param.13) | copy-start | bytes 3076

commit v12 on v11

--- a/solution.py
+++ b/solution.py
@@ -48,7 +48,7 @@
     for end in range(2):
         pltpu.make_async_copy(table.at[pl.ds(0, TILE * parts)], buf.at[end, slot], sems.at[end, slot]).wait()
 
-    mask = mask_ref[...]
+    mask = mask_ref[...].T
     total = None
     for end, w_ref in ((0, wt_ref), (1, wb_ref)):
         wide[...] = buf[end, slot].astype(jnp.float32)
@@ -80,7 +80,7 @@
         lax.fori_loop(1, count, greet, 0)
         pool[...] = jnp.zeros_like(pool)
 
-    idx = idx_ref[...]
+    idx = idx_ref[...].T
     rows = table_ref.shape[0]
     slots = lax.broadcasted_iota(jnp.int32, (LATE_TILE, rows), 1)
     preact = part_ref[...]
@@ -134,7 +134,7 @@
         grid=(edges // TILE,),
         in_specs=[
             pl.BlockSpec(memory_space=pl.ANY),
-            pl.BlockSpec((TILE, 2), lambda i, p: (i, 0)),
+            pl.BlockSpec((2, TILE), lambda i, p: (0, i)),
             pl.BlockSpec((width, hid), lambda i, p: (0, 0)),
             pl.BlockSpec((width, hid), lambda i, p: (1, 0)),
         ],
@@ -166,7 +166,7 @@
         late_kernel,
         grid=(edges // LATE_TILE,),
         in_specs=[
-            pl.BlockSpec((LATE_TILE, 2), lambda i: (i, 0)),
+            pl.BlockSpec((2, LATE_TILE), lambda i: (0, i)),
             pl.BlockSpec((LATE_TILE, hid), lambda i: (i, 0)),
             pl.BlockSpec((rows, width), lambda i: (0, 0)),
             pl.BlockSpec((width, hid), lambda i: (0, 0)),
@@ -195,7 +195,7 @@
         cost_estimate=pl.CostEstimate(
             flops=2 * edges * 2 * (rows + hid) * width, transcendentals=edges * hid,
             bytes_accessed=rows * width * 2 + edges * hid * 4),
-    )(late_index.T, partial, table, w_first, w_first, b_first.reshape(1, hid), wo8, pair_ids)
+    )(late_index, partial, table, w_first, w_first, b_first.reshape(1, hid), wo8, pair_ids)
     return scores.reshape(edges), cost
 
 
@@ -238,7 +238,7 @@
     sent = early_arrived[:, early_len, 0].astype(jnp.int32)
     located = jnp.any((source[..., None] == jnp.arange(node_count, dtype=jnp.int32))
                       & (block_of[..., None] == sent), axis=-1)
-    early_mask = (located & early).T.astype(jnp.float32)
+    early_mask = (located & early).astype(jnp.float32)
     late_index = jnp.where(located & ~early, late_spot, -1)
     partial = early_products(early_position, early_mask, early_table, w_first)
     edge_score, pair_cost = late_scores(late_index, partial, pair_ids, late_table, w_first, b_first, w_second,

time: 255 us -> 256 us (level)
  waiting for transfers between devices: 137 us -> 147 us
  other arithmetic: 11.7 us -> 4.61 us
  local copies, waits for them, and re-layouts: 17.2 us -> 13.7 us
    all_to_all x1, waiting for transfers between devices: 1.82 us -> 7.05 us  [body(): lax.all_to_all(late_picked, 'node', split_axis=0, concat_axis=0, tiled=True)]
    all_to_all x1, waiting for transfers between devices: 135 us -> 140 us  [body(): lax.all_to_all(early_picked, 'node', split_axis=0, concat_axis=0, tiled=T...]
    sub x1, other arithmetic: 2.79 us -> 0.12 us  [body(): late_spot = source * late_rows + within - EARLY_ROWS]
  transfers between devices with their start and end apart: 2 -> 2, of which waited for: 2 -> 2; matrix products, arithmetic and copies ran while one was open for 8% -> 3% of each run, Pallas kernels for 15% -> 15%
where the time goes in v12:
time: 256 us
  waiting for transfers between devices  147 us (57%)
  Pallas kernels  70.7 us (28%)
  starting transfers between devices  18.5 us (7%)
  local copies, waits for them, and re-layouts  13.7 us (5%)
  other arithmetic  4.61 us (2%)
    all_to_all x1, waiting for transfers between devices, body(): lax.all_to_all(early_picked, 'node', split_axis=0, concat_axis=0, tiled=T...  140 us
    pallas_call x1, Pallas kernels, early_products(): pl.pallas_call(functools.partial(early_kernel, edges), grid_spec=grid_spe...  38.5 us
    pallas_call x1, Pallas kernels, late_scores(): pl.pallas_call(late_kernel, grid=(edges // LATE_TILE,), in_specs=[pl.Bloc...  32.1 us
    all_to_all x1, starting transfers between devices, body(): lax.all_to_all(early_picked, 'node', split_axis=0, concat_axis=0, tiled=T...  11.1 us
    all_to_all x1, starting transfers between devices, body(): lax.all_to_all(late_picked, 'node', split_axis=0, concat_axis=0, tiled=True)  7.4 us
    all_to_all x1, waiting for transfers between devices, body(): lax.all_to_all(late_picked, 'node', split_axis=0, concat_axis=0, tiled=True)  7.05 us
  transfers between devices with their start and end apart: 2, of which 2 were waited for; matrix products, arithmetic and copies ran while one was open for 3% of the time, Pallas kernels for 15%

profile of v12, /device:TPU:2, one launch (start us, length us, event | category | flops | bytes accessed | tf_op | source)
XLA Modules:
  0.0 255.5 jit_solution(17719454452866518412)
XLA Ops:
  0.6 0.7 fusion.3
  1.3 1.7 reshape.61
  3.0 0.1 pad_slice_fusion
  3.1 0.1 broadcast_in_dim.21
  3.2 0.1 pad_maximum_fusion
  3.2 4.0 %gather_fusion.1 = bf16[64,392,128]{2,1,0:T(8,128)(2,1)} fusion(bf16[9,392,128]{2,1,0:T(8,128)(2,1)S(1)} %pad_maximum_fusion, s32[1024]{0:T(1024)S(1)} %pad_clamp_fusion), kind=kCustom, calls=%fused_computation.1 | custom fusion | bytes 12845312 | tf_op jit(solution)/shard_map/jit(_take)/gather | solution.py:222
  7.3 0.0 slice-start
  7.3 11.1 %all-to-all-start = ((bf16[64,392,128]{2,1,0:T(8,128)(2,1)}), bf16[64,392,128]{2,1,0:T(8,128)(2,1)}, u32[]{:S(2)}, u32[]{:S(2)}) async-start(bf16[64,392,128]{2,1,0:T(8,128)(2,1)} %gather_fusion.1), calls=%async_computation | async-start | bytes 12845056 | tf_op jit(solution)/shard_map/all_to_all | solution.py:224
  18.4 0.0 slice-done
  18.4 0.0 copy-start.2
  18.5 0.0 copy-start.1
  18.5 2.0 gather_fusion
  20.5 0.0 copy-done.2
  20.5 0.0 copy-done.1
  20.5 0.1 add_add_fusion
  20.6 140.2 %all-to-all-done = bf16[64,392,128]{2,1,0:T(8,128)(2,1)} async-done(((bf16[64,392,128]{2,1,0:T(8,128)(2,1)}), bf16[64,392,128]{2,1,0:T(8,128)(2,1)}, u32[]{:S(2)}, u32[]{:S(2)}) %all-to-all-start) | async-done | bytes 6422560 | tf_op jit(solution)/shard_map/all_to_all | solution.py:224
  160.8 7.4 %all-to-all-start.1 = ((bf16[64,32,512]{2,1,0:T(8,128)(2,1)}), bf16[64,32,512]{2,1,0:T(8,128)(2,1)S(1)}, u32[]{:S(2)}, u32[]{:S(2)}) async-start(bf16[64,32,512]{2,1,0:T(8,128)(2,1)} %gather_fusion), calls=%async_computation.1 | async-start | bytes 4194304 | tf_op jit(solution)/shard_map/all_to_all | solution.py:235
  168.2 0.6 copy.13
  168.8 1.4 copy.12.pid_ref
  170.2 2.1 convert_reduce_fusion
  172.3 0.4 fusion.1
  172.7 0.6 and_convert_fusion.mask_ref
  173.3 0.0 copy-start.3
  173.3 38.5 %shard_map.86.part_ref = f32[2048,512]{1,0:T(8,128)} custom-call(s32[4096]{0:T(1024)} %bitcast.12, bf16[25088,128]{1,0:T(8,128)(2,1)} %bitcast.3.table, f32[2,2048]{1,0:T(2,128)} %and_convert_fusion.mask_ref, bf16[1024,512]{1,0:T(8,128)(2,1)} %wb_ref.3, bf16[1024,512]{1,0:T(8,128)(2,1)} %wb_ref.3), custom_call_target="tpu_custom_call" | custom-call | flops 2147483648 | bytes 8388608 | tf_op jit(solution)/shard_map/pallas_call | solution.py:148
  211.8 0.6 and_select_fusion.idx_ref
  212.5 7.0 %all-to-all-done.1 = bf16[64,32,512]{2,1,0:T(8,128)(2,1)S(1)} async-done(((bf16[64,32,512]{2,1,0:T(8,128)(2,1)}), bf16[64,32,512]{2,1,0:T(8,128)(2,1)S(1)}, u32[]{:S(2)}, u32[]{:S(2)}) %all-to-all-start.1) | async-done | bytes 2097184 | tf_op jit(solution)/shard_map/all_to_all | solution.py:235
  219.5 0.0 copy-start
  219.5 0.0 copy-done.3
  219.5 0.6 broadcast_in_dim.22.wo_ref
  220.1 0.7 copy-done
  220.9 32.1 %shard_map.87 = (f32[1,2048]{1,0:T(1,128)}, f32[128]{0:T(128)}) custom-call(s32[2,2048]{1,0:T(2,128)} %and_select_fusion.idx_ref, f32[2048,512]{1,0:T(8,128)} %shard_map.86.part_ref, bf16[2048,512]{1,0:T(8,128)(2,1)} %bitcast.11, bf16[1024,512]{1,0:T(8,128)(2,1)} %wb_ref.3, bf16[1024,512]{1,0:T(8,128)(2,1)} %wb_ref.3, f32[1,512]{1,0:T(1,128)} %bitcast.16, ...), custom_call_target="tpu_custom_call" | custom-call | flops 10737418240 | bytes 6291456 | tf_op jit(solution)/shard_map/pallas_call | solution.py:165
  253.0 1.3 copy.16
  254.3 1.2 copy.17
  (5 shorter events, 0.1 us)
Async XLA Ops:
  7.3 11.1 %slice-start = ((bf16[8,128,512]{2,1,0:T(8,128)(2,1)}), bf16[8,32,512]{2,1,0:T(8,128)(2,1)S(1)}, s32[]{:S(2)}) async-start(bf16[8,128,512]{2,1,0:T(8,128)(2,1)} %param.7), calls=%async_computation.2 | async-start | bytes 524288 | tf_op jit(solution)/shard_map/slice | solution.py:221
  7.3 153.6 %all-to-all-start = ((bf16[64,392,128]{2,1,0:T(8,128)(2,1)}), bf16[64,392,128]{2,1,0:T(8,128)(2,1)}, u32[]{:S(2)}, u32[]{:S(2)}) async-start(bf16[64,392,128]{2,1,0:T(8,128)(2,1)} %gather_fusion.1), calls=%async_computation | async-start | bytes 12845056 | tf_op jit(solution)/shard_map/all_to_all | solution.py:224
  18.4 2.0 copy-start.2
  18.5 2.0 copy-start.1
  160.8 58.7 %all-to-all-start.1 = ((bf16[64,32,512]{2,1,0:T(8,128)(2,1)}), bf16[64,32,512]{2,1,0:T(8,128)(2,1)S(1)}, u32[]{:S(2)}, u32[]{:S(2)}) async-start(bf16[64,32,512]{2,1,0:T(8,128)(2,1)} %gather_fusion), calls=%async_computation.1 | async-start | bytes 4194304 | tf_op jit(solution)/shard_map/all_to_all | solution.py:235
  173.3 46.2 %copy-start.3 = (bf16[512]{0:T(512)(128)(2,1)S(1)}, bf16[512]{0:T(512)(128)(2,1)}, u32[]{:S(2)}) copy-start(bf16[512]{0:T(512)(128)(2,1)} %param.13) | copy-start | bytes 3076
  219.5 1.4 copy-start

commit v13 on v11

--- a/solution.py
+++ b/solution.py
@@ -209,37 +209,34 @@
     parts = feature_width // lanes
     early_len = EARLY_ROWS * parts
     late_rows = block_rows - EARLY_ROWS
-    slot_len = early_len + 8
+    slot_len = early_len
     wanted = send_list[0, 0]
     pick = jnp.where(wanted >= 0, wanted, blocks_here)
     narrow = embedding.reshape(blocks_here, block_rows * parts, lanes)
     narrow = jnp.concatenate([narrow, jnp.zeros((1, block_rows * parts, lanes), embedding.dtype)], axis=0)
-    marks = jnp.arange(blocks_here + 1, dtype=jnp.int32)
-    marks = jnp.where(marks < blocks_here, marks, -1).astype(embedding.dtype)
-    marks = jnp.broadcast_to(marks[:, None, None], (blocks_here + 1, 8, lanes))
-    early_source = jnp.concatenate([narrow[:, :early_len], marks], axis=1)
+    early_source = narrow[:, :early_len]
     late_source = jnp.concatenate([embedding[:, EARLY_ROWS:], jnp.zeros((1, late_rows, feature_width), embedding.dtype)], axis=0)
     early_picked = jnp.take(early_source, pick, axis=0, mode="clip")
     late_picked = jnp.take(late_source, pick, axis=0, mode="clip")
     early_arrived = lax.all_to_all(early_picked, "node", split_axis=0, concat_axis=0, tiled=True)
+    lists = lax.all_gather(wanted, "node")
+    sent = lax.dynamic_index_in_dim(lists, node_self, axis=1, keepdims=False)
     source = edge_ends // (blocks_here * block_rows)
     block_of = (edge_ends // block_rows) % blocks_here
     within = edge_ends % block_rows
     early = within < EARLY_ROWS
     early_position = source * slot_len + jnp.where(early, within, 0) * parts
-    late_rows = block_rows - EARLY_ROWS
     late_spot = source * late_rows + within - EARLY_ROWS
     pair_ids = (pair_index - node_self * PAIRS_ROW).reshape(-1, 1)
-    late_picked, early_arrived, early_position, late_spot, pair_ids = lax.optimization_barrier(
-        (late_picked, early_arrived, early_position, late_spot, pair_ids))
-    late_arrived = lax.all_to_all(late_picked, "node", split_axis=0, concat_axis=0, tiled=True)
-    early_table = early_arrived.reshape(node_count * slot_len, lanes)
-    late_table = late_arrived.reshape(node_count * late_rows, feature_width)
-    sent = early_arrived[:, early_len, 0].astype(jnp.int32)
     located = jnp.any((source[..., None] == jnp.arange(node_count, dtype=jnp.int32))
                       & (block_of[..., None] == sent), axis=-1)
     early_mask = (located & early).T.astype(jnp.float32)
     late_index = jnp.where(located & ~early, late_spot, -1)
+    late_picked, early_arrived, early_position, early_mask, late_index, pair_ids = lax.optimization_barrier(
+        (late_picked, early_arrived, early_position, early_mask, late_index, pair_ids))
+    late_arrived = lax.all_to_all(late_picked, "node", split_axis=0, concat_axis=0, tiled=True)
+    early_table = early_arrived.reshape(node_count * slot_len, lanes)
+    late_table = late_arrived.reshape(node_count * late_rows, feature_width)
     partial = early_products(early_position, early_mask, early_table, w_first)
     edge_score, pair_cost = late_scores(late_index, partial, pair_ids, late_table, w_first, b_first, w_second,
                                         lax.axis_size("edge"))

time: 255 us -> 288 us (1.13)
  blocking collectives: 0 us -> 158 us
  waiting for transfers between devices: 137 us -> 11.7 us
    all_gather x0 -> x1, blocking collectives: none -> 158 us  [body(): lists = lax.all_gather(wanted, 'node')]
    all_to_all x1, waiting for transfers between devices: 135 us -> 0.01 us  [body(): lax.all_to_all(early_picked, 'node', split_axis=0, concat_axis=0, tiled=T...]
    all_to_all x1, waiting for transfers between devices: 1.82 us -> 11.7 us  [body(): lax.all_to_all(late_picked, 'node', split_axis=0, concat_axis=0, tiled=True)]
  transfers between devices with their start and end apart: 2 -> 2, of which waited for: 2 -> 1; matrix products, arithmetic and copies ran while one was open for 8% -> 6% of each run, Pallas kernels for 15% -> 13%
where the time goes in v13:
time: 288 us; the launch traced here: 287 us
  blocking collectives  158 us (55%)
  Pallas kernels  68.8 us (24%)
  starting transfers between devices  19.9 us (7%)
  local copies, waits for them, and re-layouts  19 us (7%)
  waiting for transfers between devices  11.7 us (4%)
  other arithmetic  9.13 us (3%)
    all_gather x1, blocking collectives, body(): lists = lax.all_gather(wanted, 'node')  158 us
    pallas_call x1, Pallas kernels, early_products(): pl.pallas_call(functools.partial(early_kernel, edges), grid_spec=grid_spe...  37.3 us
    pallas_call x1, Pallas kernels, late_scores(): pl.pallas_call(late_kernel, grid=(edges // LATE_TILE,), in_specs=[pl.Bloc...  31.5 us
    all_to_all x1, waiting for transfers between devices, body(): lax.all_to_all(late_picked, 'node', split_axis=0, concat_axis=0, tiled=True)  11.7 us
    all_to_all x1, starting transfers between devices, body(): lax.all_to_all(early_picked, 'node', split_axis=0, concat_axis=0, tiled=T...  11.1 us
    all_to_all x1, starting transfers between devices, body(): lax.all_to_all(late_picked, 'node', split_axis=0, concat_axis=0, tiled=True)  8.82 us
  transfers between devices with their start and end apart: 2, of which 1 were waited for; matrix products, arithmetic and copies ran while one was open for 6% of the time, Pallas kernels for 13%

profile of v13, /device:TPU:2, one launch (start us, length us, event | category | flops | bytes accessed | tf_op | source)
XLA Modules:
  0.0 287.3 jit_solution(10909641206388151906)
XLA Ops:
  0.6 0.7 fusion.6
  1.3 1.7 reshape.49
  3.0 0.1 pad_slice_fusion
  3.1 4.0 %gather_fusion.1 = bf16[64,384,128]{2,1,0:T(8,128)(2,1)} fusion(bf16[9,384,128]{2,1,0:T(8,128)(2,1)S(1)} %pad_slice_fusion, s32[1024]{0:T(1024)S(1)} %pad_clamp_fusion), kind=kCustom, calls=%fused_computation.1 | custom fusion | bytes 12583168 | tf_op jit(solution)/shard_map/jit(_take)/gather | solution.py:219
  7.1 0.0 slice-start
  7.1 11.1 %all-to-all-start = ((bf16[64,384,128]{2,1,0:T(8,128)(2,1)}), bf16[64,384,128]{2,1,0:T(8,128)(2,1)}, u32[]{:S(2)}, u32[]{:S(2)}) async-start(bf16[64,384,128]{2,1,0:T(8,128)(2,1)} %gather_fusion.1), calls=%async_computation | async-start | bytes 12582912 | tf_op jit(solution)/shard_map/all_to_all | solution.py:221
  18.2 0.0 copy-start.1
  18.2 0.0 slice-done
  18.2 2.0 gather_fusion
  20.3 0.0 copy-done.1
  20.3 0.0 copy-start.4
  20.3 0.0 copy-start.2
  20.3 0.4 copy.46
  20.7 0.5 copy.51
  21.1 2.9 %multiply_add_fusion = (s32[2,2048]{0,1:T(8,128)S(1)}, s32[2,2048]{0,1:T(8,128)S(1)}, s32[2,2048]{0,1:T(8,128)}) fusion(pred[2,2048]{0,1:T(8,128)(4,1)S(1)} %copy.51, s32[2,2048]{0,1:T(8,128)S(1)} %copy.46), kind=kLoop, calls=%fused_computation.19 | loop fusion | flops 180224 | bytes 69632 | tf_op jit(solution)/shard_map/add | solution.py:228
  24.0 1.6 copy.56
  25.6 0.3 copy.54
  25.9 0.0 copy-done.4
  25.9 158.1 %all-gather = s32[64,1,64]{2,1,0:T(1,128)S(1)} all-gather(s32[1,1,64]{2,1,0:T(1,128)S(1)} %copy-done.4), channel_id=2, replica_groups=mesh['node'=64,'edge'=8] {'node'}, dimensions={0}, use_global_device_ids=true | all-gather | bytes 16640 | tf_op jit(solution)/shard_map/all_gather | solution.py:222
  184.0 1.3 dynamic-slice_reduce_fusion
  185.3 0.4 fusion.3
  185.7 1.1 copy.57
  186.7 0.0 copy-done.2
  186.7 2.5 convert_bitcast_fusion.mask_ref
  189.2 2.7 add_select_fusion.4
  191.9 0.0 all-to-all-done
  191.9 8.8 %all-to-all-start.1 = ((bf16[64,32,512]{2,1,0:T(8,128)(2,1)}), bf16[64,32,512]{2,1,0:T(8,128)(2,1)S(1)}, u32[]{:S(2)}, u32[]{:S(2)}) async-start(bf16[64,32,512]{2,1,0:T(8,128)(2,1)} %gather_fusion), calls=%async_computation.1 | async-start | bytes 4194304 | tf_op jit(solution)/shard_map/all_to_all | solution.py:237
  200.8 0.3 copy.59
  201.1 0.6 copy.63
  201.7 1.4 copy.60.pid_ref
  203.1 0.0 copy-start.3
  203.1 37.3 %shard_map.86.part_ref = f32[2048,512]{1,0:T(8,128)} custom-call(s32[4096]{0:T(1024)} %bitcast.16, bf16[24576,128]{1,0:T(8,128)(2,1)} %bitcast.5.table, f32[2048,2]{1,0:T(8,128)} %convert_bitcast_fusion.mask_ref, bf16[1024,512]{1,0:T(8,128)(2,1)} %wb_ref.3, bf16[1024,512]{1,0:T(8,128)(2,1)} %wb_ref.3), custom_call_target="tpu_custom_call" | custom-call | flops 2147483648 | bytes 8388608 | tf_op jit(solution)/shard_map/pallas_call | solution.py:148
  240.4 11.7 %all-to-all-done.1 = bf16[64,32,512]{2,1,0:T(8,128)(2,1)S(1)} async-done(((bf16[64,32,512]{2,1,0:T(8,128)(2,1)}), bf16[64,32,512]{2,1,0:T(8,128)(2,1)S(1)}, u32[]{:S(2)}, u32[]{:S(2)}) %all-to-all-start.1) | async-done | bytes 2097184 | tf_op jit(solution)/shard_map/all_to_all | solution.py:237
  252.0 0.0 copy-start
  252.0 0.0 copy-done.3
  252.0 0.6 broadcast_in_dim.14.wo_ref
  252.7 0.7 copy-done
  253.4 31.5 %shard_map.87 = (f32[1,2048]{1,0:T(1,128)}, f32[128]{0:T(128)}) custom-call(s32[2048,2]{1,0:T(8,128)} %bitcast.15, f32[2048,512]{1,0:T(8,128)} %shard_map.86.part_ref, bf16[2048,512]{1,0:T(8,128)(2,1)} %bitcast.14, bf16[1024,512]{1,0:T(8,128)(2,1)} %wb_ref.3, bf16[1024,512]{1,0:T(8,128)(2,1)} %wb_ref.3, f32[1,512]{1,0:T(1,128)} %bitcast.20, ...), custom_call_target="tpu_custom_call" | custom-call | flops 10737418240 | bytes 6291456 | tf_op jit(solution)/shard_map/pallas_call | solution.py:165
  284.9 1.3 copy.66
  286.2 1.1 copy.67
  (4 shorter events, 0.0 us)
Async XLA Ops:
  7.1 11.1 %slice-start = ((bf16[8,128,512]{2,1,0:T(8,128)(2,1)}), bf16[8,32,512]{2,1,0:T(8,128)(2,1)S(1)}, s32[]{:S(2)}) async-start(bf16[8,128,512]{2,1,0:T(8,128)(2,1)} %param.7), calls=%async_computation.2 | async-start | bytes 524288 | tf_op jit(solution)/shard_map/slice | solution.py:218
  7.1 184.9 %all-to-all-start = ((bf16[64,384,128]{2,1,0:T(8,128)(2,1)}), bf16[64,384,128]{2,1,0:T(8,128)(2,1)}, u32[]{:S(2)}, u32[]{:S(2)}) async-start(bf16[64,384,128]{2,1,0:T(8,128)(2,1)} %gather_fusion.1), calls=%async_computation | async-start | bytes 12582912 | tf_op jit(solution)/shard_map/all_to_all | solution.py:221
  18.2 2.1 copy-start.1
  20.3 5.7 %copy-start.4 = (s32[1,1,64]{2,1,0:T(1,128)S(1)}, s32[1,1,64]{2,1,0:T(1,128)}, u32[]{:S(2)}) copy-start(s32[1,1,64]{2,1,0:T(1,128)} %param.8) | copy-start | bytes 772
  20.3 166.5 %copy-start.2 = (s32[2048]{0:T(1024)S(1)}, s32[2048]{0:T(1024)}, u32[]{:S(2)}) copy-start(s32[2048]{0:T(1024)} %param.10) | copy-start | bytes 24580
  191.9 60.1 %all-to-all-start.1 = ((bf16[64,32,512]{2,1,0:T(8,128)(2,1)}), bf16[64,32,512]{2,1,0:T(8,128)(2,1)S(1)}, u32[]{:S(2)}, u32[]{:S(2)}) async-start(bf16[64,32,512]{2,1,0:T(8,128)(2,1)} %gather_fusion), calls=%async_computation.1 | async-start | bytes 4194304 | tf_op jit(solution)/shard_map/all_to_all | solution.py:237
  203.1 49.0 %copy-start.3 = (bf16[512]{0:T(512)(128)(2,1)S(1)}, bf16[512]{0:T(512)(128)(2,1)}, u32[]{:S(2)}) copy-start(bf16[512]{0:T(512)(128)(2,1)} %param.13) | copy-start | bytes 3076
  252.0 1.4 copy-start

commit v14 on v11

--- a/solution.py
+++ b/solution.py
@@ -9,7 +9,7 @@
 
 PAIRS_ROW = 1024
 TILE = 256
-LATE_TILE = 256
+LATE_TILE = 512
 EARLY_ROWS = 96
 
 

time: 255 us -> 253 us (level)
  no operation moved by 1% of the time
where the time goes in v14:
time: 253 us; the launch traced here: 252 us
  waiting for transfers between devices  137 us (54%)
  Pallas kernels  66.7 us (26%)
  starting transfers between devices  18.7 us (7%)
  local copies, waits for them, and re-layouts  17.2 us (7%)
  other arithmetic  11.7 us (5%)
    all_to_all x1, waiting for transfers between devices, body(): lax.all_to_all(early_picked, 'node', split_axis=0, concat_axis=0, tiled=T...  135 us
    pallas_call x1, Pallas kernels, early_products(): pl.pallas_call(functools.partial(early_kernel, edges), grid_spec=grid_spe...  37.3 us
    pallas_call x1, Pallas kernels, late_scores(): pl.pallas_call(late_kernel, grid=(edges // LATE_TILE,), in_specs=[pl.Bloc...  29.4 us
    all_to_all x1, starting transfers between devices, body(): lax.all_to_all(early_picked, 'node', split_axis=0, concat_axis=0, tiled=T...  11.1 us
    all_to_all x1, starting transfers between devices, body(): lax.all_to_all(late_picked, 'node', split_axis=0, concat_axis=0, tiled=True)  7.61 us
  transfers between devices with their start and end apart: 2, of which 2 were waited for; matrix products, arithmetic and copies ran while one was open for 8% of the time, Pallas kernels for 15%

profile of v14, /device:TPU:2, one launch (start us, length us, event | category | flops | bytes accessed | tf_op | source)
XLA Modules:
  0.0 252.1 jit_solution(5155420560534157245)
XLA Ops:
  0.6 0.7 fusion.6
  1.3 1.7 reshape.61
  3.0 0.1 pad_slice_fusion
  3.1 0.1 broadcast_in_dim.21
  3.2 0.1 pad_maximum_fusion
  3.2 4.0 %gather_fusion.1 = bf16[64,392,128]{2,1,0:T(8,128)(2,1)} fusion(bf16[9,392,128]{2,1,0:T(8,128)(2,1)S(1)} %pad_maximum_fusion, s32[1024]{0:T(1024)S(1)} %pad_clamp_fusion), kind=kCustom, calls=%fused_computation.1 | custom fusion | bytes 12845312 | tf_op jit(solution)/shard_map/jit(_take)/gather | solution.py:222
  7.3 0.0 slice-start
  7.3 11.1 %all-to-all-start = ((bf16[64,392,128]{2,1,0:T(8,128)(2,1)}), bf16[64,392,128]{2,1,0:T(8,128)(2,1)}, u32[]{:S(2)}, u32[]{:S(2)}) async-start(bf16[64,392,128]{2,1,0:T(8,128)(2,1)} %gather_fusion.1), calls=%async_computation | async-start | bytes 12845056 | tf_op jit(solution)/shard_map/all_to_all | solution.py:224
  18.4 0.0 slice-done
  18.4 0.0 copy-start.2
  18.4 0.0 copy-start.3
  18.5 2.0 gather_fusion
  20.5 0.0 copy-done.2
  20.5 0.4 copy.47
  20.9 0.5 copy.52
  21.3 0.0 copy-done.3
  21.4 2.8 %add_add_fusion = (s32[2,2048]{0,1:T(8,128)S(1)}, s32[2,2048]{0,1:T(8,128)S(1)}, s32[2,2048]{0,1:T(8,128)}) fusion(pred[2,2048]{0,1:T(8,128)(4,1)S(1)} %copy.52, s32[2,2048]{0,1:T(8,128)S(1)} %copy.47), kind=kLoop, calls=%fused_computation.18 | loop fusion | flops 172032 | bytes 69632 | tf_op jit(solution)/shard_map/sub | solution.py:231
  24.2 1.6 multiply_add_fusion
  25.7 135.1 %all-to-all-done = bf16[64,392,128]{2,1,0:T(8,128)(2,1)} async-done(((bf16[64,392,128]{2,1,0:T(8,128)(2,1)}), bf16[64,392,128]{2,1,0:T(8,128)(2,1)}, u32[]{:S(2)}, u32[]{:S(2)}) %all-to-all-start) | async-done | bytes 6422560 | tf_op jit(solution)/shard_map/all_to_all | solution.py:224
  160.8 7.6 %all-to-all-start.1 = ((bf16[64,32,512]{2,1,0:T(8,128)(2,1)}), bf16[64,32,512]{2,1,0:T(8,128)(2,1)}, u32[]{:S(2)}, u32[]{:S(2)}) async-start(bf16[64,32,512]{2,1,0:T(8,128)(2,1)} %gather_fusion), calls=%async_computation.1 | async-start | bytes 4194304 | tf_op jit(solution)/shard_map/all_to_all | solution.py:235
  168.4 0.3 copy.54
  168.8 0.0 copy-start
  168.8 1.7 copy.57
  170.4 2.1 convert_reduce_fusion
  172.6 0.4 fusion.3
  172.9 1.1 copy.58
  174.0 0.0 copy-done
  174.0 0.3 copy.59
  174.4 0.6 copy.62
  175.0 1.4 copy.61.pid_ref
  176.3 2.5 convert_bitcast_fusion.mask_ref
  178.8 0.0 copy-start.1
  178.8 37.3 %shard_map.86.part_ref = f32[2048,512]{1,0:T(8,128)} custom-call(s32[4096]{0:T(1024)} %bitcast.15, bf16[25088,128]{1,0:T(8,128)(2,1)} %bitcast.4.table, f32[2048,2]{1,0:T(8,128)} %convert_bitcast_fusion.mask_ref, bf16[1024,512]{1,0:T(8,128)(2,1)} %wb_ref.3, bf16[1024,512]{1,0:T(8,128)(2,1)} %wb_ref.3), custom_call_target="tpu_custom_call" | custom-call | flops 2147483648 | bytes 8388608 | tf_op jit(solution)/shard_map/pallas_call | solution.py:148
  216.2 0.0 copy-done.1
  216.2 0.0 copy-start.4
  216.2 1.6 select_bitcast_fusion.idx_ref
  217.8 1.8 all-to-all-done.1
  219.6 0.0 copy-done.4
  219.6 0.6 broadcast_in_dim.22.wo_ref
  220.2 29.4 %shard_map.87 = (f32[1,2048]{1,0:T(1,128)}, f32[128]{0:T(128)}) custom-call(s32[2048,2]{1,0:T(8,128)} %select_bitcast_fusion.idx_ref, f32[2048,512]{1,0:T(8,128)} %shard_map.86.part_ref, bf16[2048,512]{1,0:T(8,128)(2,1)} %bitcast.6.table_ref, bf16[1024,512]{1,0:T(8,128)(2,1)} %wb_ref.3, bf16[1024,512]{1,0:T(8,128)(2,1)} %wb_ref.3, f32[1,512]{1,0:T(1,128)} %bitcast.19, ...), custom_call_target="tpu_custom_call" | custom-call | flops 10737418240 | bytes 6291456 | tf_op jit(solution)/shard_map/pallas_call | solution.py:165
  249.6 1.3 copy.65
  250.9 1.2 copy.66
  (5 shorter events, 0.1 us)
Async XLA Ops:
  7.3 11.1 %slice-start = ((bf16[8,128,512]{2,1,0:T(8,128)(2,1)}), bf16[8,32,512]{2,1,0:T(8,128)(2,1)S(1)}, s32[]{:S(2)}) async-start(bf16[8,128,512]{2,1,0:T(8,128)(2,1)} %param.7), calls=%async_computation.2 | async-start | bytes 524288 | tf_op jit(solution)/shard_map/slice | solution.py:221
  7.3 153.6 %all-to-all-start = ((bf16[64,392,128]{2,1,0:T(8,128)(2,1)}), bf16[64,392,128]{2,1,0:T(8,128)(2,1)}, u32[]{:S(2)}, u32[]{:S(2)}) async-start(bf16[64,392,128]{2,1,0:T(8,128)(2,1)} %gather_fusion.1), calls=%async_computation | async-start | bytes 12845056 | tf_op jit(solution)/shard_map/all_to_all | solution.py:224
  18.4 2.0 copy-start.2
  18.4 2.9 %copy-start.3 = (s32[2048]{0:T(1024)S(1)}, s32[2048]{0:T(1024)}, u32[]{:S(2)}) copy-start(s32[2048]{0:T(1024)} %param.10) | copy-start | bytes 24580
  160.8 58.8 %all-to-all-start.1 = ((bf16[64,32,512]{2,1,0:T(8,128)(2,1)}), bf16[64,32,512]{2,1,0:T(8,128)(2,1)}, u32[]{:S(2)}, u32[]{:S(2)}) async-start(bf16[64,32,512]{2,1,0:T(8,128)(2,1)} %gather_fusion), calls=%async_computation.1 | async-start | bytes 4194304 | tf_op jit(solution)/shard_map/all_to_all | solution.py:235
  168.8 5.3 %copy-start = (s32[2,2048]{0,1:T(8,128)S(1)}, s32[2,2048]{0,1:T(8,128)}, u32[]{:S(2)}) copy-start(s32[2,2048]{0,1:T(8,128)} %multiply_add_fusion) | copy-start | bytes 49156
  178.8 37.3 %copy-start.1 = (pred[2,2048]{0,1:T(8,128)(4,1)S(1)}, pred[2,2048]{0,1:T(8,128)(4,1)}, u32[]{:S(2)}) copy-start(pred[2,2048]{0,1:T(8,128)(4,1)} %copy.58) | copy-start | bytes 12292
  216.2 3.5 %copy-start.4 = (bf16[512]{0:T(512)(128)(2,1)S(1)}, bf16[512]{0:T(512)(128)(2,1)}, u32[]{:S(2)}) copy-start(bf16[512]{0:T(512)(128)(2,1)} %param.13) | copy-start | bytes 3076

commit v15 on v14

--- a/solution.py
+++ b/solution.py
@@ -9,7 +9,7 @@
 
 PAIRS_ROW = 1024
 TILE = 256
-LATE_TILE = 512
+LATE_TILE = 1024
 EARLY_ROWS = 96
 
 

time: 253 us -> 253 us (level)
  no operation moved by 1% of the time
where the time goes in v15:
time: 253 us; the launch traced here: 252 us
  waiting for transfers between devices  137 us (54%)
  Pallas kernels  66.8 us (26%)
  starting transfers between devices  18.7 us (7%)
  local copies, waits for them, and re-layouts  17.2 us (7%)
  other arithmetic  11.7 us (5%)
    all_to_all x1, waiting for transfers between devices, body(): lax.all_to_all(early_picked, 'node', split_axis=0, concat_axis=0, tiled=T...  135 us
    pallas_call x1, Pallas kernels, early_products(): pl.pallas_call(functools.partial(early_kernel, edges), grid_spec=grid_spe...  37.3 us
    pallas_call x1, Pallas kernels, late_scores(): pl.pallas_call(late_kernel, grid=(edges // LATE_TILE,), in_specs=[pl.Bloc...  29.5 us
    all_to_all x1, starting transfers between devices, body(): lax.all_to_all(early_picked, 'node', split_axis=0, concat_axis=0, tiled=T...  11.1 us
    all_to_all x1, starting transfers between devices, body(): lax.all_to_all(late_picked, 'node', split_axis=0, concat_axis=0, tiled=True)  7.61 us
  transfers between devices with their start and end apart: 2, of which 2 were waited for; matrix products, arithmetic and copies ran while one was open for 8% of the time, Pallas kernels for 15%

profile of v15, /device:TPU:2, one launch (start us, length us, event | category | flops | bytes accessed | tf_op | source)
XLA Modules:
  0.0 252.2 jit_solution(16577660455997673049)
XLA Ops:
  0.6 0.7 fusion.6
  1.3 1.7 reshape.61
  3.0 0.1 pad_slice_fusion
  3.1 0.1 broadcast_in_dim.21
  3.2 0.1 pad_maximum_fusion
  3.2 4.0 %gather_fusion.1 = bf16[64,392,128]{2,1,0:T(8,128)(2,1)} fusion(bf16[9,392,128]{2,1,0:T(8,128)(2,1)S(1)} %pad_maximum_fusion, s32[1024]{0:T(1024)S(1)} %pad_clamp_fusion), kind=kCustom, calls=%fused_computation.1 | custom fusion | bytes 12845312 | tf_op jit(solution)/shard_map/jit(_take)/gather | solution.py:222
  7.3 0.0 slice-start
  7.3 11.1 %all-to-all-start = ((bf16[64,392,128]{2,1,0:T(8,128)(2,1)}), bf16[64,392,128]{2,1,0:T(8,128)(2,1)}, u32[]{:S(2)}, u32[]{:S(2)}) async-start(bf16[64,392,128]{2,1,0:T(8,128)(2,1)} %gather_fusion.1), calls=%async_computation | async-start | bytes 12845056 | tf_op jit(solution)/shard_map/all_to_all | solution.py:224
  18.4 0.0 slice-done
  18.4 0.0 copy-start.2
  18.4 0.0 copy-start.3
  18.5 2.0 gather_fusion
  20.5 0.0 copy-done.2
  20.5 0.4 copy.47
  20.9 0.5 copy.52
  21.3 0.0 copy-done.3
  21.4 2.8 %add_add_fusion = (s32[2,2048]{0,1:T(8,128)S(1)}, s32[2,2048]{0,1:T(8,128)S(1)}, s32[2,2048]{0,1:T(8,128)}) fusion(pred[2,2048]{0,1:T(8,128)(4,1)S(1)} %copy.52, s32[2,2048]{0,1:T(8,128)S(1)} %copy.47), kind=kLoop, calls=%fused_computation.18 | loop fusion | flops 172032 | bytes 69632 | tf_op jit(solution)/shard_map/sub | solution.py:231
  24.2 1.6 multiply_add_fusion
  25.7 135.1 %all-to-all-done = bf16[64,392,128]{2,1,0:T(8,128)(2,1)} async-done(((bf16[64,392,128]{2,1,0:T(8,128)(2,1)}), bf16[64,392,128]{2,1,0:T(8,128)(2,1)}, u32[]{:S(2)}, u32[]{:S(2)}) %all-to-all-start) | async-done | bytes 6422560 | tf_op jit(solution)/shard_map/all_to_all | solution.py:224
  160.8 7.6 %all-to-all-start.1 = ((bf16[64,32,512]{2,1,0:T(8,128)(2,1)}), bf16[64,32,512]{2,1,0:T(8,128)(2,1)}, u32[]{:S(2)}, u32[]{:S(2)}) async-start(bf16[64,32,512]{2,1,0:T(8,128)(2,1)} %gather_fusion), calls=%async_computation.1 | async-start | bytes 4194304 | tf_op jit(solution)/shard_map/all_to_all | solution.py:235
  168.4 0.3 copy.54
  168.8 0.0 copy-start
  168.8 1.7 copy.57
  170.4 2.1 convert_reduce_fusion
  172.6 0.4 fusion.3
  172.9 1.1 copy.58
  174.0 0.0 copy-done
  174.0 0.3 copy.59
  174.4 0.6 copy.62
  175.0 1.4 copy.61.pid_ref
  176.3 2.5 convert_bitcast_fusion.mask_ref
  178.8 0.0 copy-start.1
  178.8 37.3 %shard_map.86.part_ref = f32[2048,512]{1,0:T(8,128)} custom-call(s32[4096]{0:T(1024)} %bitcast.15, bf16[25088,128]{1,0:T(8,128)(2,1)} %bitcast.4.table, f32[2048,2]{1,0:T(8,128)} %convert_bitcast_fusion.mask_ref, bf16[1024,512]{1,0:T(8,128)(2,1)} %wb_ref.3, bf16[1024,512]{1,0:T(8,128)(2,1)} %wb_ref.3), custom_call_target="tpu_custom_call" | custom-call | flops 2147483648 | bytes 8388608 | tf_op jit(solution)/shard_map/pallas_call | solution.py:148
  216.1 0.0 copy-done.1
  216.2 0.0 copy-start.4
  216.2 1.6 select_bitcast_fusion.idx_ref
  217.8 1.8 all-to-all-done.1
  219.6 0.0 copy-done.4
  219.6 0.6 broadcast_in_dim.22.wo_ref
  220.2 29.5 %shard_map.87 = (f32[1,2048]{1,0:T(1,128)}, f32[128]{0:T(128)}) custom-call(s32[2048,2]{1,0:T(8,128)} %select_bitcast_fusion.idx_ref, f32[2048,512]{1,0:T(8,128)} %shard_map.86.part_ref, bf16[2048,512]{1,0:T(8,128)(2,1)} %bitcast.6.table_ref, bf16[1024,512]{1,0:T(8,128)(2,1)} %wb_ref.3, bf16[1024,512]{1,0:T(8,128)(2,1)} %wb_ref.3, f32[1,512]{1,0:T(1,128)} %bitcast.19, ...), custom_call_target="tpu_custom_call" | custom-call | flops 10737418240 | bytes 6291456 | tf_op jit(solution)/shard_map/pallas_call | solution.py:165
  249.7 1.3 copy.65
  251.0 1.2 copy.66
  (5 shorter events, 0.1 us)
Async XLA Ops:
  7.3 11.1 %slice-start = ((bf16[8,128,512]{2,1,0:T(8,128)(2,1)}), bf16[8,32,512]{2,1,0:T(8,128)(2,1)S(1)}, s32[]{:S(2)}) async-start(bf16[8,128,512]{2,1,0:T(8,128)(2,1)} %param.7), calls=%async_computation.2 | async-start | bytes 524288 | tf_op jit(solution)/shard_map/slice | solution.py:221
  7.3 153.6 %all-to-all-start = ((bf16[64,392,128]{2,1,0:T(8,128)(2,1)}), bf16[64,392,128]{2,1,0:T(8,128)(2,1)}, u32[]{:S(2)}, u32[]{:S(2)}) async-start(bf16[64,392,128]{2,1,0:T(8,128)(2,1)} %gather_fusion.1), calls=%async_computation | async-start | bytes 12845056 | tf_op jit(solution)/shard_map/all_to_all | solution.py:224
  18.4 2.0 copy-start.2
  18.4 2.9 %copy-start.3 = (s32[2048]{0:T(1024)S(1)}, s32[2048]{0:T(1024)}, u32[]{:S(2)}) copy-start(s32[2048]{0:T(1024)} %param.10) | copy-start | bytes 24580
  160.8 58.8 %all-to-all-start.1 = ((bf16[64,32,512]{2,1,0:T(8,128)(2,1)}), bf16[64,32,512]{2,1,0:T(8,128)(2,1)}, u32[]{:S(2)}, u32[]{:S(2)}) async-start(bf16[64,32,512]{2,1,0:T(8,128)(2,1)} %gather_fusion), calls=%async_computation.1 | async-start | bytes 4194304 | tf_op jit(solution)/shard_map/all_to_all | solution.py:235
  168.8 5.3 %copy-start = (s32[2,2048]{0,1:T(8,128)S(1)}, s32[2,2048]{0,1:T(8,128)}, u32[]{:S(2)}) copy-start(s32[2,2048]{0,1:T(8,128)} %multiply_add_fusion) | copy-start | bytes 49156
  178.8 37.3 %copy-start.1 = (pred[2,2048]{0,1:T(8,128)(4,1)S(1)}, pred[2,2048]{0,1:T(8,128)(4,1)}, u32[]{:S(2)}) copy-start(pred[2,2048]{0,1:T(8,128)(4,1)} %copy.58) | copy-start | bytes 12292
  216.2 3.5 %copy-start.4 = (bf16[512]{0:T(512)(128)(2,1)S(1)}, bf16[512]{0:T(512)(128)(2,1)}, u32[]{:S(2)}) copy-start(bf16[512]{0:T(512)(128)(2,1)} %param.13) | copy-start | bytes 3076

commit v16 on v14

--- a/solution.py
+++ b/solution.py
@@ -8,7 +8,7 @@
 from jax.sharding import PartitionSpec as P
 
 PAIRS_ROW = 1024
-TILE = 256
+TILE = 512
 LATE_TILE = 512
 EARLY_ROWS = 96
 

time: 253 us -> 253 us (level)
  transfers between devices with their start and end apart: 2 -> 2, of which waited for: 2 -> 2; matrix products, arithmetic and copies ran while one was open for 8% -> 8% of each run, Pallas kernels for 15% -> 14%
where the time goes in v16:
time: 253 us; the launch traced here: 252 us
  waiting for transfers between devices  138 us (55%)
  Pallas kernels  65.5 us (26%)
  starting transfers between devices  18.7 us (7%)
  local copies, waits for them, and re-layouts  17.2 us (7%)
  other arithmetic  11.7 us (5%)
    all_to_all x1, waiting for transfers between devices, body(): lax.all_to_all(early_picked, 'node', split_axis=0, concat_axis=0, tiled=T...  135 us
    pallas_call x1, Pallas kernels, early_products(): pl.pallas_call(functools.partial(early_kernel, edges), grid_spec=grid_spe...  36.2 us
    pallas_call x1, Pallas kernels, late_scores(): pl.pallas_call(late_kernel, grid=(edges // LATE_TILE,), in_specs=[pl.Bloc...  29.4 us
    all_to_all x1, starting transfers between devices, body(): lax.all_to_all(early_picked, 'node', split_axis=0, concat_axis=0, tiled=T...  11.1 us
    all_to_all x1, starting transfers between devices, body(): lax.all_to_all(late_picked, 'node', split_axis=0, concat_axis=0, tiled=True)  7.61 us
  transfers between devices with their start and end apart: 2, of which 2 were waited for; matrix products, arithmetic and copies ran while one was open for 8% of the time, Pallas kernels for 14%

profile of v16, /device:TPU:2, one launch (start us, length us, event | category | flops | bytes accessed | tf_op | source)
XLA Modules:
  0.0 252.1 jit_solution(5570126146003510621)
XLA Ops:
  0.6 0.7 fusion.6
  1.3 1.7 reshape.61
  3.0 0.1 pad_slice_fusion
  3.1 0.1 broadcast_in_dim.21
  3.2 0.1 pad_maximum_fusion
  3.2 4.0 %gather_fusion.1 = bf16[64,392,128]{2,1,0:T(8,128)(2,1)} fusion(bf16[9,392,128]{2,1,0:T(8,128)(2,1)S(1)} %pad_maximum_fusion, s32[1024]{0:T(1024)S(1)} %pad_clamp_fusion), kind=kCustom, calls=%fused_computation.1 | custom fusion | bytes 12845312 | tf_op jit(solution)/shard_map/jit(_take)/gather | solution.py:222
  7.3 0.0 slice-start
  7.3 11.1 %all-to-all-start = ((bf16[64,392,128]{2,1,0:T(8,128)(2,1)}), bf16[64,392,128]{2,1,0:T(8,128)(2,1)}, u32[]{:S(2)}, u32[]{:S(2)}) async-start(bf16[64,392,128]{2,1,0:T(8,128)(2,1)} %gather_fusion.1), calls=%async_computation | async-start | bytes 12845056 | tf_op jit(solution)/shard_map/all_to_all | solution.py:224
  18.4 0.0 slice-done
  18.4 0.0 copy-start.2
  18.4 0.0 copy-start.3
  18.5 2.0 gather_fusion
  20.5 0.0 copy-done.2
  20.5 0.4 copy.47
  20.9 0.5 copy.52
  21.3 0.0 copy-done.3
  21.4 2.8 %add_add_fusion = (s32[2,2048]{0,1:T(8,128)S(1)}, s32[2,2048]{0,1:T(8,128)S(1)}, s32[2,2048]{0,1:T(8,128)}) fusion(pred[2,2048]{0,1:T(8,128)(4,1)S(1)} %copy.52, s32[2,2048]{0,1:T(8,128)S(1)} %copy.47), kind=kLoop, calls=%fused_computation.18 | loop fusion | flops 172032 | bytes 69632 | tf_op jit(solution)/shard_map/sub | solution.py:231
  24.2 1.6 multiply_add_fusion
  25.7 135.1 %all-to-all-done = bf16[64,392,128]{2,1,0:T(8,128)(2,1)} async-done(((bf16[64,392,128]{2,1,0:T(8,128)(2,1)}), bf16[64,392,128]{2,1,0:T(8,128)(2,1)}, u32[]{:S(2)}, u32[]{:S(2)}) %all-to-all-start) | async-done | bytes 6422560 | tf_op jit(solution)/shard_map/all_to_all | solution.py:224
  160.8 7.6 %all-to-all-start.1 = ((bf16[64,32,512]{2,1,0:T(8,128)(2,1)}), bf16[64,32,512]{2,1,0:T(8,128)(2,1)}, u32[]{:S(2)}, u32[]{:S(2)}) async-start(bf16[64,32,512]{2,1,0:T(8,128)(2,1)} %gather_fusion), calls=%async_computation.1 | async-start | bytes 4194304 | tf_op jit(solution)/shard_map/all_to_all | solution.py:235
  168.4 0.3 copy.54
  168.8 0.0 copy-start
  168.8 1.7 copy.57
  170.4 2.1 convert_reduce_fusion
  172.6 0.4 fusion.3
  172.9 1.1 copy.58
  174.0 0.0 copy-done
  174.0 0.3 copy.59
  174.4 0.6 copy.62
  175.0 1.4 copy.61.pid_ref
  176.3 2.5 convert_bitcast_fusion.mask_ref
  178.8 0.0 copy-start.1
  178.8 36.2 %shard_map.86.part_ref = f32[2048,512]{1,0:T(8,128)} custom-call(s32[4096]{0:T(1024)} %bitcast.15, bf16[25088,128]{1,0:T(8,128)(2,1)} %bitcast.4.table, f32[2048,2]{1,0:T(8,128)} %convert_bitcast_fusion.mask_ref, bf16[1024,512]{1,0:T(8,128)(2,1)} %wb_ref.3, bf16[1024,512]{1,0:T(8,128)(2,1)} %wb_ref.3), custom_call_target="tpu_custom_call" | custom-call | flops 2147483648 | bytes 8388608 | tf_op jit(solution)/shard_map/pallas_call | solution.py:148
  215.0 0.0 copy-done.1
  215.0 0.0 copy-start.4
  215.0 1.6 select_bitcast_fusion.idx_ref
  216.7 2.9 %all-to-all-done.1 = bf16[64,32,512]{2,1,0:T(8,128)(2,1)} async-done(((bf16[64,32,512]{2,1,0:T(8,128)(2,1)}), bf16[64,32,512]{2,1,0:T(8,128)(2,1)}, u32[]{:S(2)}, u32[]{:S(2)}) %all-to-all-start.1) | async-done | bytes 2097184 | tf_op jit(solution)/shard_map/all_to_all | solution.py:235
  219.6 0.0 copy-done.4
  219.6 0.6 broadcast_in_dim.22.wo_ref
  220.2 29.4 %shard_map.87 = (f32[1,2048]{1,0:T(1,128)}, f32[128]{0:T(128)}) custom-call(s32[2048,2]{1,0:T(8,128)} %select_bitcast_fusion.idx_ref, f32[2048,512]{1,0:T(8,128)} %shard_map.86.part_ref, bf16[2048,512]{1,0:T(8,128)(2,1)} %bitcast.6.table_ref, bf16[1024,512]{1,0:T(8,128)(2,1)} %wb_ref.3, bf16[1024,512]{1,0:T(8,128)(2,1)} %wb_ref.3, f32[1,512]{1,0:T(1,128)} %bitcast.19, ...), custom_call_target="tpu_custom_call" | custom-call | flops 10737418240 | bytes 6291456 | tf_op jit(solution)/shard_map/pallas_call | solution.py:165
  249.6 1.3 copy.65
  250.9 1.2 copy.66
  (5 shorter events, 0.1 us)
Async XLA Ops:
  7.3 11.1 %slice-start = ((bf16[8,128,512]{2,1,0:T(8,128)(2,1)}), bf16[8,32,512]{2,1,0:T(8,128)(2,1)S(1)}, s32[]{:S(2)}) async-start(bf16[8,128,512]{2,1,0:T(8,128)(2,1)} %param.7), calls=%async_computation.2 | async-start | bytes 524288 | tf_op jit(solution)/shard_map/slice | solution.py:221
  7.3 153.6 %all-to-all-start = ((bf16[64,392,128]{2,1,0:T(8,128)(2,1)}), bf16[64,392,128]{2,1,0:T(8,128)(2,1)}, u32[]{:S(2)}, u32[]{:S(2)}) async-start(bf16[64,392,128]{2,1,0:T(8,128)(2,1)} %gather_fusion.1), calls=%async_computation | async-start | bytes 12845056 | tf_op jit(solution)/shard_map/all_to_all | solution.py:224
  18.4 2.0 copy-start.2
  18.4 2.9 %copy-start.3 = (s32[2048]{0:T(1024)S(1)}, s32[2048]{0:T(1024)}, u32[]{:S(2)}) copy-start(s32[2048]{0:T(1024)} %param.10) | copy-start | bytes 24580
  160.8 58.8 %all-to-all-start.1 = ((bf16[64,32,512]{2,1,0:T(8,128)(2,1)}), bf16[64,32,512]{2,1,0:T(8,128)(2,1)}, u32[]{:S(2)}, u32[]{:S(2)}) async-start(bf16[64,32,512]{2,1,0:T(8,128)(2,1)} %gather_fusion), calls=%async_computation.1 | async-start | bytes 4194304 | tf_op jit(solution)/shard_map/all_to_all | solution.py:235
  168.8 5.3 %copy-start = (s32[2,2048]{0,1:T(8,128)S(1)}, s32[2,2048]{0,1:T(8,128)}, u32[]{:S(2)}) copy-start(s32[2,2048]{0,1:T(8,128)} %multiply_add_fusion) | copy-start | bytes 49156
  178.8 36.2 %copy-start.1 = (pred[2,2048]{0,1:T(8,128)(4,1)S(1)}, pred[2,2048]{0,1:T(8,128)(4,1)}, u32[]{:S(2)}) copy-start(pred[2,2048]{0,1:T(8,128)(4,1)} %copy.58) | copy-start | bytes 12292
  215.0 4.6 %copy-start.4 = (bf16[512]{0:T(512)(128)(2,1)S(1)}, bf16[512]{0:T(512)(128)(2,1)}, u32[]{:S(2)}) copy-start(bf16[512]{0:T(512)(128)(2,1)} %param.13) | copy-start | bytes 3076

commit v17 on v16

--- a/solution.py
+++ b/solution.py
@@ -212,12 +212,12 @@
     slot_len = early_len + 8
     wanted = send_list[0, 0]
     pick = jnp.where(wanted >= 0, wanted, blocks_here)
-    narrow = embedding.reshape(blocks_here, block_rows * parts, lanes)
-    narrow = jnp.concatenate([narrow, jnp.zeros((1, block_rows * parts, lanes), embedding.dtype)], axis=0)
+    narrow = embedding[:, :EARLY_ROWS].reshape(blocks_here, early_len, lanes)
+    narrow = jnp.concatenate([narrow, jnp.zeros((1, early_len, lanes), embedding.dtype)], axis=0)
     marks = jnp.arange(blocks_here + 1, dtype=jnp.int32)
     marks = jnp.where(marks < blocks_here, marks, -1).astype(embedding.dtype)
     marks = jnp.broadcast_to(marks[:, None, None], (blocks_here + 1, 8, lanes))
-    early_source = jnp.concatenate([narrow[:, :early_len], marks], axis=1)
+    early_source = jnp.concatenate([narrow, marks], axis=1)
     late_source = jnp.concatenate([embedding[:, EARLY_ROWS:], jnp.zeros((1, late_rows, feature_width), embedding.dtype)], axis=0)
     early_picked = jnp.take(early_source, pick, axis=0, mode="clip")
     late_picked = jnp.take(late_source, pick, axis=0, mode="clip")

time: 253 us -> 252 us (level)
  no operation moved by 1% of the time
where the time goes in v17:
time: 252 us; the launch traced here: 251 us
  waiting for transfers between devices  138 us (55%)
  Pallas kernels  65.5 us (26%)
  starting transfers between devices  18.7 us (7%)
  local copies, waits for them, and re-layouts  16.4 us (7%)
  other arithmetic  11.8 us (5%)
    all_to_all x1, waiting for transfers between devices, body(): lax.all_to_all(early_picked, 'node', split_axis=0, concat_axis=0, tiled=T...  135 us
    pallas_call x1, Pallas kernels, early_products(): pl.pallas_call(functools.partial(early_kernel, edges), grid_spec=grid_spe...  36.2 us
    pallas_call x1, Pallas kernels, late_scores(): pl.pallas_call(late_kernel, grid=(edges // LATE_TILE,), in_specs=[pl.Bloc...  29.4 us
    all_to_all x1, starting transfers between devices, body(): lax.all_to_all(early_picked, 'node', split_axis=0, concat_axis=0, tiled=T...  11.1 us
    all_to_all x1, starting transfers between devices, body(): lax.all_to_all(late_picked, 'node', split_axis=0, concat_axis=0, tiled=True)  7.61 us
  transfers between devices with their start and end apart: 2, of which 2 were waited for; matrix products, arithmetic and copies ran while one was open for 8% of the time, Pallas kernels for 14%

profile of v17, /device:TPU:2, one launch (start us, length us, event | category | flops | bytes accessed | tf_op | source)
XLA Modules:
  0.0 251.2 jit_solution(6769982768243729550)
XLA Ops:
  0.6 0.0 slice-start
  0.7 0.7 fusion.8
  1.4 0.4 slice-done
  1.8 0.5 reshape.61
  2.3 0.1 broadcast_in_dim.21
  2.3 0.1 fusion.6
  2.4 4.0 %gather_fusion.1 = bf16[64,392,128]{2,1,0:T(8,128)(2,1)} fusion(bf16[9,392,128]{2,1,0:T(8,128)(2,1)S(1)} %fusion.6, s32[1024]{0:T(1024)S(1)} %pad_clamp_fusion), kind=kCustom, calls=%fused_computation.1 | custom fusion | bytes 12845312 | tf_op jit(solution)/shard_map/jit(_take)/gather | solution.py:222
  6.4 0.0 slice-start.1
  6.4 11.1 %all-to-all-start = ((bf16[64,392,128]{2,1,0:T(8,128)(2,1)}), bf16[64,392,128]{2,1,0:T(8,128)(2,1)}, u32[]{:S(2)}, u32[]{:S(2)}) async-start(bf16[64,392,128]{2,1,0:T(8,128)(2,1)} %gather_fusion.1), calls=%async_computation | async-start | bytes 12845056 | tf_op jit(solution)/shard_map/all_to_all | solution.py:224
  17.6 0.0 slice-done.1
  17.6 0.0 copy-start.2
  17.6 0.0 copy-start.3
  17.6 2.0 gather_fusion
  19.6 0.0 copy-done.2
  19.6 0.4 copy.47
  20.0 0.5 copy.52
  20.5 0.0 copy-done.3
  20.5 2.8 %add_add_fusion = (s32[2,2048]{0,1:T(8,128)S(1)}, s32[2,2048]{0,1:T(8,128)S(1)}, s32[2,2048]{0,1:T(8,128)}) fusion(pred[2,2048]{0,1:T(8,128)(4,1)S(1)} %copy.52, s32[2,2048]{0,1:T(8,128)S(1)} %copy.47), kind=kLoop, calls=%fused_computation.19 | loop fusion | flops 172032 | bytes 69632 | tf_op jit(solution)/shard_map/sub | solution.py:231
  23.3 1.6 multiply_add_fusion
  24.9 135.1 %all-to-all-done = bf16[64,392,128]{2,1,0:T(8,128)(2,1)} async-done(((bf16[64,392,128]{2,1,0:T(8,128)(2,1)}), bf16[64,392,128]{2,1,0:T(8,128)(2,1)}, u32[]{:S(2)}, u32[]{:S(2)}) %all-to-all-start) | async-done | bytes 6422560 | tf_op jit(solution)/shard_map/all_to_all | solution.py:224
  160.0 7.6 %all-to-all-start.1 = ((bf16[64,32,512]{2,1,0:T(8,128)(2,1)}), bf16[64,32,512]{2,1,0:T(8,128)(2,1)}, u32[]{:S(2)}, u32[]{:S(2)}) async-start(bf16[64,32,512]{2,1,0:T(8,128)(2,1)} %gather_fusion), calls=%async_computation.1 | async-start | bytes 4194304 | tf_op jit(solution)/shard_map/all_to_all | solution.py:235
  167.6 0.3 copy.54
  167.9 0.0 copy-start
  168.0 1.7 copy.57
  169.6 2.1 convert_reduce_fusion
  171.7 0.4 fusion.4
  172.1 1.1 copy.58
  173.2 0.0 copy-done
  173.2 0.3 copy.59
  173.5 0.6 copy.62
  174.2 1.4 copy.61.pid_ref
  175.5 2.5 convert_bitcast_fusion.mask_ref
  178.0 0.0 copy-start.1
  178.0 36.2 %shard_map.86.part_ref = f32[2048,512]{1,0:T(8,128)} custom-call(s32[4096]{0:T(1024)} %bitcast.15, bf16[25088,128]{1,0:T(8,128)(2,1)} %bitcast.4.table, f32[2048,2]{1,0:T(8,128)} %convert_bitcast_fusion.mask_ref, bf16[1024,512]{1,0:T(8,128)(2,1)} %wb_ref.3, bf16[1024,512]{1,0:T(8,128)(2,1)} %wb_ref.3), custom_call_target="tpu_custom_call" | custom-call | flops 2147483648 | bytes 8388608 | tf_op jit(solution)/shard_map/pallas_call | solution.py:148
  214.2 0.0 copy-done.1
  214.2 0.0 copy-start.4
  214.3 1.6 select_bitcast_fusion.idx_ref
  215.9 2.9 %all-to-all-done.1 = bf16[64,32,512]{2,1,0:T(8,128)(2,1)} async-done(((bf16[64,32,512]{2,1,0:T(8,128)(2,1)}), bf16[64,32,512]{2,1,0:T(8,128)(2,1)}, u32[]{:S(2)}, u32[]{:S(2)}) %all-to-all-start.1) | async-done | bytes 2097184 | tf_op jit(solution)/shard_map/all_to_all | solution.py:235
  218.8 0.0 copy-done.4
  218.8 0.6 broadcast_in_dim.22.wo_ref
  219.4 29.4 %shard_map.87 = (f32[1,2048]{1,0:T(1,128)}, f32[128]{0:T(128)}) custom-call(s32[2048,2]{1,0:T(8,128)} %select_bitcast_fusion.idx_ref, f32[2048,512]{1,0:T(8,128)} %shard_map.86.part_ref, bf16[2048,512]{1,0:T(8,128)(2,1)} %bitcast.6.table_ref, bf16[1024,512]{1,0:T(8,128)(2,1)} %wb_ref.3, bf16[1024,512]{1,0:T(8,128)(2,1)} %wb_ref.3, f32[1,512]{1,0:T(1,128)} %bitcast.19, ...), custom_call_target="tpu_custom_call" | custom-call | flops 10737418240 | bytes 6291456 | tf_op jit(solution)/shard_map/pallas_call | solution.py:165
  248.8 1.3 copy.65
  250.0 1.2 copy.66
  (5 shorter events, 0.1 us)
Async XLA Ops:
  0.6 1.2 slice-start
  6.4 11.1 %slice-start.1 = ((bf16[8,128,512]{2,1,0:T(8,128)(2,1)}), bf16[8,32,512]{2,1,0:T(8,128)(2,1)S(1)}, s32[]{:S(2)}) async-start(bf16[8,128,512]{2,1,0:T(8,128)(2,1)} %param.7), calls=%async_computation.3 | async-start | bytes 524288 | tf_op jit(solution)/shard_map/slice | solution.py:221
  6.4 153.6 %all-to-all-start = ((bf16[64,392,128]{2,1,0:T(8,128)(2,1)}), bf16[64,392,128]{2,1,0:T(8,128)(2,1)}, u32[]{:S(2)}, u32[]{:S(2)}) async-start(bf16[64,392,128]{2,1,0:T(8,128)(2,1)} %gather_fusion.1), calls=%async_computation | async-start | bytes 12845056 | tf_op jit(solution)/shard_map/all_to_all | solution.py:224
  17.6 2.0 copy-start.2
  17.6 2.9 %copy-start.3 = (s32[2048]{0:T(1024)S(1)}, s32[2048]{0:T(1024)}, u32[]{:S(2)}) copy-start(s32[2048]{0:T(1024)} %param.10) | copy-start | bytes 24580
  160.0 58.8 %all-to-all-start.1 = ((bf16[64,32,512]{2,1,0:T(8,128)(2,1)}), bf16[64,32,512]{2,1,0:T(8,128)(2,1)}, u32[]{:S(2)}, u32[]{:S(2)}) async-start(bf16[64,32,512]{2,1,0:T(8,128)(2,1)} %gather_fusion), calls=%async_computation.1 | async-start | bytes 4194304 | tf_op jit(solution)/shard_map/all_to_all | solution.py:235
  167.9 5.3 %copy-start = (s32[2,2048]{0,1:T(8,128)S(1)}, s32[2,2048]{0,1:T(8,128)}, u32[]{:S(2)}) copy-start(s32[2,2048]{0,1:T(8,128)} %multiply_add_fusion) | copy-start | bytes 49156
  178.0 36.2 %copy-start.1 = (pred[2,2048]{0,1:T(8,128)(4,1)S(1)}, pred[2,2048]{0,1:T(8,128)(4,1)}, u32[]{:S(2)}) copy-start(pred[2,2048]{0,1:T(8,128)(4,1)} %copy.58) | copy-start | bytes 12292
  214.2 4.5 %copy-start.4 = (bf16[512]{0:T(512)(128)(2,1)S(1)}, bf16[512]{0:T(512)(128)(2,1)}, u32[]{:S(2)}) copy-start(bf16[512]{0:T(512)(128)(2,1)} %param.13) | copy-start | bytes 3076

commit v18 on v17

--- a/solution.py
+++ b/solution.py
@@ -211,14 +211,13 @@
     late_rows = block_rows - EARLY_ROWS
     slot_len = early_len + 8
     wanted = send_list[0, 0]
-    pick = jnp.where(wanted >= 0, wanted, blocks_here)
+    pick = wanted + 1
     narrow = embedding[:, :EARLY_ROWS].reshape(blocks_here, early_len, lanes)
-    narrow = jnp.concatenate([narrow, jnp.zeros((1, early_len, lanes), embedding.dtype)], axis=0)
-    marks = jnp.arange(blocks_here + 1, dtype=jnp.int32)
-    marks = jnp.where(marks < blocks_here, marks, -1).astype(embedding.dtype)
+    narrow = jnp.concatenate([jnp.zeros((1, early_len, lanes), embedding.dtype), narrow], axis=0)
+    marks = (jnp.arange(blocks_here + 1, dtype=jnp.int32) - 1).astype(embedding.dtype)
     marks = jnp.broadcast_to(marks[:, None, None], (blocks_here + 1, 8, lanes))
     early_source = jnp.concatenate([narrow, marks], axis=1)
-    late_source = jnp.concatenate([embedding[:, EARLY_ROWS:], jnp.zeros((1, late_rows, feature_width), embedding.dtype)], axis=0)
+    late_source = jnp.concatenate([jnp.zeros((1, late_rows, feature_width), embedding.dtype), embedding[:, EARLY_ROWS:]], axis=0)
     early_picked = jnp.take(early_source, pick, axis=0, mode="clip")
     late_picked = jnp.take(late_source, pick, axis=0, mode="clip")
     early_arrived = lax.all_to_all(early_picked, "node", split_axis=0, concat_axis=0, tiled=True)

time: 252 us -> 252 us (level)
  no operation moved by 1% of the time
where the time goes in v18:
time: 252 us; the launch traced here: 251 us
  waiting for transfers between devices  138 us (55%)
  Pallas kernels  65.5 us (26%)
  starting transfers between devices  18.7 us (7%)
  local copies, waits for them, and re-layouts  16.4 us (7%)
  other arithmetic  11.8 us (5%)
    all_to_all x1, waiting for transfers between devices, body(): lax.all_to_all(early_picked, 'node', split_axis=0, concat_axis=0, tiled=T...  135 us
    pallas_call x1, Pallas kernels, early_products(): pl.pallas_call(functools.partial(early_kernel, edges), grid_spec=grid_spe...  36.2 us
    pallas_call x1, Pallas kernels, late_scores(): pl.pallas_call(late_kernel, grid=(edges // LATE_TILE,), in_specs=[pl.Bloc...  29.3 us
    all_to_all x1, starting transfers between devices, body(): lax.all_to_all(early_picked, 'node', split_axis=0, concat_axis=0, tiled=T...  11.1 us
    all_to_all x1, starting transfers between devices, body(): lax.all_to_all(late_picked, 'node', split_axis=0, concat_axis=0, tiled=True)  7.61 us
  transfers between devices with their start and end apart: 2, of which 2 were waited for; matrix products, arithmetic and copies ran while one was open for 8% of the time, Pallas kernels for 14%

profile of v18, /device:TPU:2, one launch (start us, length us, event | category | flops | bytes accessed | tf_op | source)
XLA Modules:
  0.0 251.2 jit_solution(14178160187109737233)
XLA Ops:
  0.6 0.0 slice-start
  0.7 0.7 add_bitcast_fusion
  1.4 0.4 slice-done
  1.8 0.5 reshape.52
  2.3 0.1 broadcast_in_dim.10
  2.3 0.1 fusion.6
  2.4 4.0 %gather_fusion.1 = bf16[64,392,128]{2,1,0:T(8,128)(2,1)} fusion(bf16[9,392,128]{2,1,0:T(8,128)(2,1)S(1)} %fusion.6, s32[1024]{0:T(1024)S(1)} %pad_clamp_fusion), kind=kCustom, calls=%fused_computation.1 | custom fusion | bytes 12845312 | tf_op jit(solution)/shard_map/jit(_take)/gather | solution.py:221
  6.4 0.0 slice-start.1
  6.4 11.1 %all-to-all-start = ((bf16[64,392,128]{2,1,0:T(8,128)(2,1)}), bf16[64,392,128]{2,1,0:T(8,128)(2,1)}, u32[]{:S(2)}, u32[]{:S(2)}) async-start(bf16[64,392,128]{2,1,0:T(8,128)(2,1)} %gather_fusion.1), calls=%async_computation | async-start | bytes 12845056 | tf_op jit(solution)/shard_map/all_to_all | solution.py:223
  17.6 0.0 slice-done.1
  17.6 0.0 copy-start.2
  17.6 0.0 copy-start.3
  17.6 2.0 gather_fusion
  19.6 0.0 copy-done.2
  19.6 0.4 copy.47
  20.0 0.5 copy.52
  20.5 0.0 copy-done.3
  20.5 2.8 %add_add_fusion = (s32[2,2048]{0,1:T(8,128)S(1)}, s32[2,2048]{0,1:T(8,128)S(1)}, s32[2,2048]{0,1:T(8,128)}) fusion(pred[2,2048]{0,1:T(8,128)(4,1)S(1)} %copy.52, s32[2,2048]{0,1:T(8,128)S(1)} %copy.47), kind=kLoop, calls=%fused_computation.19 | loop fusion | flops 172032 | bytes 69632 | tf_op jit(solution)/shard_map/sub | solution.py:230
  23.3 1.6 multiply_add_fusion
  24.9 135.1 %all-to-all-done = bf16[64,392,128]{2,1,0:T(8,128)(2,1)} async-done(((bf16[64,392,128]{2,1,0:T(8,128)(2,1)}), bf16[64,392,128]{2,1,0:T(8,128)(2,1)}, u32[]{:S(2)}, u32[]{:S(2)}) %all-to-all-start) | async-done | bytes 6422560 | tf_op jit(solution)/shard_map/all_to_all | solution.py:223
  160.0 7.6 %all-to-all-start.1 = ((bf16[64,32,512]{2,1,0:T(8,128)(2,1)}), bf16[64,32,512]{2,1,0:T(8,128)(2,1)}, u32[]{:S(2)}, u32[]{:S(2)}) async-start(bf16[64,32,512]{2,1,0:T(8,128)(2,1)} %gather_fusion), calls=%async_computation.1 | async-start | bytes 4194304 | tf_op jit(solution)/shard_map/all_to_all | solution.py:234
  167.6 0.3 copy.54
  168.0 0.0 copy-start
  168.0 1.7 copy.57
  169.6 2.1 convert_reduce_fusion
  171.7 0.4 fusion.4
  172.1 1.1 copy.58
  173.2 0.0 copy-done
  173.2 0.3 copy.59
  173.5 0.6 copy.62
  174.2 1.4 copy.61.pid_ref
  175.5 2.5 convert_bitcast_fusion.mask_ref
  178.0 0.0 copy-start.1
  178.0 36.2 %shard_map.86.part_ref = f32[2048,512]{1,0:T(8,128)} custom-call(s32[4096]{0:T(1024)} %bitcast.13, bf16[25088,128]{1,0:T(8,128)(2,1)} %bitcast.3.table, f32[2048,2]{1,0:T(8,128)} %convert_bitcast_fusion.mask_ref, bf16[1024,512]{1,0:T(8,128)(2,1)} %wb_ref.3, bf16[1024,512]{1,0:T(8,128)(2,1)} %wb_ref.3), custom_call_target="tpu_custom_call" | custom-call | flops 2147483648 | bytes 8388608 | tf_op jit(solution)/shard_map/pallas_call | solution.py:148
  214.2 0.0 copy-done.1
  214.3 0.0 copy-start.4
  214.3 1.6 select_bitcast_fusion.idx_ref
  215.9 2.9 %all-to-all-done.1 = bf16[64,32,512]{2,1,0:T(8,128)(2,1)} async-done(((bf16[64,32,512]{2,1,0:T(8,128)(2,1)}), bf16[64,32,512]{2,1,0:T(8,128)(2,1)}, u32[]{:S(2)}, u32[]{:S(2)}) %all-to-all-start.1) | async-done | bytes 2097184 | tf_op jit(solution)/shard_map/all_to_all | solution.py:234
  218.8 0.0 copy-done.4
  218.8 0.6 broadcast_in_dim.12.wo_ref
  219.4 29.3 %shard_map.87 = (f32[1,2048]{1,0:T(1,128)}, f32[128]{0:T(128)}) custom-call(s32[2048,2]{1,0:T(8,128)} %select_bitcast_fusion.idx_ref, f32[2048,512]{1,0:T(8,128)} %shard_map.86.part_ref, bf16[2048,512]{1,0:T(8,128)(2,1)} %bitcast.5.table_ref, bf16[1024,512]{1,0:T(8,128)(2,1)} %wb_ref.3, bf16[1024,512]{1,0:T(8,128)(2,1)} %wb_ref.3, f32[1,512]{1,0:T(1,128)} %bitcast.17, ...), custom_call_target="tpu_custom_call" | custom-call | flops 10737418240 | bytes 6291456 | tf_op jit(solution)/shard_map/pallas_call | solution.py:165
  248.8 1.3 copy.65
  250.0 1.2 copy.66
  (5 shorter events, 0.1 us)
Async XLA Ops:
  0.6 1.2 slice-start
  6.4 11.1 %slice-start.1 = ((bf16[8,128,512]{2,1,0:T(8,128)(2,1)}), bf16[8,32,512]{2,1,0:T(8,128)(2,1)S(1)}, s32[]{:S(2)}) async-start(bf16[8,128,512]{2,1,0:T(8,128)(2,1)} %param.7), calls=%async_computation.3 | async-start | bytes 524288 | tf_op jit(solution)/shard_map/slice | solution.py:220
  6.4 153.6 %all-to-all-start = ((bf16[64,392,128]{2,1,0:T(8,128)(2,1)}), bf16[64,392,128]{2,1,0:T(8,128)(2,1)}, u32[]{:S(2)}, u32[]{:S(2)}) async-start(bf16[64,392,128]{2,1,0:T(8,128)(2,1)} %gather_fusion.1), calls=%async_computation | async-start | bytes 12845056 | tf_op jit(solution)/shard_map/all_to_all | solution.py:223
  17.6 2.0 copy-start.2
  17.6 2.9 %copy-start.3 = (s32[2048]{0:T(1024)S(1)}, s32[2048]{0:T(1024)}, u32[]{:S(2)}) copy-start(s32[2048]{0:T(1024)} %param.10) | copy-start | bytes 24580
  160.0 58.8 %all-to-all-start.1 = ((bf16[64,32,512]{2,1,0:T(8,128)(2,1)}), bf16[64,32,512]{2,1,0:T(8,128)(2,1)}, u32[]{:S(2)}, u32[]{:S(2)}) async-start(bf16[64,32,512]{2,1,0:T(8,128)(2,1)} %gather_fusion), calls=%async_computation.1 | async-start | bytes 4194304 | tf_op jit(solution)/shard_map/all_to_all | solution.py:234
  168.0 5.3 %copy-start = (s32[2,2048]{0,1:T(8,128)S(1)}, s32[2,2048]{0,1:T(8,128)}, u32[]{:S(2)}) copy-start(s32[2,2048]{0,1:T(8,128)} %multiply_add_fusion) | copy-start | bytes 49156
  178.0 36.2 %copy-start.1 = (pred[2,2048]{0,1:T(8,128)(4,1)S(1)}, pred[2,2048]{0,1:T(8,128)(4,1)}, u32[]{:S(2)}) copy-start(pred[2,2048]{0,1:T(8,128)(4,1)} %copy.58) | copy-start | bytes 12292
  214.3 4.5 %copy-start.4 = (bf16[512]{0:T(512)(128)(2,1)S(1)}, bf16[512]{0:T(512)(128)(2,1)}, u32[]{:S(2)}) copy-start(bf16[512]{0:T(512)(128)(2,1)} %param.13) | copy-start | bytes 3076

commit v19 on v18

--- a/solution.py
+++ b/solution.py
@@ -85,7 +85,7 @@
     slots = lax.broadcasted_iota(jnp.int32, (LATE_TILE, rows), 1)
     preact = part_ref[...]
     for end, w_ref in ((0, wt_ref), (1, wb_ref)):
-        onehot = (idx[:, end:end + 1] == slots).astype(table_ref.dtype)
+        onehot = jnp.where(idx[:, end:end + 1] == slots, jnp.ones((), table_ref.dtype), jnp.zeros((), table_ref.dtype))
         picked = jnp.dot(onehot, table_ref[...], preferred_element_type=jnp.float32).astype(table_ref.dtype)
         preact = preact + jnp.dot(picked, w_ref[...], preferred_element_type=jnp.float32)
     hidden = gelu_tanh(preact + bias_ref[...])

time: 252 us -> 252 us (level)
  the two profiles are of different devices: /device:TPU:2 before, /device:TPU:4 now
where the time goes in v19:
time: 252 us; the launch traced here: 251 us
  waiting for transfers between devices  140 us (56%)
  Pallas kernels  65.5 us (26%)
  starting transfers between devices  17 us (7%)
  local copies, waits for them, and re-layouts  16.4 us (7%)
  other arithmetic  11.8 us (5%)
    all_to_all x1, waiting for transfers between devices, body(): lax.all_to_all(early_picked, 'node', split_axis=0, concat_axis=0, tiled=T...  137 us
    pallas_call x1, Pallas kernels, early_products(): pl.pallas_call(functools.partial(early_kernel, edges), grid_spec=grid_spe...  36.2 us
    pallas_call x1, Pallas kernels, late_scores(): pl.pallas_call(late_kernel, grid=(edges // LATE_TILE,), in_specs=[pl.Bloc...  29.4 us
    all_to_all x1, starting transfers between devices, body(): lax.all_to_all(early_picked, 'node', split_axis=0, concat_axis=0, tiled=T...  11.1 us
    all_to_all x1, starting transfers between devices, body(): lax.all_to_all(late_picked, 'node', split_axis=0, concat_axis=0, tiled=True)  5.93 us
  transfers between devices with their start and end apart: 2, of which 2 were waited for; matrix products, arithmetic and copies ran while one was open for 8% of the time, Pallas kernels for 14%

profile of v19, /device:TPU:4, one launch (start us, length us, event | category | flops | bytes accessed | tf_op | source)
XLA Modules:
  0.0 251.2 jit_solution(17964270444156567182)
XLA Ops:
  0.6 0.0 slice-start
  0.7 0.7 add_bitcast_fusion
  1.4 0.4 slice-done
  1.8 0.5 reshape.52
  2.3 0.1 broadcast_in_dim.10
  2.3 0.1 fusion.6
  2.4 4.0 %gather_fusion.1 = bf16[64,392,128]{2,1,0:T(8,128)(2,1)} fusion(bf16[9,392,128]{2,1,0:T(8,128)(2,1)S(1)} %fusion.6, s32[1024]{0:T(1024)S(1)} %pad_clamp_fusion), kind=kCustom, calls=%fused_computation.1 | custom fusion | bytes 12845312 | tf_op jit(solution)/shard_map/jit(_take)/gather | solution.py:221
  6.4 0.0 slice-start.1
  6.4 11.1 %all-to-all-start = ((bf16[64,392,128]{2,1,0:T(8,128)(2,1)}), bf16[64,392,128]{2,1,0:T(8,128)(2,1)}, u32[]{:S(2)}, u32[]{:S(2)}) async-start(bf16[64,392,128]{2,1,0:T(8,128)(2,1)} %gather_fusion.1), calls=%async_computation | async-start | bytes 12845056 | tf_op jit(solution)/shard_map/all_to_all | solution.py:223
  17.6 0.0 slice-done.1
  17.6 0.0 copy-start.2
  17.6 0.0 copy-start.3
  17.6 2.0 gather_fusion
  19.6 0.0 copy-done.2
  19.6 0.4 copy.47
  20.0 0.5 copy.52
  20.5 0.0 copy-done.3
  20.5 2.8 %add_add_fusion = (s32[2,2048]{0,1:T(8,128)S(1)}, s32[2,2048]{0,1:T(8,128)S(1)}, s32[2,2048]{0,1:T(8,128)}) fusion(pred[2,2048]{0,1:T(8,128)(4,1)S(1)} %copy.52, s32[2,2048]{0,1:T(8,128)S(1)} %copy.47), kind=kLoop, calls=%fused_computation.19 | loop fusion | flops 172032 | bytes 69632 | tf_op jit(solution)/shard_map/sub | solution.py:230
  23.3 1.6 multiply_add_fusion
  24.9 136.8 %all-to-all-done = bf16[64,392,128]{2,1,0:T(8,128)(2,1)} async-done(((bf16[64,392,128]{2,1,0:T(8,128)(2,1)}), bf16[64,392,128]{2,1,0:T(8,128)(2,1)}, u32[]{:S(2)}, u32[]{:S(2)}) %all-to-all-start) | async-done | bytes 6422560 | tf_op jit(solution)/shard_map/all_to_all | solution.py:223
  161.7 5.9 %all-to-all-start.1 = ((bf16[64,32,512]{2,1,0:T(8,128)(2,1)}), bf16[64,32,512]{2,1,0:T(8,128)(2,1)}, u32[]{:S(2)}, u32[]{:S(2)}) async-start(bf16[64,32,512]{2,1,0:T(8,128)(2,1)} %gather_fusion), calls=%async_computation.1 | async-start | bytes 4194304 | tf_op jit(solution)/shard_map/all_to_all | solution.py:234
  167.6 0.3 copy.54
  167.9 0.0 copy-start
  167.9 1.7 copy.57
  169.6 2.1 convert_reduce_fusion
  171.7 0.4 fusion.4
  172.1 1.1 copy.58
  173.2 0.0 copy-done
  173.2 0.3 copy.59
  173.5 0.6 copy.62
  174.1 1.4 copy.61.pid_ref
  175.5 2.5 convert_bitcast_fusion.mask_ref
  178.0 0.0 copy-start.1
  178.0 36.2 %shard_map.86.part_ref = f32[2048,512]{1,0:T(8,128)} custom-call(s32[4096]{0:T(1024)} %bitcast.13, bf16[25088,128]{1,0:T(8,128)(2,1)} %bitcast.3.table, f32[2048,2]{1,0:T(8,128)} %convert_bitcast_fusion.mask_ref, bf16[1024,512]{1,0:T(8,128)(2,1)} %wb_ref.3, bf16[1024,512]{1,0:T(8,128)(2,1)} %wb_ref.3), custom_call_target="tpu_custom_call" | custom-call | flops 2147483648 | bytes 8388608 | tf_op jit(solution)/shard_map/pallas_call | solution.py:148
  214.2 0.0 copy-done.1
  214.2 0.0 copy-start.4
  214.2 1.6 select_bitcast_fusion.idx_ref
  215.8 2.9 %all-to-all-done.1 = bf16[64,32,512]{2,1,0:T(8,128)(2,1)} async-done(((bf16[64,32,512]{2,1,0:T(8,128)(2,1)}), bf16[64,32,512]{2,1,0:T(8,128)(2,1)}, u32[]{:S(2)}, u32[]{:S(2)}) %all-to-all-start.1) | async-done | bytes 2097184 | tf_op jit(solution)/shard_map/all_to_all | solution.py:234
  218.8 0.0 copy-done.4
  218.8 0.6 broadcast_in_dim.12.wo_ref
  219.4 29.4 %shard_map.87 = (f32[1,2048]{1,0:T(1,128)}, f32[128]{0:T(128)}) custom-call(s32[2048,2]{1,0:T(8,128)} %select_bitcast_fusion.idx_ref, f32[2048,512]{1,0:T(8,128)} %shard_map.86.part_ref, bf16[2048,512]{1,0:T(8,128)(2,1)} %bitcast.5.table_ref, bf16[1024,512]{1,0:T(8,128)(2,1)} %wb_ref.3, bf16[1024,512]{1,0:T(8,128)(2,1)} %wb_ref.3, f32[1,512]{1,0:T(1,128)} %bitcast.17, ...), custom_call_target="tpu_custom_call" | custom-call | flops 10737418240 | bytes 6291456 | tf_op jit(solution)/shard_map/pallas_call | solution.py:165
  248.7 1.3 copy.65
  250.0 1.2 copy.66
  (5 shorter events, 0.1 us)
Async XLA Ops:
  0.6 1.2 slice-start
  6.4 11.1 %slice-start.1 = ((bf16[8,128,512]{2,1,0:T(8,128)(2,1)}), bf16[8,32,512]{2,1,0:T(8,128)(2,1)S(1)}, s32[]{:S(2)}) async-start(bf16[8,128,512]{2,1,0:T(8,128)(2,1)} %param.7), calls=%async_computation.3 | async-start | bytes 524288 | tf_op jit(solution)/shard_map/slice | solution.py:220
  6.4 155.2 %all-to-all-start = ((bf16[64,392,128]{2,1,0:T(8,128)(2,1)}), bf16[64,392,128]{2,1,0:T(8,128)(2,1)}, u32[]{:S(2)}, u32[]{:S(2)}) async-start(bf16[64,392,128]{2,1,0:T(8,128)(2,1)} %gather_fusion.1), calls=%async_computation | async-start | bytes 12845056 | tf_op jit(solution)/shard_map/all_to_all | solution.py:223
  17.6 2.0 copy-start.2
  17.6 2.9 %copy-start.3 = (s32[2048]{0:T(1024)S(1)}, s32[2048]{0:T(1024)}, u32[]{:S(2)}) copy-start(s32[2048]{0:T(1024)} %param.10) | copy-start | bytes 24580
  161.7 57.1 %all-to-all-start.1 = ((bf16[64,32,512]{2,1,0:T(8,128)(2,1)}), bf16[64,32,512]{2,1,0:T(8,128)(2,1)}, u32[]{:S(2)}, u32[]{:S(2)}) async-start(bf16[64,32,512]{2,1,0:T(8,128)(2,1)} %gather_fusion), calls=%async_computation.1 | async-start | bytes 4194304 | tf_op jit(solution)/shard_map/all_to_all | solution.py:234
  167.9 5.3 %copy-start = (s32[2,2048]{0,1:T(8,128)S(1)}, s32[2,2048]{0,1:T(8,128)}, u32[]{:S(2)}) copy-start(s32[2,2048]{0,1:T(8,128)} %multiply_add_fusion) | copy-start | bytes 49156
  178.0 36.2 %copy-start.1 = (pred[2,2048]{0,1:T(8,128)(4,1)S(1)}, pred[2,2048]{0,1:T(8,128)(4,1)}, u32[]{:S(2)}) copy-start(pred[2,2048]{0,1:T(8,128)(4,1)} %copy.58) | copy-start | bytes 12292
  214.2 4.6 %copy-start.4 = (bf16[512]{0:T(512)(128)(2,1)S(1)}, bf16[512]{0:T(512)(128)(2,1)}, u32[]{:S(2)}) copy-start(bf16[512]{0:T(512)(128)(2,1)} %param.13) | copy-start | bytes 3076
